TPU v7x, 32 devices: a whole 2x2x4 slice. The times are simulated.
32 devices in a mesh: lat: 8 (over y, x, core), lon: 4 (over z).
Axes of the slice: x: 2, y: 2, z: 4, core: 2. Of those that a mesh axis runs over, the one named last changes fastest.
Arguments:
- adjoint: float32 [8, 8, 256, 512], P(None, None, 'lat', 'lon'), may hold values from -6 to 6
- transport: float32 [6, 8, 256, 512], P(None, None, 'lat', 'lon'), may hold values from 0.03 to 0.14
- cell_weight: float32 [256, 512], P('lat', 'lon'), may hold values from 0.1 to 1
- region_local: int32 [256, 512], P('lat', 'lon'), may hold values from 0 to 255
- tile_regions: int32 [32, 256], replicated, may hold values from 0 to 2047, as said below
- polar_rows: int32 [256], P('lat'), may hold values 0 or 1
- week_index: int32 [1], replicated, may hold values from 0 to 51
- grad_in: bfloat16 [2048, 416], P(('lat', 'lon')), may hold values from -6 to 6
- covariance: bfloat16 [2048, 2048], P(('lat', 'lon')), may hold values from -0.25 to 0.25
Outputs:
- adjoint_out: float32 [8, 8, 256, 512], P(None, None, 'lat', 'lon')
- precond: float32 [2048, 416], P(('lat', 'lon'))
Inputs may be any that keep to these rules, and one draw needn't show every extreme that they name: `tile_regions`: each row holds 256 different region numbers; with per = 8, entries o * per to o * per + per - 1 of a row lie in regions o * 64 to o * 64 + 63, for every o.
All inputs are finite; a program needn't handle non-finite values. No bound on the sum of `polar_rows` on one device may be relied on, other than what follows from the above.
Results may differ from a plain program's by a relative error of at most 0.00066.
Values may be sent and summed in bfloat16 or wider, within the bound.
No kernel may reach another device: no remote copies, remote signals or barrier semaphores. Data moves between devices by JAX's collectives and lax.ppermute only.
A program may use at most 128 MiB of HBM per device.

v0:
```python
import jax
import jax.numpy as jnp
from jax import lax
from jax.sharding import PartitionSpec as P


def extended(x, sides, width):
    for axis, dim in sides:
        size, length = (lax.axis_size(axis), x.shape[dim])
        up = [(i, (i + 1) % size) for i in range(size)]
        down = [(j, i) for i, j in up]
        last = lax.slice_in_dim(x, length - width, length, axis=dim)
        leading = lax.slice_in_dim(x, 0, width, axis=dim)
        before = lax.ppermute(last, axis, up)
        after = lax.ppermute(leading, axis, down)
        x = jnp.concatenate([before, x, after], axis=dim)
    return x


def advance(padded, rates):
    centre = padded[:, :, 1:-1, 1:-1]
    to_east = padded[:, :, 1:-1, 2:] - centre
    to_west = padded[:, :, 1:-1, :-2] - centre
    to_north = padded[:, :, 2:, 1:-1] - centre
    to_south = padded[:, :, :-2, 1:-1] - centre
    flat_zero = jnp.zeros_like(centre[:, :1])
    upper = jnp.concatenate([centre[:, 1:] - centre[:, :-1], flat_zero], axis=1)
    lower = jnp.concatenate([flat_zero, centre[:, :-1] - centre[:, 1:]], axis=1)
    return (
        centre
        + rates[0] * to_east
        + rates[1] * to_west
        + rates[2] * to_north
        + rates[3] * to_south
        + rates[4] * upper
        + rates[5] * lower
    )


def pole_mask(padded, margin, interior):
    band = lax.axis_index("lat")
    last_band = lax.axis_size("lat") - 1
    row_ids = jnp.arange(interior + 2 * margin, dtype=jnp.int32)
    outside = (row_ids < margin) & (band == 0) | (row_ids >= interior + margin) & (
        band == last_band
    )
    return jnp.where(outside[None, None, :, None], 0.0, padded)


def shards(
    adjoint,
    transport,
    cell_weight,
    region_local,
    tile_regions,
    polar_rows,
    week_index,
    grad_in,
    covariance,
):
    tracers, levels, lat_rows, lon_cols = adjoint.shape
    region_count = covariance.shape[1]
    own_rows = covariance.shape[0]
    week_cols = grad_in.shape[1] // tracers
    lon_count = lax.axis_size("lon")
    my_tile = lax.axis_index("lat") * lon_count + lax.axis_index("lon")
    base = jnp.dot(
        covariance,
        lax.all_gather(grad_in, ("lat", "lon"), axis=0, tiled=True),
        preferred_element_type=jnp.float32,
    )
    field = adjoint
    for repeat in range(2):
        padded = extended(field, (("lat", 2), ("lon", 3)), 1)
        field = advance(pole_mask(padded, 1, lat_rows), transport)
    row_sums = lax.psum(jnp.sum(field, axis=3), "lon")
    zonal = row_sums / (lon_cols * lon_count)
    flags = polar_rows.astype(jnp.float32)[None, None, :, None]
    adjoint_out = field + 0.5 * flags * (zonal[..., None] - field)
    surface = (adjoint_out[:, 0] * cell_weight[None]).reshape(tracers, -1)
    local_count = tile_regions.shape[1]
    one_hot = (
        region_local.reshape(1, -1) == jnp.arange(local_count, dtype=jnp.int32)[:, None]
    ).astype(jnp.float32)
    local_sums = lax.dot_general(
        one_hot,
        surface,
        (((1,), (1,)), ((), ())),
        precision=lax.Precision.HIGHEST,
        preferred_element_type=jnp.float32,
    )
    my_regions = lax.dynamic_index_in_dim(tile_regions, my_tile, 0, keepdims=False)
    dense = jnp.zeros((region_count, tracers), jnp.float32).at[my_regions].add(local_sums)
    fresh_all = lax.psum(dense, ("lat", "lon")).astype(jnp.bfloat16)
    added = jnp.dot(covariance, fresh_all, preferred_element_type=jnp.float32)
    week_hot = (jnp.arange(week_cols, dtype=jnp.int32) == week_index[0]).astype(jnp.float32)
    precond = (
        base.reshape(own_rows, week_cols, tracers) + week_hot[None, :, None] * added[:, None, :]
    )
    return (adjoint_out, precond.reshape(own_rows, week_cols * tracers))


def solution(mesh):
    in_specs = (
        P(None, None, "lat", "lon"),
        P(None, None, "lat", "lon"),
        P("lat", "lon"),
        P("lat", "lon"),
        P(),
        P("lat"),
        P(),
        P(("lat", "lon"), None),
        P(("lat", "lon"), None),
    )
    out_specs = (P(None, None, "lat", "lon"), P(("lat", "lon"), None))
    return jax.shard_map(shards, mesh=mesh, in_specs=in_specs, out_specs=out_specs, check_vma=False)
```

profile of v0, /device:TPU:0, one launch (start us, length us, event | category | flops | bytes accessed | tf_op | source)
XLA Modules:
  0.0 179.2 jit_solution(4061105329152444854)
XLA Ops:
  7.2 1.1 fusion.30
  8.3 0.5 collective-permute-start
  8.9 2.9 %collective-permute-start.1 = (f32[8,8,1,128]{3,1,2,0:T(8,128)S(1)}, f32[8,8,1,128]{3,1,2,0:T(8,128)S(1)}, u32[]{:S(2)}, u32[]{:S(2)}) collective-permute-start(f32[8,8,1,128]{3,1,2,0:T(8,128)S(1)} %bitcast.36), channel_id=1, source_target_pairs={{4,0},{8,4},{12,8},{16,12},{20,16},{24,20},{28,24},{0,28},{5,1},{9... | collective-permute-start | bytes 98312 | tf_op jit(solution)/shard_map/ppermute | solution.py:15
  11.8 1.3 slice_bitcast_fusion.5
  13.1 0.7 convert_multiply_fusion
  13.8 3.6 %copy.81 = f32[8,8,32,128]{2,1,3,0:T(8,128)} copy(f32[8,8,32,128]{3,2,1,0:T(8,128)} %param.9) | data formatting | bytes 2097152 | tf_op args[0]
  17.4 2.6 %copy.80 = f32[8,8,1,128]{2,1,3,0:T(8,128)} copy(f32[8,8,1,128]{3,1,2,0:T(8,128)S(1)} %collective-permute-done) | data formatting | bytes 65536 | tf_op jit(solution)/shard_map/ppermute | solution.py:14
  20.1 2.6 %copy.82 = f32[8,8,1,128]{2,1,3,0:T(8,128)} copy(f32[8,8,1,128]{3,1,2,0:T(8,128)S(1)} %collective-permute-done.1) | data formatting | bytes 65536 | tf_op jit(solution)/shard_map/ppermute | solution.py:15
  22.7 0.9 pad_maximum_fusion.5
  23.6 2.3 %collective-permute-start.2 = (f32[8,8,34,1]{2,1,3,0:T(8,128)S(1)}, f32[8,8,34,1]{2,1,3,0:T(8,128)S(1)}, u32[]{:S(2)}, u32[]{:S(2)}) collective-permute-start(f32[8,8,34,1]{2,1,3,0:T(8,128)S(1)} %get-tuple-element.16), channel_id=1, source_target_pairs={{0,1},{1,2},{2,3},{3,0},{4,5},{5,6},{6,7},{7,4},{8,9},{9,10},{10,1... | collective-permute-start | bytes 26120 | tf_op jit(solution)/shard_map/ppermute | solution.py:14
  26.0 2.1 %collective-permute-start.3 = (f32[8,8,34,1]{2,1,3,0:T(8,128)S(1)}, f32[8,8,34,1]{2,1,3,0:T(8,128)S(1)}, u32[]{:S(2)}, u32[]{:S(2)}) collective-permute-start(f32[8,8,34,1]{2,1,3,0:T(8,128)S(1)} %get-tuple-element.17), channel_id=1, source_target_pairs={{1,0},{2,1},{3,2},{0,3},{5,4},{6,5},{7,6},{4,7},{9,8},{10,9},{11,1... | collective-permute-start | bytes 26120 | tf_op jit(solution)/shard_map/ppermute | solution.py:15
  28.1 0.2 copy.83
  28.3 1.0 copy.84
  29.3 1.0 copy.85
  30.3 1.0 copy.86
  31.4 1.0 copy.87
  32.4 1.0 copy.88
  33.4 5.8 %maximum_select_fusion = f32[8,8,34,130]{2,1,3,0:T(8,128)S(1)} fusion(f32[8,8,34,1]{2,1,3,0:T(8,128)S(1)} %collective-permute-done.3, f32[8,8,1,128]{2,1,3,0:T(8,128)} %copy.82, f32[8,8,32,128]{2,1,3,0:T(8,128)} %copy.81, f32[8,8,1,128]{2,1,3,0:T(8,128)} %copy.80, f32[8,8,34,1]{2,1,3,0:T(8,128)S(1)} %collective-permute-done.2, pred[34]{0:T(512)(128)(4,1)S(1)} %and_or_fusion), kind=kLoop, calls=%fused_computation.1 | loop fusion | flops 1414400 | bytes 2263074 | tf_op jit(solution)/shard_map/jit(_where)/select_n | solution.py:47
  39.2 2.2 %slice_subtract_fusion.11 = (f32[8,7,32,128]{2,1,3,0:T(8,128)S(1)}, f32[8,7,32,128]{2,1,3,0:T(8,128)S(1)}) fusion(f32[8,8,34,130]{2,1,3,0:T(8,128)S(1)} %maximum_select_fusion), kind=kLoop, calls=%fused_computation.37 | loop fusion | flops 458752 | bytes 3670016 | tf_op jit(solution)/shard_map/sub | solution.py:27
  41.4 6.1 %fusion.13 = f32[8,8,32,128]{2,1,3,0:T(8,128)S(1)} fusion(f32[8,8,34,130]{2,1,3,0:T(8,128)S(1)} %maximum_select_fusion, f32[8,7,32,128]{2,1,3,0:T(8,128)S(1)} %get-tuple-element.21, f32[8,7,32,128]{2,1,3,0:T(8,128)S(1)} %get-tuple-element.20, f32[8,32,128]{1,0,2:T(8,128)} %copy.88, f32[8,32,128]{1,0,2:T(8,128)} %copy.87, f32[8,32,128]{1,0,2:T(8,128)} %copy.86, ...), kind=kLoop, calls=%fused_computation.21 | loop fusion | flops 4194304 | bytes 8912896 | tf_op jit(solution)/shard_map/add | solution.py:30
  47.6 4.6 %fusion.29 = (f32[8,8,1,128]{2,1,3,0:T(8,128)}, f32[8,8,1,128]{2,1,3,0:T(8,128)}) fusion(f32[8,8,32,128]{2,1,3,0:T(8,128)S(1)} %fusion.13), kind=kLoop, calls=%fused_computation.66 | loop fusion | bytes 131072 | tf_op jit(solution)/shard_map/slice | solution.py:12
  52.2 2.8 %copy.89 = f32[8,8,1,128]{3,1,2,0:T(8,128)S(1)} copy(f32[8,8,1,128]{2,1,3,0:T(8,128)} %get-tuple-element.22) | data formatting | bytes 65536 | tf_op jit(solution)/shard_map/slice | solution.py:12
  55.1 0.0 collective-permute-start.4
  55.1 2.9 %copy.90 = f32[8,8,1,128]{3,1,2,0:T(8,128)S(1)} copy(f32[8,8,1,128]{2,1,3,0:T(8,128)} %get-tuple-element.23) | data formatting | bytes 65536 | tf_op jit(solution)/shard_map/slice | solution.py:13
  58.0 2.9 %collective-permute-start.5 = (f32[8,8,1,128]{3,1,2,0:T(8,128)S(1)}, f32[8,8,1,128]{3,1,2,0:T(8,128)S(1)}, u32[]{:S(2)}, u32[]{:S(2)}) collective-permute-start(f32[8,8,1,128]{3,1,2,0:T(8,128)S(1)} %copy.90), channel_id=1, source_target_pairs={{4,0},{8,4},{12,8},{16,12},{20,16},{24,20},{28,24},{0,28},{5,1},{9... | collective-permute-start | bytes 98312 | tf_op jit(solution)/shard_map/ppermute | solution.py:15
  60.8 0.7 compare_select_fusion
  62.2 2.7 %copy.91 = f32[8,8,1,128]{2,1,3,0:T(8,128)} copy(f32[8,8,1,128]{3,1,2,0:T(8,128)S(1)} %collective-permute-done.4) | data formatting | bytes 65536 | tf_op jit(solution)/shard_map/ppermute | solution.py:14
  64.9 2.7 %copy.92 = f32[8,8,1,128]{2,1,3,0:T(8,128)} copy(f32[8,8,1,128]{3,1,2,0:T(8,128)S(1)} %collective-permute-done.5) | data formatting | bytes 65536 | tf_op jit(solution)/shard_map/ppermute | solution.py:15
  67.6 1.0 pad_maximum_fusion.2
  68.5 0.2 collective-permute-start.6
  68.7 3.7 %collective-permute-start.7 = (f32[8,8,34,1]{2,1,3,0:T(8,128)S(1)}, f32[8,8,34,1]{2,1,3,0:T(8,128)S(1)}, u32[]{:S(2)}, u32[]{:S(2)}) collective-permute-start(f32[8,8,34,1]{2,1,3,0:T(8,128)S(1)} %get-tuple-element.15), channel_id=1, source_target_pairs={{1,0},{2,1},{3,2},{0,3},{5,4},{6,5},{7,6},{4,7},{9,8},{10,9},{11,1... | collective-permute-start | bytes 26120 | tf_op jit(solution)/shard_map/ppermute | solution.py:15
  72.4 0.1 mul.173
  72.5 0.1 mul.174
  72.6 1.7 collective-permute-done.6
  74.3 5.8 %maximum_select_fusion.1 = f32[8,8,34,130]{2,1,3,0:T(8,128)S(1)} fusion(f32[8,8,34,1]{2,1,3,0:T(8,128)S(1)} %collective-permute-done.7, f32[8,8,1,128]{2,1,3,0:T(8,128)} %copy.92, f32[8,8,32,128]{2,1,3,0:T(8,128)} %copy-done.1, f32[8,8,1,128]{2,1,3,0:T(8,128)} %copy.91, f32[8,8,34,1]{2,1,3,0:T(8,128)S(1)} %collective-permute-done.6, ...), kind=kLoop, calls=%fused_computation.2 | loop fusion | flops 1414400 | bytes 2263074 | tf_op jit(solution)/shard_map/jit(_where)/select_n | solution.py:47
  80.2 2.2 %slice_subtract_fusion.9 = (f32[8,7,32,128]{2,1,3,0:T(8,128)S(1)}, f32[8,7,32,128]{2,1,3,0:T(8,128)S(1)}) fusion(f32[8,8,34,130]{2,1,3,0:T(8,128)S(1)} %maximum_select_fusion.1), kind=kLoop, calls=%fused_computation.35 | loop fusion | flops 458752 | bytes 3670016 | tf_op jit(solution)/shard_map/sub | solution.py:27
  82.5 6.0 %fusion.27 = (f32[8,8,32]{2,1,0:T(8,128)S(1)}, f32[8,8,32,128]{2,1,3,0:T(8,128)}) fusion(f32[8,7,32,128]{2,1,3,0:T(8,128)S(1)} %get-tuple-element.19, f32[8,32,128]{1,0,2:T(8,128)S(1)} %copy-done.7, f32[8,7,32,128]{2,1,3,0:T(8,128)S(1)} %get-tuple-element.18, f32[8,32,128]{1,0,2:T(8,128)S(1)} %copy-done.6, f32[8,8,34,130]{2,1,3,0:T(8,128)S(1)} %maximum_select_fusion.1, ...), kind=kLoop, calls=%fused_computation.65 | loop fusion | flops 4454400 | bytes 8921088 | tf_op jit(solution)/shard_map/reduce_sum | solution.py:76
  88.4 19.5 %psum.14 = f32[8,8,32]{2,1,0:T(8,128)S(1)} all-reduce(f32[8,8,32]{2,1,0:T(8,128)S(1)} %get-tuple-element.12), channel_id=1, replica_groups=mesh['lat'=8,'lon'=4] {'lon'}, use_global_device_ids=true, to_apply=%region_1.2 | all-reduce | flops 2048 | bytes 16384 | tf_op jit(solution)/shard_map/psum | solution.py:76
  108.0 2.6 %multiply_add_fusion = f32[8,8,32,128]{2,1,3,0:T(8,128)S(1)} fusion(f32[8,8,32,128]{2,1,3,0:T(8,128)} %get-tuple-element.13, f32[8,8,32]{2,1,0:T(8,128)S(1)} %broadcast_multiply_fusion, f32[32]{0:T(128)S(1)} %convert_multiply_fusion), kind=kLoop, calls=%fused_computation.32 | loop fusion | flops 786432 | bytes 2105472 | tf_op jit(solution)/shard_map/add | solution.py:79
  110.6 1.9 %copy-done.2 = f32[8,8,32,128]{2,1,3,0:T(8,128)} copy-done((f32[8,8,32,128]{2,1,3,0:T(8,128)}, f32[8,8,32,128]{2,1,3,0:T(8,128)S(1)}, u32[]{:S(2)}) %copy-start.2) | copy-done | bytes 1048600
  112.6 3.7 %copy.96 = f32[8,8,32,128]{3,2,1,0:T(8,128)} copy(f32[8,8,32,128]{2,1,3,0:T(8,128)} %copy-done.2) | data formatting | bytes 2097152
  116.2 0.3 copy.93
  116.5 2.0 %fusion.20 = f32[256,8]{1,0:T(8,128)S(1)} fusion(s32[4096]{0:T(1024)S(1)} %bitcast.39, f32[1,8,32,128]{3,2,1,0:T(8,128)S(1)} %bitcast.35, f32[4096]{0:T(1024)S(1)} %bitcast.40), kind=kOutput, calls=%fused_computation.33 | convolution fusion | flops 101744640 | bytes 172032 | tf_op jit(solution)/shard_map/dot_general | solution.py:85
  118.5 1.7 scatter_custom_fusion
  120.1 49.0 %psum.15 = bf16[2048,8]{1,0:T(8,128)(2,1)S(1)} all-reduce(f32[2048,8]{1,0:T(8,128)S(1)} %scatter_custom_fusion), channel_id=1, replica_groups=mesh['lat'=8,'lon'=4] {'lat','lon'}, use_global_device_ids=true, to_apply=%region_3.4 | all-reduce | flops 16384 | bytes 98304 | tf_op jit(solution)/shard_map/psum | solution.py:94
  169.2 0.3 convolution_bitcast_fusion
  169.5 0.1 copy.95
  169.7 2.7 %convolution_add_fusion = f32[64,416]{1,0:T(8,128)} fusion(bf16[64,2048]{1,0:T(8,128)(2,1)S(1)} %copy-done, bf16[2048,416]{1,0:T(8,128)(2,1)} %all-gather.2.cloned.1.call-done, f32[64,416]{1,0:T(8,128)S(1)} %copy.95, f32[416]{0:T(512)S(1)} %mul.174), kind=kOutput, calls=%fused_computation.39 | convolution fusion | flops 109105152 | bytes 2180736 | tf_op jit(solution)/shard_map/dot_general | solution.py:67
  (35 shorter events, 0.2 us)
Async XLA Ops:
  7.2 162.0 %copy-start = (bf16[64,2048]{1,0:T(8,128)(2,1)S(1)}, bf16[64,2048]{1,0:T(8,128)(2,1)}, u32[]{:S(2)}) copy-start(bf16[64,2048]{1,0:T(8,128)(2,1)} %param.17) | copy-start | bytes 786436
  7.2 162.5 %all-gather.2.cloned.1.call-start = ((), (), s32[]{:S(2)}) async-start(), calls=%async_computation | async-start | bytes 2162688 | tf_op jit(solution)/shard_map/all_gather | solution.py:69
  8.3 9.1 %collective-permute-start = (f32[8,8,1,128]{3,1,2,0:T(8,128)S(1)}, f32[8,8,1,128]{3,1,2,0:T(8,128)S(1)}, u32[]{:S(2)}, u32[]{:S(2)}) collective-permute-start(f32[8,8,1,128]{3,1,2,0:T(8,128)S(1)} %bitcast.37), channel_id=1, source_target_pairs={{0,4},{4,8},{8,12},{12,16},{16,20},{20,24},{24,28},{28,0},{1,5},{5... | collective-permute-start | bytes 98312 | tf_op jit(solution)/shard_map/ppermute | solution.py:14
  8.9 11.2 %collective-permute-start.1 = (f32[8,8,1,128]{3,1,2,0:T(8,128)S(1)}, f32[8,8,1,128]{3,1,2,0:T(8,128)S(1)}, u32[]{:S(2)}, u32[]{:S(2)}) collective-permute-start(f32[8,8,1,128]{3,1,2,0:T(8,128)S(1)} %bitcast.36), channel_id=1, source_target_pairs={{4,0},{8,4},{12,8},{16,12},{20,16},{24,20},{28,24},{0,28},{5,1},{9... | collective-permute-start | bytes 98312 | tf_op jit(solution)/shard_map/ppermute | solution.py:15
  23.6 9.7 %collective-permute-start.2 = (f32[8,8,34,1]{2,1,3,0:T(8,128)S(1)}, f32[8,8,34,1]{2,1,3,0:T(8,128)S(1)}, u32[]{:S(2)}, u32[]{:S(2)}) collective-permute-start(f32[8,8,34,1]{2,1,3,0:T(8,128)S(1)} %get-tuple-element.16), channel_id=1, source_target_pairs={{0,1},{1,2},{2,3},{3,0},{4,5},{5,6},{6,7},{7,4},{8,9},{9,10},{10,1... | collective-permute-start | bytes 26120 | tf_op jit(solution)/shard_map/ppermute | solution.py:14
  26.0 7.4 %collective-permute-start.3 = (f32[8,8,34,1]{2,1,3,0:T(8,128)S(1)}, f32[8,8,34,1]{2,1,3,0:T(8,128)S(1)}, u32[]{:S(2)}, u32[]{:S(2)}) collective-permute-start(f32[8,8,34,1]{2,1,3,0:T(8,128)S(1)} %get-tuple-element.17), channel_id=1, source_target_pairs={{1,0},{2,1},{3,2},{0,3},{5,4},{6,5},{7,6},{4,7},{9,8},{10,9},{11,1... | collective-permute-start | bytes 26120 | tf_op jit(solution)/shard_map/ppermute | solution.py:15
  47.6 4.6 %copy-start.1 = (f32[8,8,32,128]{2,1,3,0:T(8,128)}, f32[8,8,32,128]{2,1,3,0:T(8,128)S(1)}, u32[]{:S(2)}) copy-start(f32[8,8,32,128]{2,1,3,0:T(8,128)S(1)} %fusion.13) | copy-start | bytes 3145732
  55.1 7.1 %collective-permute-start.4 = (f32[8,8,1,128]{3,1,2,0:T(8,128)S(1)}, f32[8,8,1,128]{3,1,2,0:T(8,128)S(1)}, u32[]{:S(2)}, u32[]{:S(2)}) collective-permute-start(f32[8,8,1,128]{3,1,2,0:T(8,128)S(1)} %copy.89), channel_id=1, source_target_pairs={{0,4},{4,8},{8,12},{12,16},{16,20},{20,24},{24,28},{28,0},{1,5},{5... | collective-permute-start | bytes 98312 | tf_op jit(solution)/shard_map/ppermute | solution.py:14
  58.0 6.9 %collective-permute-start.5 = (f32[8,8,1,128]{3,1,2,0:T(8,128)S(1)}, f32[8,8,1,128]{3,1,2,0:T(8,128)S(1)}, u32[]{:S(2)}, u32[]{:S(2)}) collective-permute-start(f32[8,8,1,128]{3,1,2,0:T(8,128)S(1)} %copy.90), channel_id=1, source_target_pairs={{4,0},{8,4},{12,8},{16,12},{20,16},{24,20},{28,24},{0,28},{5,1},{9... | collective-permute-start | bytes 98312 | tf_op jit(solution)/shard_map/ppermute | solution.py:15
  68.5 5.8 %collective-permute-start.6 = (f32[8,8,34,1]{2,1,3,0:T(8,128)S(1)}, f32[8,8,34,1]{2,1,3,0:T(8,128)S(1)}, u32[]{:S(2)}, u32[]{:S(2)}) collective-permute-start(f32[8,8,34,1]{2,1,3,0:T(8,128)S(1)} %get-tuple-element.14), channel_id=1, source_target_pairs={{0,1},{1,2},{2,3},{3,0},{4,5},{5,6},{6,7},{7,4},{8,9},{9,10},{10,1... | collective-permute-start | bytes 26120 | tf_op jit(solution)/shard_map/ppermute | solution.py:14
  68.7 5.6 %collective-permute-start.7 = (f32[8,8,34,1]{2,1,3,0:T(8,128)S(1)}, f32[8,8,34,1]{2,1,3,0:T(8,128)S(1)}, u32[]{:S(2)}, u32[]{:S(2)}) collective-permute-start(f32[8,8,34,1]{2,1,3,0:T(8,128)S(1)} %get-tuple-element.15), channel_id=1, source_target_pairs={{1,0},{2,1},{3,2},{0,3},{5,4},{6,5},{7,6},{4,7},{9,8},{10,9},{11,1... | collective-permute-start | bytes 26120 | tf_op jit(solution)/shard_map/ppermute | solution.py:15
  80.1 2.3 %copy-start.3 = (f32[8,32,128]{1,0,2:T(8,128)S(1)}, f32[8,32,128]{1,0,2:T(8,128)}, u32[]{:S(2)}) copy-start(f32[8,32,128]{1,0,2:T(8,128)} %copy.84) | copy-start | bytes 393220
  80.2 2.3 %copy-start.4 = (f32[8,32,128]{1,0,2:T(8,128)S(1)}, f32[8,32,128]{1,0,2:T(8,128)}, u32[]{:S(2)}) copy-start(f32[8,32,128]{1,0,2:T(8,128)} %copy.85) | copy-start | bytes 393220
  80.2 2.3 %copy-start.5 = (f32[8,32,128]{1,0,2:T(8,128)S(1)}, f32[8,32,128]{1,0,2:T(8,128)}, u32[]{:S(2)}) copy-start(f32[8,32,128]{1,0,2:T(8,128)} %copy.86) | copy-start | bytes 393220
  80.2 2.3 %copy-start.6 = (f32[8,32,128]{1,0,2:T(8,128)S(1)}, f32[8,32,128]{1,0,2:T(8,128)}, u32[]{:S(2)}) copy-start(f32[8,32,128]{1,0,2:T(8,128)} %copy.87) | copy-start | bytes 393220
  80.2 2.3 %copy-start.7 = (f32[8,32,128]{1,0,2:T(8,128)S(1)}, f32[8,32,128]{1,0,2:T(8,128)}, u32[]{:S(2)}) copy-start(f32[8,32,128]{1,0,2:T(8,128)} %copy.88) | copy-start | bytes 393220
  110.6 2.0 %copy-start.2 = (f32[8,8,32,128]{2,1,3,0:T(8,128)}, f32[8,8,32,128]{2,1,3,0:T(8,128)S(1)}, u32[]{:S(2)}) copy-start(f32[8,8,32,128]{2,1,3,0:T(8,128)S(1)} %multiply_add_fusion) | copy-start | bytes 3145732
  112.6 3.9 %copy-start.8 = (s32[32,128]{1,0:T(8,128)S(1)}, s32[32,128]{1,0:T(8,128)}, u32[]{:S(2)}) copy-start(s32[32,128]{1,0:T(8,128)} %param.12) | copy-start | bytes 49156
  112.6 3.9 %copy-start.9 = (f32[32,128]{1,0:T(8,128)S(1)}, f32[32,128]{1,0:T(8,128)}, u32[]{:S(2)}) copy-start(f32[32,128]{1,0:T(8,128)} %param.11) | copy-start | bytes 49156
  112.6 3.7 %slice-start = ((f32[8,8,32,128]{2,1,3,0:T(8,128)}), f32[8,1,32,128]{2,1,3,0:T(1,128)S(1)}, s32[]{:S(2)}) async-start(f32[8,8,32,128]{2,1,3,0:T(8,128)} %copy-done.2), calls=%async_computation.1 | async-start | bytes 1048576 | tf_op jit(solution)/shard_map/slice | solution.py:80
Sparse Core Ops, SparseCore 0:
  12.0 58.4 all-gather.1
where the time goes:
time: 180 us; the launch traced here: 179 us
  blocking collectives  68.5 us (38%)
  local copies, waits for them, and re-layouts  38.5 us (21%)
  other arithmetic  35.8 us (20%)
  between operations  15 us (8%)
  starting transfers between devices  14.7 us (8%)
  matrix products  4.95 us (3%)
    psum x1, blocking collectives, shards(): fresh_all = lax.psum(dense, ('lat', 'lon')).astype(jnp.bfloat16)  49 us
    psum x1, blocking collectives, shards(): row_sums = lax.psum(jnp.sum(field, axis=3), 'lon')  19.5 us
    select_n x2, other arithmetic, pole_mask(): return jnp.where(outside[None, None, :, None], 0.0, padded)  11.7 us
    ppermute x4, starting transfers between devices, extended(): after = lax.ppermute(leading, axis, down)  11.6 us
    unnamed x22, local copies, waits for them, and re-layouts  9.28 us
    slice x3, local copies, waits for them, and re-layouts, extended(): last = lax.slice_in_dim(x, length - width, length, axis=dim)  8.58 us
    add x1, other arithmetic, advance(): centre + rates[0] * to_east + rates[1] * to_west + rates[2] * to_north  6.13 us
    reduce_sum x1, other arithmetic, shards(): row_sums = lax.psum(jnp.sum(field, axis=3), 'lon')  5.98 us
  transfers between devices with their start and end apart: 9, of which 1 were waited for; matrix products, arithmetic and copies ran while one was open for 41% of the time, Pallas kernels for 0%

commit v1 on v0

v1 whole, which is shorter than its diff:
```python
import functools
import math

import jax
import jax.numpy as jnp
from jax import lax
from jax.experimental import pallas as pl
from jax.experimental.pallas import tpu as pltpu
from jax.sharding import PartitionSpec as P

AXES = ("lat", "lon")
F32 = jnp.float32
BF16 = jnp.bfloat16
LANES = 128
OFF = 8
VMEM = pl.BlockSpec(memory_space=pltpu.VMEM)
SMEM = pl.BlockSpec(memory_space=pltpu.SMEM)
HBM = pl.BlockSpec(memory_space=pl.ANY)


def iota(shape, dim):
    return lax.broadcasted_iota(jnp.int32, shape, dim)


BIG = 4 << 20


def nbytes(shape, dtype):
    return math.prod(shape) * jnp.dtype(dtype).itemsize


def call(body, outs, in_specs, scratch=(), aliases=None, keep=True):
    def placed(s, d):
        return pltpu.VMEM(s, d) if keep and nbytes(s, d) <= BIG else jax.ShapeDtypeStruct(s, d)

    def apply(*args):
        own = sum(nbytes(x.shape, x.dtype) for x in scratch if x.memory_space == pltpu.VMEM)
        own += sum(nbytes(x.shape, x.dtype) for x in args if nbytes(x.shape, x.dtype) > BIG)
        own += sum(nbytes(s, d) for s, d in outs if not keep or nbytes(s, d) > BIG)
        run = pl.pallas_call(
            body,
            out_shape=[placed(s, d) for s, d in outs],
            in_specs=in_specs,
            out_specs=[VMEM] * len(outs),
            scratch_shapes=list(scratch),
            input_output_aliases=aliases or {},
            compiler_params=pltpu.CompilerParams(vmem_limit_bytes=own + (6 << 20)),
        )
        return run(*(pltpu.with_memory_space_constraint(x, pltpu.VMEM)
                     if spec is VMEM and nbytes(x.shape, x.dtype) <= BIG else x
                     for x, spec in zip(args, in_specs)))

    return apply


def split3(x):
    hi = x.astype(BF16).astype(F32)
    rest = x - hi
    mid = rest.astype(BF16).astype(F32)
    return hi, mid, rest - mid


def rows_kernel(trc, lev, f_last, f_first, t_last, t_first, up, down):
    def row(ref, group, at):
        return ref[pl.ds(group * lev * 8 + at, lev, stride=8), :]

    for k in range(trc):
        up[k] = row(f_last, k, 6)
        up[trc + k] = row(f_last, k, 7)
        down[k] = row(f_first, k, 1)
        down[trc + k] = row(f_first, k, 0)
    for d in range(6):
        up[2 * trc + d] = row(t_last, d, 7)
        down[2 * trc + d] = row(t_first, d, 0)


def border_rows(field, rates):
    trc, lev, rows, _ = field.shape
    last = rows // 8 - 1

    def body(f_last, f_first, t_last, t_first, up, down):
        flat = lambda ref: ref.reshape(ref.shape[0] * 8, LANES)
        rows_kernel(trc, lev, flat(f_last), flat(f_first), flat(t_last), flat(t_first), up, down)

    f3 = field.reshape(trc * lev, rows, LANES)
    t3 = rates.reshape(6 * lev, rows, LANES)
    out = pltpu.VMEM((2 * trc + 6, lev, LANES), F32)
    return pl.pallas_call(
        body,
        grid=(1,),
        out_shape=[out, out],
        in_specs=[
            pl.BlockSpec((trc * lev, 8, LANES), lambda i: (0, last, 0)),
            pl.BlockSpec((trc * lev, 8, LANES), lambda i: (0, 0, 0)),
            pl.BlockSpec((6 * lev, 8, LANES), lambda i: (0, last, 0)),
            pl.BlockSpec((6 * lev, 8, LANES), lambda i: (0, 0, 0)),
        ],
        out_specs=[VMEM] * 2,
        compiler_params=pltpu.CompilerParams(vmem_limit_bytes=8 << 20),
        name="border_rows",
    )(f3, f3, t3, t3)


def border_cols(field, rates):
    trc, lev, rows, _ = field.shape
    tiles = trc * lev

    def body(f, t, east, west):
        lane = iota((8, LANES), 1)
        east[pl.ds(2 * rows, 8), :] = jnp.zeros((8, LANES), F32)
        west[pl.ds(2 * rows, 8), :] = jnp.zeros((8, LANES), F32)
        for c in range(0, rows, 8):
            e = jnp.zeros((8, LANES), F32)
            w = jnp.zeros((8, LANES), F32)
            for m in range(tiles):
                v = f[m, pl.ds(c, 8), :]
                e = jnp.where(lane == m, pltpu.roll(v, (m - 127) % LANES, 1), e)
                e = jnp.where(lane == 64 + m, pltpu.roll(v, (64 + m - 126) % LANES, 1), e)
                w = jnp.where(lane == m, pltpu.roll(v, m % LANES, 1), w)
                w = jnp.where(lane == 64 + m, pltpu.roll(v, (64 + m - 1) % LANES, 1), w)
            east[pl.ds(c, 8), :] = e
            west[pl.ds(c, 8), :] = w
            e = jnp.zeros((8, LANES), F32)
            w = jnp.zeros((8, LANES), F32)
            for j in range(6 * lev):
                v = t[j, pl.ds(c, 8), :]
                e = jnp.where(lane == j, pltpu.roll(v, (j - 127) % LANES, 1), e)
                w = jnp.where(lane == j, pltpu.roll(v, j % LANES, 1), w)
            east[pl.ds(rows + c, 8), :] = e
            west[pl.ds(rows + c, 8), :] = w

    return call(body, [((2 * rows + 8, LANES), F32)] * 2, [VMEM, VMEM])(
        field.reshape(tiles, rows, LANES), rates.reshape(6 * lev, rows, LANES))


def masks(band, bands):
    south = jnp.where(band > 0, 1.0, 0.0).astype(F32)
    north = jnp.where(band < bands - 1, 1.0, 0.0).astype(F32)
    return south, north


def corners(east, west, before, after, band, bands):
    rows = (east.shape[0] - 8) // 2
    lev = before.shape[1]
    trc = (before.shape[0] - 6) // 2

    def body(band_ref, east_in, west_in, b, a, e_ref, w_ref):
        lane, sub = iota((lev, LANES), 1), iota((lev, LANES), 0)
        e_ref[...] = east_in[...]
        w_ref[...] = west_in[...]
        for which, (ref, mask) in enumerate(zip((b, a), masks(band_ref[0], bands))):
            to_e = jnp.zeros((lev, LANES), F32)
            to_w = jnp.zeros((lev, LANES), F32)
            for k in range(trc):
                v = ref[trc + k] * mask
                here = lane == k * lev + sub
                to_e = jnp.where(here, jnp.broadcast_to(v[:, LANES - 1 :], v.shape), to_e)
                to_w = jnp.where(here, jnp.broadcast_to(v[:, :1], v.shape), to_w)
            e_ref[pl.ds(2 * rows + which, 1), :] = jnp.sum(to_e, axis=0, keepdims=True)
            w_ref[pl.ds(2 * rows + which, 1), :] = jnp.sum(to_w, axis=0, keepdims=True)

    return call(body, [(x.shape, F32) for x in (east, west)], [SMEM] + [VMEM] * 4)(
        band, east, west, before, after)


def transport_kernel(trc, lev, rows, bands, band_ref, field, tv, w_in, e_in, my_east, my_west, b, a, my_up, my_down,
                     lam, level0, row_sums, f1, cols, gw, ge):
    high = rows + 2 * OFF
    lane = iota((8, LANES), 1)
    sub = iota((lev, LANES), 0)
    lane_l = iota((lev, LANES), 1)
    f0 = field.reshape(trc * lev * rows, LANES)
    bf, af = (x.reshape((2 * trc + 6) * lev, LANES) for x in (b, a))
    south_mask, north_mask = masks(band_ref[0], bands)
    edge = iota((8, LANES), 0)
    tvf = tv.reshape(6 * lev * rows, LANES)
    lamf = lam.reshape(trc * lev * rows, LANES)
    for which, (ref, mine, mask) in enumerate(zip((b, a), (my_down, my_up), masks(band_ref[0], bands))):
        rate = [ref[2 * trc + d] for d in range(6)]
        rate[4] = jnp.where(sub < lev - 1, rate[4], 0.0)
        rate[5] = jnp.where(sub > 0, rate[5], 0.0)
        mid = 1.0 - rate[0] - rate[1] - rate[2] - rate[3] - rate[4] - rate[5]
        west_corner = jnp.broadcast_to(w_in[pl.ds(2 * rows + which, 1), :], (lev, LANES))
        east_corner = jnp.broadcast_to(e_in[pl.ds(2 * rows + which, 1), :], (lev, LANES))
        for k in range(trc):
            c = ref[trc + k]
            far, own = ref[k], mine[trc + k]
            north, south = (own, far) if which == 0 else (far, own)
            here = lane_l == k * lev + sub
            wc = jnp.sum(jnp.where(here, west_corner, 0.0), axis=1, keepdims=True)
            ec = jnp.sum(jnp.where(here, east_corner, 0.0), axis=1, keepdims=True)
            east = jnp.where(lane_l == LANES - 1, ec, pltpu.roll(c, LANES - 1, 1))
            west = jnp.where(lane_l == 0, wc, pltpu.roll(c, 1, 1))
            upper = pltpu.roll(c, lev - 1, 0)
            lower = pltpu.roll(c, 1, 0)
            g = (mid * c + rate[0] * east + rate[1] * west + rate[2] * north + rate[3] * south
                 + rate[4] * upper + rate[5] * lower)
            at = OFF - 1 if which == 0 else OFF + rows
            f1[pl.ds(k * lev * high + at, lev, stride=high), :] = g * mask
    level_of = lane % lev
    for ref, mine, out, side in ((w_in, my_west, gw, 0), (e_in, my_east, ge, 1)):
        cols[pl.ds(OFF, rows), :] = ref[pl.ds(0, rows), :]
        cols[pl.ds(OFF - 1, 1), :] = ref[pl.ds(2 * rows, 1), :]
        cols[pl.ds(OFF + rows, 1), :] = ref[pl.ds(2 * rows + 1, 1), :]
        for r in range(0, rows, 8):
            c = cols[pl.ds(OFF + r, 8), :]
            north, south = cols[pl.ds(OFF + r + 1, 8), :], cols[pl.ds(OFF + r - 1, 8), :]
            far, own = pltpu.roll(c, 64, 1), mine[pl.ds(r, 8), :]
            east, west = (own, far) if side == 0 else (far, own)
            packed = ref[pl.ds(rows + r, 8), :]
            rate = [jnp.take_along_axis(packed, d * lev + level_of, axis=1) for d in range(6)]
            rate[4] = jnp.where(level_of < lev - 1, rate[4], 0.0)
            rate[5] = jnp.where(level_of > 0, rate[5], 0.0)
            mid = 1.0 - rate[0] - rate[1] - rate[2] - rate[3] - rate[4] - rate[5]
            upper, lower = pltpu.roll(c, LANES - 1, 1), pltpu.roll(c, 1, 1)
            out[pl.ds(r, 8), :] = (mid * c + rate[0] * east + rate[1] * west + rate[2] * north + rate[3] * south
                                   + rate[4] * upper + rate[5] * lower)

    def step(load, west_ghost, east_ghost, emit):
        for l in range(lev):
            for r in range(0, rows, 8):
                rate = [tvf[pl.ds((d * lev + l) * rows + r, 8), :] for d in range(6)]
                mid = 1.0 - rate[0] - rate[1] - rate[2] - rate[3]
                if l < lev - 1:
                    mid = mid - rate[4]
                if l > 0:
                    mid = mid - rate[5]
                wg, eg = west_ghost[pl.ds(r, 8), :], east_ghost[pl.ds(r, 8), :]
                for k in range(trc):
                    m = k * lev + l
                    c = load(k, l, r, 0)
                    west = jnp.where(lane == 0, pltpu.roll(wg, (LANES - m) % LANES, 1), pltpu.roll(c, 1, 1))
                    east = jnp.where(lane == LANES - 1, pltpu.roll(eg, LANES - 1 - m, 1), pltpu.roll(c, LANES - 1, 1))
                    v = (mid * c + rate[0] * east + rate[1] * west
                         + rate[2] * load(k, l, r, 1) + rate[3] * load(k, l, r, -1))
                    if l < lev - 1:
                        v = v + rate[4] * load(k, l + 1, r, 0)
                    if l > 0:
                        v = v + rate[5] * load(k, l - 1, r, 0)
                    emit(k, l, r, v)

    def load0(k, l, r, by):
        at = (k * lev + l) * rows + r
        if r + by < 0:
            ghost = bf[pl.ds((trc + k) * lev + l, 8, stride=0), :] * south_mask
            return jnp.where(edge == 0, ghost, pltpu.roll(f0[pl.ds(at, 8), :], 1, 0))
        if r + by + 8 > rows:
            ghost = af[pl.ds((trc + k) * lev + l, 8, stride=0), :] * north_mask
            return jnp.where(edge == 7, ghost, pltpu.roll(f0[pl.ds(at, 8), :], 7, 0))
        return f0[pl.ds(at + by, 8), :]

    def load1(k, l, r, by):
        return f1[pl.ds((k * lev + l) * high + OFF + r + by, 8), :]

    def emit1(k, l, r, v):
        f1[pl.ds((k * lev + l) * high + OFF + r, 8), :] = v

    sums = {}

    def emit2(k, l, r, v):
        lamf[pl.ds((k * lev + l) * rows + r, 8), :] = v
        if l == 0:
            level0[pl.ds(r * trc + k, 8, stride=trc), :] = v
        total = jnp.sum(v, axis=1, keepdims=True)
        old = sums[r] if k else row_sums[pl.ds(r, 8), :]
        sums[r] = jnp.where(lane == l * trc + k, total, old)
        if k == trc - 1:
            row_sums[pl.ds(r, 8), :] = sums[r]

    row_sums[...] = jnp.zeros(row_sums.shape, F32)
    step(load0, w_in, e_in, emit1)
    step(load1, gw, ge, emit2)


def transport(band, bands, field, rates, w_in, e_in, east, west, before, after, up, down, trc, lev, rows):
    high = rows + 2 * OFF
    return call(
        functools.partial(transport_kernel, trc, lev, rows, bands),
        [((trc * lev, rows, LANES), F32), ((rows * trc, LANES), F32), ((rows, LANES), F32)],
        [SMEM] + [VMEM] * 10,
        [
            pltpu.VMEM((trc * lev * high, LANES), F32),
            pltpu.VMEM((high, LANES), F32),
            pltpu.VMEM((rows, LANES), F32),
            pltpu.VMEM((rows, LANES), F32),
        ],
    )(band, field.reshape(trc * lev, rows, LANES), rates.reshape(6 * lev, rows, LANES),
      w_in, e_in, east, west, before, after, up, down)


def tables(region_local, cell_weight, polar_rows, local):
    rows, cols = region_local.shape

    def body(rl, w_ref, p_ref, hot, zc, half, w1, wz):
        eye = iota((rows, rows), 0) == iota((rows, rows), 1)
        flags = jnp.broadcast_to(p_ref[...].astype(F32), (rows, rows))
        hp = 0.5 * jnp.sum(jnp.where(eye, flags, 0.0), axis=1, keepdims=True)
        hp = jnp.broadcast_to(hp, (rows, cols))
        half[...] = hp
        w = w_ref[...]
        w1[...] = w * (1.0 - hp)
        w1z = w * hp
        row_id = iota((rows, cols), 0)
        entry = iota((local, cols), 0)
        for r in range(rows):
            hot[:, pl.ds(r * cols, cols)] = (rl[pl.ds(r, 1), :] == entry).astype(F32).astype(BF16)
            parts = split3(jnp.where(row_id == r, w1z, 0.0))
            for i in range(3):
                wz[pl.ds(i * rows, rows), pl.ds(r * cols, cols)] = parts[i].astype(BF16)
        z = lax.dot_general(wz[...], hot[...], (((1,), (1,)), ((), ())), preferred_element_type=F32)
        zc[...] = z[:rows] + z[rows : 2 * rows] + z[2 * rows :]

    return call(
        body,
        [((local, rows * cols), BF16), ((rows, local), F32), ((rows, cols), F32), ((rows, cols), F32)],
        [VMEM] * 3,
        [pltpu.VMEM((3 * rows, rows * cols), BF16)],
    )(region_local, cell_weight, polar_rows.reshape(1, rows))


def places(tile_regions, own_rows):
    count, local = tile_regions.shape
    regions = own_rows * count
    per = local // count
    owners = LANES // own_rows

    def body(tr, inv):
        lane = iota((8, LANES), 1)

        def block(i, carry):
            t = pl.multiple_of(i * 8, 8)
            for q in range(regions // LANES):
                first = q * owners * per
                src = tr[pl.ds(t, 8), pl.ds(first // LANES * LANES, LANES)]
                start = first % LANES + lane // own_rows * per
                found = jnp.full((8, LANES), -1, jnp.int32)
                for e in range(per):
                    got = jnp.take_along_axis(src, start + e, axis=1)
                    found = jnp.where(got == q * LANES + lane, start + e, found)
                inv[q, pl.ds(t, 8), :] = found
            return carry

        lax.fori_loop(0, count // 8, block, 0)

    return call(body, [((regions // LANES, count, LANES), jnp.int32)], [VMEM])(tile_regions)[0]


def local_sums(level0, w1, hot):
    rows, cols = w1.shape
    trc = level0.shape[0] // rows
    local = hot.shape[0]

    def body(l0, w, hot_ref, out, lhs):
        for r in range(rows):
            s = l0[pl.ds(r * trc, trc), :] * w[pl.ds(r, 1), :]
            hi, mid, lo = split3(s)
            at = pl.ds(r * cols, cols)
            lhs[pl.ds(0, 2 * trc), at] = jnp.concatenate([hi, mid], axis=0).astype(BF16)
            lhs[pl.ds(2 * trc, 2 * trc), at] = jnp.concatenate([lo, jnp.zeros_like(lo)], axis=0).astype(BF16)
        s = lax.dot_general(lhs[...], hot_ref[...], (((1,), (1,)), ((), ())), preferred_element_type=F32)
        out[...] = s[:trc] + s[trc : 2 * trc] + s[2 * trc : 3 * trc]

    return call(body, [((trc, local), F32)], [VMEM] * 3, [pltpu.VMEM((4 * trc, rows * cols), BF16)])(level0, w1, hot)[0]


def regional(parts, s1, zc, trc, devices, columns):
    rows, _ = parts[0].shape
    local = s1.shape[1]

    def body(*refs):
        ins, (s_ref, zc_ref, zonal, out) = refs[: len(parts)], refs[len(parts) :]
        z = ins[0][...]
        for ref in ins[1:]:
            z = z + ref[...]
        z = z / columns
        zonal[...] = z
        s = s_ref[...] + lax.dot_general(
            z[:, :trc], zc_ref[...], (((0,), (0,)), ((), ())), precision=lax.Precision.HIGHEST,
            preferred_element_type=F32)
        for d in range(devices):
            out[d] = s

    return call(body, [((rows, LANES), F32), ((devices, trc, local), F32)], [VMEM] * (len(parts) + 2))(*parts, s1, zc)


def filtered(lam, zonal, half, trc, lev):
    tiles, rows, _ = lam.shape

    def body(l_ref, z_ref, h_ref, out):
        for r in range(0, rows, 8):
            z, h = z_ref[pl.ds(r, 8), :], h_ref[pl.ds(r, 8), :]
            for m in range(tiles):
                i = m % lev * trc + m // lev
                v = l_ref[m, pl.ds(r, 8), :]
                out[m, pl.ds(r, 8), :] = v + h * (jnp.broadcast_to(z[:, i : i + 1], v.shape) - v)

    return call(body, [(lam.shape, F32)], [VMEM] * 3, keep=False)(lam, zonal, half)[0]


def finish(week, sums, inv, cov, base, trc):
    count, _, local = sums.shape
    own_rows, regions = cov.shape
    cols = base.shape[1]
    per = local // count
    owners = LANES // own_rows

    def body(week_ref, s_ref, inv_ref, cov_ref, base_ref, out, fresh):
        def block(q, carry):
            src_at = q * owners * per // LANES * LANES
            src_at = src_at if isinstance(q, int) else pl.multiple_of(src_at, LANES)
            total = [jnp.zeros((trc, LANES), F32) for _ in range(4)]
            for t in range(count):
                idx = inv_ref[q, pl.ds(t, trc, stride=0), :]
                got = jnp.take_along_axis(s_ref[t, :, pl.ds(src_at, LANES)], jnp.maximum(idx, 0), axis=1)
                total[t % 4] = total[t % 4] + jnp.where(idx >= 0, got, 0.0)
            fresh[q] = total[0] + total[1] + (total[2] + total[3])
            return carry

        blocks = regions // LANES
        if blocks <= 16:
            for q in range(blocks):
                block(q, 0)
        else:
            lax.fori_loop(0, blocks, block, 0)
        fresh_rows = jnp.concatenate([fresh[q] for q in range(blocks)], axis=1)
        wide = jnp.concatenate([fresh_rows, jnp.zeros((LANES - trc, regions), F32)], axis=0).astype(BF16)
        added = lax.dot_general(cov_ref[...], wide, (((1,), (1,)), ((), ())), preferred_element_type=F32)
        start = week_ref[0] * trc
        added = pltpu.roll(added, start % LANES, 1)
        for c in range(0, cols, LANES):
            width = min(LANES, cols - c)
            here = jnp.where(start // LANES == c // LANES, added[:, :width], 0.0)
            out[:, pl.ds(c, width)] = base_ref[:, pl.ds(c, width)] + here

    return call(
        body, [((own_rows, cols), F32)], [SMEM] + [VMEM] * 4, [pltpu.VMEM((regions // LANES, trc, LANES), F32)], keep=False
    )(week, sums, inv, cov, base)[0]


def ring(size):
    up = [(i, (i + 1) % size) for i in range(size)]
    return up, [(j, i) for i, j in up]


def partners(devices, bit):
    return [(i, i ^ bit) for i in range(devices)]


def append(parts):
    rows, cols = sum(x.shape[0] for x in parts), parts[0].shape[1]

    def body(*refs):
        at = 0
        for ref in refs[:-1]:
            refs[-1][pl.ds(at, ref.shape[0]), :] = ref[...]
            at += ref.shape[0]

    return call(body, [((rows, cols), parts[0].dtype)], [VMEM] * len(parts))(*parts)[0]


def base_product(tile, mine, theirs, cov, turn):
    own_rows, regions = cov.shape
    cols = mine.shape[1]
    half = len(turn) // 2

    def body(tile_ref, a, b, cov_ref, out, grad):
        for j, flip in enumerate(turn):
            src = a if j < half else b
            at = pl.multiple_of((tile_ref[0] ^ flip) * own_rows, own_rows)
            grad[pl.ds(at, own_rows), :] = src[pl.ds(j % half * own_rows, own_rows), :]
        out[...] = jnp.dot(cov_ref[...], grad[...], preferred_element_type=F32)

    return call(
        body, [((own_rows, cols), F32)], [SMEM] + [VMEM] * 3, [pltpu.VMEM((regions, cols), cov.dtype)]
    )(tile, mine, theirs, cov)[0]


def shards(adjoint, transport_rates, cell_weight, region_local, tile_regions, polar_rows, week_index, grad_in, covariance):
    trc, lev, rows, cols = adjoint.shape
    own_rows, _ = covariance.shape
    lats, lons = lax.axis_size("lat"), lax.axis_size("lon")
    devices = lats * lons
    band = lax.axis_index("lat").astype(jnp.int32).reshape(1)
    tile = band * lons + lax.axis_index("lon").astype(jnp.int32)
    north_to, south_to = ring(lats)
    east_to, west_to = ring(lons)

    lon_bits, bits = lons.bit_length() - 1, devices.bit_length() - 1
    order = list(range(1, lon_bits)) + list(range(lon_bits + 1, bits)) + [0, lon_bits]
    turn = [0]
    for bit in order:
        turn = turn + [j ^ (1 << bit) for j in turn]

    def exchange(i, x):
        return lax.ppermute(x, AXES, partners(devices, 1 << order[i]))

    have = grad_in
    for i in range(len(order) - 1):
        have = append([have, exchange(i, have)])
    theirs = exchange(len(order) - 1, have)

    up, down = border_rows(adjoint, transport_rates)
    before = lax.ppermute(up, "lat", north_to)
    after = lax.ppermute(down, "lat", south_to)
    east, west = border_cols(adjoint, transport_rates)
    east, west = corners(east, west, before, after, band, lats)
    w_in = lax.ppermute(east, "lon", east_to)
    e_in = lax.ppermute(west, "lon", west_to)
    hot, zc, half, w1 = tables(region_local, cell_weight, polar_rows, tile_regions.shape[1])
    inv = places(tile_regions, own_rows)
    lam, level0, row_sums = transport(
        band, lats, adjoint, transport_rates, w_in, e_in, east, west, before, after, up, down, trc, lev, rows)

    if lons <= 4:
        parts = [row_sums] + [lax.ppermute(row_sums, "lon", partners(lons, k)) for k in range(1, lons)]
    else:
        got = lax.all_to_all(
            jnp.broadcast_to(row_sums[None], (lons,) + row_sums.shape), "lon", 0, 0, tiled=True)
        parts = [jnp.sum(got, axis=0)]
    s1 = local_sums(level0, w1, hot)
    zonal, copies = regional(parts, s1, zc, trc, devices, cols * lons)
    sums = lax.all_to_all(copies, AXES, 0, 0, tiled=True)
    adjoint_out = filtered(lam, zonal, half, trc, lev).reshape(adjoint.shape)
    base = base_product(tile, have, theirs, covariance, turn)
    precond = finish(week_index, sums, inv, covariance, base, trc)
    return adjoint_out, precond


def solution(mesh):
    in_specs = (
        P(None, None, "lat", "lon"),
        P(None, None, "lat", "lon"),
        P("lat", "lon"),
        P("lat", "lon"),
        P(),
        P("lat"),
        P(),
        P(("lat", "lon"), None),
        P(("lat", "lon"), None),
    )
    out_specs = (P(None, None, "lat", "lon"), P(("lat", "lon"), None))
    return jax.shard_map(shards, mesh=mesh, in_specs=in_specs, out_specs=out_specs, check_vma=False)
```

time: 180 us -> 86.8 us (0.48)
  blocking collectives: 68.5 us -> 0 us
  other arithmetic: 35.8 us -> 0 us
  local copies, waits for them, and re-layouts: 38.5 us -> 4.6 us
  waiting for transfers between devices: 1.77 us -> 32 us
  Pallas kernels: 0 us -> 24.5 us
  between operations: 15 us -> 1.46 us
  starting transfers between devices: 14.7 us -> 24 us
  matrix products: 4.95 us -> 0 us
    psum x2 -> x0, blocking collectives: 68.5 us -> none  [the longest x1 49 us: shards(): fresh_all = lax.psum(dense, ('lat', 'lon')).astype(jnp.bfloat16)]
    ppermute x8 -> x12, waiting for transfers between devices: 1.74 us -> 27.8 us  [the longest x5 21.4 us: exchange(): return lax.ppermute(x, AXES, partners(devices, 1 << order[i]))]
    pallas_call x0 -> x15, Pallas kernels: none -> 24.5 us  [the longest x14 24.4 us: apply(): run(*(pltpu.with_memory_space_constraint(x, pltpu.VMEM) if spec is VMEM a...]
    select_n x3 -> x0, other arithmetic: 12.4 us -> none  [the longest x2 11.7 us: pole_mask(): return jnp.where(outside[None, None, :, None], 0.0, padded)]
    slice x7 -> x0, local copies, waits for them, and re-layouts: 11.7 us -> none  [the longest x3 8.58 us: extended(): last = lax.slice_in_dim(x, length - width, length, axis=dim)]
    ppermute x4 -> x1, local copies, waits for them, and re-layouts: 10.7 us -> 1.45 us  [exchange(): return lax.ppermute(x, AXES, partners(devices, 1 << order[i]))]
    add x2 -> x0, other arithmetic: 8.76 us -> none  [the longest x1 6.13 us: advance(): centre + rates[0] * to_east + rates[1] * to_west + rates[2] * to_north]
    unnamed x22 -> x20, local copies, waits for them, and re-layouts: 9.28 us -> 1.86 us
  transfers between devices with their start and end apart: 9 -> 13, of which waited for: 1 -> 8; matrix products, arithmetic and copies ran while one was open for 41% -> 2% of each run, Pallas kernels for 0% -> 25%
where the time goes in v1:
time: 86.8 us; the launch traced here: 86.6 us
  waiting for transfers between devices  32 us (37%)
  Pallas kernels  24.5 us (28%)
  starting transfers between devices  24 us (28%)
  local copies, waits for them, and re-layouts  4.6 us (5%)
  between operations  1.46 us (2%)
    pallas_call x14, Pallas kernels, apply(): run(*(pltpu.with_memory_space_constraint(x, pltpu.VMEM) if spec is VMEM a...  24.4 us
    ppermute x5, waiting for transfers between devices, exchange(): return lax.ppermute(x, AXES, partners(devices, 1 << order[i]))  21.4 us
    ppermute x5, starting transfers between devices, exchange(): return lax.ppermute(x, AXES, partners(devices, 1 << order[i]))  8.66 us
    ppermute x3, starting transfers between devices, shards(): lax.ppermute(row_sums, 'lon', partners(lons, k))  4.43 us
    all_to_all x1, waiting for transfers between devices, shards(): sums = lax.all_to_all(copies, AXES, 0, 0, tiled=True)  4.23 us
    ppermute x1, starting transfers between devices, shards(): e_in = lax.ppermute(west, 'lon', west_to)  3.78 us
    ppermute x3, waiting for transfers between devices, shards(): lax.ppermute(row_sums, 'lon', partners(lons, k))  3.6 us
    all_to_all x1, starting transfers between devices, shards(): sums = lax.all_to_all(copies, AXES, 0, 0, tiled=True)  2.58 us
  transfers between devices with their start and end apart: 13, of which 8 were waited for; matrix products, arithmetic and copies ran while one was open for 2% of the time, Pallas kernels for 25%

profile of v1, /device:TPU:0, one launch (start us, length us, event | category | flops | bytes accessed | tf_op | source)
XLA Modules:
  0.0 86.6 jit_solution(14677943498896685060)
XLA Ops:
  0.6 4.1 %collective-permute-start.7 = (bf16[64,416]{1,0:T(8,128)(2,1)}, bf16[64,416]{1,0:T(8,128)(2,1)S(1)}, u32[]{:S(2)}, u32[]{:S(2)}) collective-permute-start(bf16[64,416]{1,0:T(8,128)(2,1)} %refs_0_.1), channel_id=1, source_target_pairs={{0,2},{1,3},{2,0},{3,1},{4,6},{5,7},{6,4},{7,5},{8,10},{9,11},{10,... | collective-permute-start | bytes 159752 | tf_op jit(solution)/shard_map/ppermute | solution.py:495
  4.8 3.9 %collective-permute-done.7.refs_1_ = bf16[64,416]{1,0:T(8,128)(2,1)S(1)} collective-permute-done((bf16[64,416]{1,0:T(8,128)(2,1)}, bf16[64,416]{1,0:T(8,128)(2,1)S(1)}, u32[]{:S(2)}, u32[]{:S(2)}) %collective-permute-start.7) | collective-permute-done | bytes 53280 | tf_op jit(solution)/shard_map/ppermute | solution.py:495
  8.6 0.8 copy-done.5
  9.5 1.8 %collective-permute-start.8 = (bf16[128,416]{1,0:T(8,128)(2,1)S(1)}, bf16[128,416]{1,0:T(8,128)(2,1)S(1)}, u32[]{:S(2)}, u32[]{:S(2)}) collective-permute-start(bf16[128,416]{1,0:T(8,128)(2,1)S(1)} %shard_map.112.refs_0_), channel_id=1, source_target_pairs={{0,8},{1,9},{2,10},{3,11},{4,12},{5,13},{6,14},{7,15},{8,0},{9,1},... | collective-permute-start | bytes 319496 | tf_op jit(solution)/shard_map/ppermute | solution.py:495
  11.2 3.3 %collective-permute-done.8.refs_1_ = bf16[128,416]{1,0:T(8,128)(2,1)S(1)} collective-permute-done((bf16[128,416]{1,0:T(8,128)(2,1)S(1)}, bf16[128,416]{1,0:T(8,128)(2,1)S(1)}, u32[]{:S(2)}, u32[]{:S(2)}) %collective-permute-start.8) | collective-permute-done | bytes 106528 | tf_op jit(solution)/shard_map/ppermute | solution.py:495
  14.5 1.8 %collective-permute-start.9 = (bf16[256,416]{1,0:T(8,128)(2,1)S(1)}, bf16[256,416]{1,0:T(8,128)(2,1)S(1)}, u32[]{:S(2)}, u32[]{:S(2)}) collective-permute-start(bf16[256,416]{1,0:T(8,128)(2,1)S(1)} %shard_map.113.refs_0_), channel_id=1, source_target_pairs={{0,16},{1,17},{2,18},{3,19},{4,20},{5,21},{6,22},{7,23},{8,24},{9,... | collective-permute-start | bytes 638984 | tf_op jit(solution)/shard_map/ppermute | solution.py:495
  16.3 4.6 %collective-permute-done.9.refs_1_ = bf16[256,416]{1,0:T(8,128)(2,1)S(1)} collective-permute-done((bf16[256,416]{1,0:T(8,128)(2,1)S(1)}, bf16[256,416]{1,0:T(8,128)(2,1)S(1)}, u32[]{:S(2)}, u32[]{:S(2)}) %collective-permute-start.9) | collective-permute-done | bytes 213024 | tf_op jit(solution)/shard_map/ppermute | solution.py:495
  21.0 0.0 copy-start
  21.0 0.0 copy-start.1
  21.0 1.0 %collective-permute-start.10 = (bf16[512,416]{1,0:T(8,128)(2,1)S(1)}, bf16[512,416]{1,0:T(8,128)(2,1)S(1)}, u32[]{:S(2)}, u32[]{:S(2)}) collective-permute-start(bf16[512,416]{1,0:T(8,128)(2,1)S(1)} %shard_map.114.refs_0_), channel_id=1, source_target_pairs={{0,1},{1,0},{2,3},{3,2},{4,5},{5,4},{6,7},{7,6},{8,9},{9,8},{10,11... | collective-permute-start | bytes 1277960 | tf_op jit(solution)/shard_map/ppermute | solution.py:495
  22.0 9.6 %collective-permute-done.10.refs_1_ = bf16[512,416]{1,0:T(8,128)(2,1)S(1)} collective-permute-done((bf16[512,416]{1,0:T(8,128)(2,1)S(1)}, bf16[512,416]{1,0:T(8,128)(2,1)S(1)}, u32[]{:S(2)}, u32[]{:S(2)}) %collective-permute-start.10) | collective-permute-done | bytes 426016 | tf_op jit(solution)/shard_map/ppermute | solution.py:495
  31.6 0.1 shard_map.115.a
  31.7 1.3 %copy.11 = bf16[1024,416]{0,1:T(8,128)(2,1)} copy(bf16[1024,416]{1,0:T(8,128)(2,1)S(1)} %shard_map.115.a) | data formatting | bytes 1703936 | tf_op jit(solution)/shard_map/pallas_call | solution.py:49
  33.0 0.0 collective-permute-start.11
  33.0 0.0 copy-done
  33.0 0.0 copy-done.1
  33.0 0.1 border_rows.1
  33.1 0.6 collective-permute-start
  33.7 2.2 %collective-permute-start.1 = (f32[22,8,128]{2,1,0:T(8,128)S(1)}, f32[22,8,128]{2,1,0:T(8,128)S(1)}, u32[]{:S(2)}, u32[]{:S(2)}) collective-permute-start(f32[22,8,128]{2,1,0:T(8,128)S(1)} %get-tuple-element.20.my_down), channel_id=1, source_target_pairs={{4,0},{8,4},{12,8},{16,12},{20,16},{24,20},{28,24},{0,28},{5,1},{9... | collective-permute-start | bytes 270344 | tf_op jit(solution)/shard_map/ppermute | solution.py:504
  35.8 1.5 %shard_map.104 = (f32[72,128]{1,0:T(8,128)S(1)}, f32[72,128]{1,0:T(8,128)S(1)}) custom-call(f32[64,32,128]{2,1,0:T(8,128)S(1)} %bitcast.8, f32[48,32,128]{2,1,0:T(8,128)S(1)} %bitcast.12), custom_call_target="tpu_custom_call" | custom-call | tf_op jit(solution)/shard_map/pallas_call | solution.py:49
  37.4 0.7 collective-permute-done.b
  38.0 0.0 collective-permute-done.1.a
  38.0 0.1 shard_map.105
  38.1 1.8 %collective-permute-start.2 = (f32[72,128]{1,0:T(8,128)S(1)}, f32[72,128]{1,0:T(8,128)S(1)}, u32[]{:S(2)}, u32[]{:S(2)}) collective-permute-start(f32[72,128]{1,0:T(8,128)S(1)} %get-tuple-element.21.my_east), channel_id=1, source_target_pairs={{0,1},{1,2},{2,3},{3,0},{4,5},{5,6},{6,7},{7,4},{8,9},{9,10},{10,1... | collective-permute-start | bytes 110600 | tf_op jit(solution)/shard_map/ppermute | solution.py:507
  39.9 3.8 %collective-permute-start.3 = (f32[72,128]{1,0:T(8,128)S(1)}, f32[72,128]{1,0:T(8,128)S(1)}, u32[]{:S(2)}, u32[]{:S(2)}) collective-permute-start(f32[72,128]{1,0:T(8,128)S(1)} %get-tuple-element.22.my_west), channel_id=1, source_target_pairs={{1,0},{2,1},{3,2},{0,3},{5,4},{6,5},{7,6},{4,7},{9,8},{10,9},{11,1... | collective-permute-start | bytes 110600 | tf_op jit(solution)/shard_map/ppermute | solution.py:508
  43.7 2.1 %collective-permute-done.2.w_in = f32[72,128]{1,0:T(8,128)S(1)} collective-permute-done((f32[72,128]{1,0:T(8,128)S(1)}, f32[72,128]{1,0:T(8,128)S(1)}, u32[]{:S(2)}, u32[]{:S(2)}) %collective-permute-start.2) | collective-permute-done | bytes 36896 | tf_op jit(solution)/shard_map/ppermute | solution.py:507
  45.9 0.0 collective-permute-done.3.e_in
  45.9 13.6 %shard_map.106 = (f32[64,32,128]{2,1,0:T(8,128)S(1)}, f32[256,128]{1,0:T(8,128)S(1)}, f32[32,128]{1,0:T(8,128)S(1)}) custom-call(s32[1]{0:T(128)} %bitcast.band_ref, f32[64,32,128]{2,1,0:T(8,128)S(1)} %bitcast.9, f32[48,32,128]{2,1,0:T(8,128)S(1)} %bitcast.13, f32[72,128]{1,0:T(8,128)S(1)} %collective-permute-done.2.w_in, ...), custom_call_target="tpu_custom_call" | custom-call | tf_op jit(solution)/shard_map/pallas_call | solution.py:49
  59.5 1.0 %copy-done.2 = f32[64,32,128]{2,1,0:T(8,128)} copy-done((f32[64,32,128]{2,1,0:T(8,128)}, f32[64,32,128]{2,1,0:T(8,128)S(1)}, u32[]{:S(2)}) %copy-start.2) | copy-done | bytes 1048600
  60.5 1.5 %collective-permute-start.4 = (f32[32,128]{1,0:T(8,128)S(1)}, f32[32,128]{1,0:T(8,128)S(1)}, u32[]{:S(2)}, u32[]{:S(2)}) collective-permute-start(f32[32,128]{1,0:T(8,128)S(1)} %get-tuple-element.24.refs_0_), channel_id=1, source_target_pairs={{0,1},{1,0},{2,3},{3,2},{4,5},{5,4},{6,7},{7,6},{8,9},{9,8},{10,11... | collective-permute-start | bytes 49160 | tf_op jit(solution)/shard_map/ppermute | solution.py:515
  61.9 3.0 %collective-permute-start.5 = (f32[32,128]{1,0:T(8,128)S(1)}, f32[32,128]{1,0:T(8,128)S(1)}, u32[]{:S(2)}, u32[]{:S(2)}) collective-permute-start(f32[32,128]{1,0:T(8,128)S(1)} %get-tuple-element.24.refs_0_), channel_id=1, source_target_pairs={{0,2},{1,3},{2,0},{3,1},{4,6},{5,7},{6,4},{7,5},{8,10},{9,11},{10,... | collective-permute-start | bytes 49160 | tf_op jit(solution)/shard_map/ppermute | solution.py:515
  64.9 0.0 collective-permute-start.6
  64.9 1.1 %shard_map.107 = (bf16[256,4096]{1,0:T(8,128)(2,1)S(1)}, f32[32,256]{1,0:T(8,128)S(1)}, f32[32,128]{1,0:T(8,128)S(1)}, f32[32,128]{1,0:T(8,128)S(1)}) custom-call(s32[32,128]{1,0:T(8,128)S(1)} %copy-done.7, f32[32,128]{1,0:T(8,128)S(1)} %copy-done.8, s32[1,32]{1,0:T(1,128)S(1)} %bitcast.14), custom_call_target="tpu_custom_call" | custom-call | tf_op jit(solution)/shard_map/pallas_call | solution.py:49
  66.0 0.8 shard_map.108.refs_4_
  66.8 0.0 collective-permute-done.4.refs_1_
  66.8 0.0 collective-permute-done.5.refs_2_
  66.9 3.6 %collective-permute-done.6.refs_3_ = f32[32,128]{1,0:T(8,128)S(1)} collective-permute-done((f32[32,128]{1,0:T(8,128)S(1)}, f32[32,128]{1,0:T(8,128)S(1)}, u32[]{:S(2)}, u32[]{:S(2)}) %collective-permute-start.6) | collective-permute-done | bytes 16416 | tf_op jit(solution)/shard_map/ppermute | solution.py:515
  70.4 0.9 %shard_map.109 = (f32[32,128]{1,0:T(8,128)S(1)}, f32[32,8,256]{2,1,0:T(8,128)}) custom-call(f32[32,128]{1,0:T(8,128)S(1)} %get-tuple-element.24.refs_0_, f32[32,128]{1,0:T(8,128)S(1)} %collective-permute-done.4.refs_1_, f32[32,128]{1,0:T(8,128)S(1)} %collective-permute-done.5.refs_2_, f32[32,128]{1,0:T(8,128)S(1)} %collective-permute-done.6.refs_3_, ...), custom_call_target="tpu_custom_call" | custom-call | tf_op jit(solution)/shard_map/pallas_call | solution.py:49
  71.4 2.6 %all-to-all-start = ((f32[32,8,256]{2,1,0:T(8,128)}), f32[32,8,256]{2,1,0:T(8,128)S(1)}, u32[]{:S(2)}, u32[]{:S(2)}) async-start(f32[32,8,256]{2,1,0:T(8,128)} %get-tuple-element.31), calls=%async_computation | async-start | bytes 524288 | tf_op jit(solution)/shard_map/all_to_all | solution.py:522
  74.0 0.0 copy-done.6
  74.0 0.0 copy-start.4
  74.0 1.7 %shard_map.111.inv_ref = s32[16,32,128]{2,1,0:T(8,128)S(1)} custom-call(s32[32,256]{1,0:T(8,128)S(1)} %copy-done.6), custom_call_target="tpu_custom_call" | custom-call | tf_op jit(solution)/shard_map/pallas_call | solution.py:49
  76.4 1.5 %shard_map.110 = f32[64,32,128]{2,1,0:T(8,128)} custom-call(f32[64,32,128]{2,1,0:T(8,128)S(1)} %copy-done.3, f32[32,128]{1,0:T(8,128)S(1)} %get-tuple-element.29.z_ref, f32[32,128]{1,0:T(8,128)S(1)} %get-tuple-element.30.h_ref), custom_call_target="tpu_custom_call" | custom-call | tf_op jit(solution)/shard_map/pallas_call | solution.py:49
  77.9 0.0 collective-permute-done.11
  77.9 1.4 %copy.12.b = bf16[1024,416]{1,0:T(8,128)(2,1)S(1)} copy(bf16[1024,416]{0,1:T(8,128)(2,1)} %collective-permute-done.11) | data formatting | bytes 1703936 | tf_op jit(solution)/shard_map/ppermute | solution.py:495
  79.3 0.6 shard_map.116.base_ref
  80.0 4.2 %all-to-all-done.s_ref = f32[32,8,256]{2,1,0:T(8,128)S(1)} async-done(((f32[32,8,256]{2,1,0:T(8,128)}), f32[32,8,256]{2,1,0:T(8,128)S(1)}, u32[]{:S(2)}, u32[]{:S(2)}) %all-to-all-start) | async-done | bytes 262176 | tf_op jit(solution)/shard_map/all_to_all | solution.py:522
  84.2 2.4 %shard_map.117 = f32[64,416]{1,0:T(8,128)} custom-call(s32[1]{0:T(128)S(6)} %copy.13.week_ref, f32[32,8,256]{2,1,0:T(8,128)S(1)} %all-to-all-done.s_ref, s32[16,32,128]{2,1,0:T(8,128)S(1)} %shard_map.111.inv_ref, bf16[64,2048]{1,0:T(8,128)(2,1)S(1)} %copy-done.4, f32[64,416]{1,0:T(8,128)S(1)} %shard_map.116.base_ref), custom_call_target="tpu_custom_call" | custom-call | tf_op jit(solution)/shard_map/pallas_call | solution.py:49
  (15 shorter events, 0.1 us)
Async XLA Ops:
  0.6 8.0 %collective-permute-start.7 = (bf16[64,416]{1,0:T(8,128)(2,1)}, bf16[64,416]{1,0:T(8,128)(2,1)S(1)}, u32[]{:S(2)}, u32[]{:S(2)}) collective-permute-start(bf16[64,416]{1,0:T(8,128)(2,1)} %refs_0_.1), channel_id=1, source_target_pairs={{0,2},{1,3},{2,0},{3,1},{4,6},{5,7},{6,4},{7,5},{8,10},{9,11},{10,... | collective-permute-start | bytes 159752 | tf_op jit(solution)/shard_map/ppermute | solution.py:495
  8.6 0.8 copy-start.5
  9.5 5.0 %collective-permute-start.8 = (bf16[128,416]{1,0:T(8,128)(2,1)S(1)}, bf16[128,416]{1,0:T(8,128)(2,1)S(1)}, u32[]{:S(2)}, u32[]{:S(2)}) collective-permute-start(bf16[128,416]{1,0:T(8,128)(2,1)S(1)} %shard_map.112.refs_0_), channel_id=1, source_target_pairs={{0,8},{1,9},{2,10},{3,11},{4,12},{5,13},{6,14},{7,15},{8,0},{9,1},... | collective-permute-start | bytes 319496 | tf_op jit(solution)/shard_map/ppermute | solution.py:495
  14.5 6.4 %collective-permute-start.9 = (bf16[256,416]{1,0:T(8,128)(2,1)S(1)}, bf16[256,416]{1,0:T(8,128)(2,1)S(1)}, u32[]{:S(2)}, u32[]{:S(2)}) collective-permute-start(bf16[256,416]{1,0:T(8,128)(2,1)S(1)} %shard_map.113.refs_0_), channel_id=1, source_target_pairs={{0,16},{1,17},{2,18},{3,19},{4,20},{5,21},{6,22},{7,23},{8,24},{9,... | collective-permute-start | bytes 638984 | tf_op jit(solution)/shard_map/ppermute | solution.py:495
  21.0 12.0 %copy-start = (f32[8,8,32,128]{3,2,1,0:T(8,128)S(1)}, f32[8,8,32,128]{3,2,1,0:T(8,128)}, u32[]{:S(2)}) copy-start(f32[8,8,32,128]{3,2,1,0:T(8,128)} %param.9) | copy-start | bytes 3145732
  21.0 12.0 %copy-start.1 = (f32[6,8,32,128]{3,2,1,0:T(8,128)S(1)}, f32[6,8,32,128]{3,2,1,0:T(8,128)}, u32[]{:S(2)}) copy-start(f32[6,8,32,128]{3,2,1,0:T(8,128)} %param.10) | copy-start | bytes 2359300
  21.0 10.6 %collective-permute-start.10 = (bf16[512,416]{1,0:T(8,128)(2,1)S(1)}, bf16[512,416]{1,0:T(8,128)(2,1)S(1)}, u32[]{:S(2)}, u32[]{:S(2)}) collective-permute-start(bf16[512,416]{1,0:T(8,128)(2,1)S(1)} %shard_map.114.refs_0_), channel_id=1, source_target_pairs={{0,1},{1,0},{2,3},{3,2},{4,5},{5,4},{6,7},{7,6},{8,9},{9,8},{10,11... | collective-permute-start | bytes 1277960 | tf_op jit(solution)/shard_map/ppermute | solution.py:495
  33.0 44.9 %collective-permute-start.11 = (bf16[1024,416]{0,1:T(8,128)(2,1)}, bf16[1024,416]{0,1:T(8,128)(2,1)}, u32[]{:S(2)}, u32[]{:S(2)}) collective-permute-start(bf16[1024,416]{0,1:T(8,128)(2,1)} %copy.11), channel_id=1, source_target_pairs={{0,4},{1,5},{2,6},{3,7},{4,0},{5,1},{6,2},{7,3},{8,12},{9,13},{10,... | collective-permute-start | bytes 2555912 | tf_op jit(solution)/shard_map/ppermute | solution.py:495
  33.1 4.9 %collective-permute-start = (f32[22,8,128]{2,1,0:T(8,128)S(1)}, f32[22,8,128]{2,1,0:T(8,128)S(1)}, u32[]{:S(2)}, u32[]{:S(2)}) collective-permute-start(f32[22,8,128]{2,1,0:T(8,128)S(1)} %get-tuple-element.19.my_up), channel_id=1, source_target_pairs={{0,4},{4,8},{8,12},{12,16},{16,20},{20,24},{24,28},{28,0},{1,5},{5... | collective-permute-start | bytes 270344 | tf_op jit(solution)/shard_map/ppermute | solution.py:503
  33.7 31.3 %copy-start.7 = (s32[32,128]{1,0:T(8,128)S(1)}, s32[32,128]{1,0:T(8,128)}, u32[]{:S(2)}) copy-start(s32[32,128]{1,0:T(8,128)} %rl.1) | copy-start | bytes 49156
  33.7 31.3 %copy-start.8 = (f32[32,128]{1,0:T(8,128)S(1)}, f32[32,128]{1,0:T(8,128)}, u32[]{:S(2)}) copy-start(f32[32,128]{1,0:T(8,128)} %w_ref.1) | copy-start | bytes 49156
  33.7 31.3 %copy-start.9 = (s32[32]{0:T(128)S(1)}, s32[32]{0:T(128)}, u32[]{:S(2)}) copy-start(s32[32]{0:T(128)} %param.14) | copy-start | bytes 388
  33.7 4.4 %collective-permute-start.1 = (f32[22,8,128]{2,1,0:T(8,128)S(1)}, f32[22,8,128]{2,1,0:T(8,128)S(1)}, u32[]{:S(2)}, u32[]{:S(2)}) collective-permute-start(f32[22,8,128]{2,1,0:T(8,128)S(1)} %get-tuple-element.20.my_down), channel_id=1, source_target_pairs={{4,0},{8,4},{12,8},{16,12},{20,16},{24,20},{28,24},{0,28},{5,1},{9... | collective-permute-start | bytes 270344 | tf_op jit(solution)/shard_map/ppermute | solution.py:504
  38.1 7.7 %collective-permute-start.2 = (f32[72,128]{1,0:T(8,128)S(1)}, f32[72,128]{1,0:T(8,128)S(1)}, u32[]{:S(2)}, u32[]{:S(2)}) collective-permute-start(f32[72,128]{1,0:T(8,128)S(1)} %get-tuple-element.21.my_east), channel_id=1, source_target_pairs={{0,1},{1,2},{2,3},{3,0},{4,5},{5,6},{6,7},{7,4},{8,9},{9,10},{10,1... | collective-permute-start | bytes 110600 | tf_op jit(solution)/shard_map/ppermute | solution.py:507
  39.9 34.0 %copy-start.6 = (s32[32,256]{1,0:T(8,128)S(1)}, s32[32,256]{1,0:T(8,128)}, u32[]{:S(2)}) copy-start(s32[32,256]{1,0:T(8,128)} %tr.1) | copy-start | bytes 98308
  39.9 5.9 %collective-permute-start.3 = (f32[72,128]{1,0:T(8,128)S(1)}, f32[72,128]{1,0:T(8,128)S(1)}, u32[]{:S(2)}, u32[]{:S(2)}) collective-permute-start(f32[72,128]{1,0:T(8,128)S(1)} %get-tuple-element.22.my_west), channel_id=1, source_target_pairs={{1,0},{2,1},{3,2},{0,3},{5,4},{6,5},{7,6},{4,7},{9,8},{10,9},{11,1... | collective-permute-start | bytes 110600 | tf_op jit(solution)/shard_map/ppermute | solution.py:508
  59.5 1.0 %copy-start.2 = (f32[64,32,128]{2,1,0:T(8,128)}, f32[64,32,128]{2,1,0:T(8,128)S(1)}, u32[]{:S(2)}) copy-start(f32[64,32,128]{2,1,0:T(8,128)S(1)} %get-tuple-element.23.l_ref) | copy-start | bytes 3145732
  60.5 15.9 %copy-start.3 = (f32[64,32,128]{2,1,0:T(8,128)S(1)}, f32[64,32,128]{2,1,0:T(8,128)}, u32[]{:S(2)}) copy-start(f32[64,32,128]{2,1,0:T(8,128)} %copy-done.2) | copy-start | bytes 3145732
  60.5 6.4 %collective-permute-start.4 = (f32[32,128]{1,0:T(8,128)S(1)}, f32[32,128]{1,0:T(8,128)S(1)}, u32[]{:S(2)}, u32[]{:S(2)}) collective-permute-start(f32[32,128]{1,0:T(8,128)S(1)} %get-tuple-element.24.refs_0_), channel_id=1, source_target_pairs={{0,1},{1,0},{2,3},{3,2},{4,5},{5,4},{6,7},{7,6},{8,9},{9,8},{10,11... | collective-permute-start | bytes 49160 | tf_op jit(solution)/shard_map/ppermute | solution.py:515
  61.9 4.9 %collective-permute-start.5 = (f32[32,128]{1,0:T(8,128)S(1)}, f32[32,128]{1,0:T(8,128)S(1)}, u32[]{:S(2)}, u32[]{:S(2)}) collective-permute-start(f32[32,128]{1,0:T(8,128)S(1)} %get-tuple-element.24.refs_0_), channel_id=1, source_target_pairs={{0,2},{1,3},{2,0},{3,1},{4,6},{5,7},{6,4},{7,5},{8,10},{9,11},{10,... | collective-permute-start | bytes 49160 | tf_op jit(solution)/shard_map/ppermute | solution.py:515
  64.9 5.5 %collective-permute-start.6 = (f32[32,128]{1,0:T(8,128)S(1)}, f32[32,128]{1,0:T(8,128)S(1)}, u32[]{:S(2)}, u32[]{:S(2)}) collective-permute-start(f32[32,128]{1,0:T(8,128)S(1)} %get-tuple-element.24.refs_0_), channel_id=1, source_target_pairs={{0,3},{1,2},{2,1},{3,0},{4,7},{5,6},{6,5},{7,4},{8,11},{9,10},{10,... | collective-permute-start | bytes 49160 | tf_op jit(solution)/shard_map/ppermute | solution.py:515
  71.4 12.8 %all-to-all-start = ((f32[32,8,256]{2,1,0:T(8,128)}), f32[32,8,256]{2,1,0:T(8,128)S(1)}, u32[]{:S(2)}, u32[]{:S(2)}) async-start(f32[32,8,256]{2,1,0:T(8,128)} %get-tuple-element.31), calls=%async_computation | async-start | bytes 524288 | tf_op jit(solution)/shard_map/all_to_all | solution.py:522
  74.0 5.4 %copy-start.4 = (bf16[64,2048]{1,0:T(8,128)(2,1)S(1)}, bf16[64,2048]{1,0:T(8,128)(2,1)}, u32[]{:S(2)}) copy-start(bf16[64,2048]{1,0:T(8,128)(2,1)} %cov_ref.3) | copy-start | bytes 786436

commit v2 on v1

--- a/solution.py
+++ b/solution.py
@@ -7,6 +7,7 @@
 from jax.experimental import pallas as pl
 from jax.experimental.pallas import tpu as pltpu
 from jax.sharding import PartitionSpec as P
+
 
 AXES = ("lat", "lon")
 F32 = jnp.float32
@@ -34,7 +35,7 @@
         return pltpu.VMEM(s, d) if keep and nbytes(s, d) <= BIG else jax.ShapeDtypeStruct(s, d)
 
     def apply(*args):
-        own = sum(nbytes(x.shape, x.dtype) for x in scratch if x.memory_space == pltpu.VMEM)
+        own = sum(nbytes(x.shape, x.dtype) for x in scratch if getattr(x, "memory_space", None) == pltpu.VMEM)
         own += sum(nbytes(x.shape, x.dtype) for x in args if nbytes(x.shape, x.dtype) > BIG)
         own += sum(nbytes(s, d) for s, d in outs if not keep or nbytes(s, d) > BIG)
         run = pl.pallas_call(
@@ -46,9 +47,15 @@
             input_output_aliases=aliases or {},
             compiler_params=pltpu.CompilerParams(vmem_limit_bytes=own + (6 << 20)),
         )
-        return run(*(pltpu.with_memory_space_constraint(x, pltpu.VMEM)
-                     if spec is VMEM and nbytes(x.shape, x.dtype) <= BIG else x
-                     for x, spec in zip(args, in_specs)))
+
+        def place(x, spec):
+            if spec is HBM:
+                return pltpu.with_memory_space_constraint(x, pltpu.HBM)
+            if spec is VMEM and nbytes(x.shape, x.dtype) <= BIG:
+                return pltpu.with_memory_space_constraint(x, pltpu.VMEM)
+            return x
+
+        return run(*(place(x, spec) for x, spec in zip(args, in_specs)))
 
     return apply
 
@@ -60,45 +67,44 @@
     return hi, mid, rest - mid
 
 
-def rows_kernel(trc, lev, f_last, f_first, t_last, t_first, up, down):
-    def row(ref, group, at):
-        return ref[pl.ds(group * lev * 8 + at, lev, stride=8), :]
-
-    for k in range(trc):
-        up[k] = row(f_last, k, 6)
-        up[trc + k] = row(f_last, k, 7)
-        down[k] = row(f_first, k, 1)
-        down[trc + k] = row(f_first, k, 0)
-    for d in range(6):
-        up[2 * trc + d] = row(t_last, d, 7)
-        down[2 * trc + d] = row(t_first, d, 0)
-
-
 def border_rows(field, rates):
     trc, lev, rows, _ = field.shape
-    last = rows // 8 - 1
-
-    def body(f_last, f_first, t_last, t_first, up, down):
-        flat = lambda ref: ref.reshape(ref.shape[0] * 8, LANES)
-        rows_kernel(trc, lev, flat(f_last), flat(f_first), flat(t_last), flat(t_first), up, down)
-
-    f3 = field.reshape(trc * lev, rows, LANES)
-    t3 = rates.reshape(6 * lev, rows, LANES)
-    out = pltpu.VMEM((2 * trc + 6, lev, LANES), F32)
-    return pl.pallas_call(
+    tiles = trc * lev
+
+    def body(f, t, up, down, f_last, f_first, t_last, t_first, sem):
+        moves = [
+            pltpu.make_async_copy(src.at[:, pl.ds(at, 8), :], dst, sem.at[i])
+            for i, (src, at, dst) in enumerate(
+                ((f, rows - 8, f_last), (f, 0, f_first), (t, rows - 8, t_last), (t, 0, t_first)))
+        ]
+        for move in moves:
+            move.start()
+
+        def row(ref, group, at):
+            return ref.reshape(ref.shape[0] * 8, LANES)[pl.ds(group * lev * 8 + at, lev, stride=8), :]
+
+        moves[0].wait()
+        for k in range(trc):
+            up[k] = row(f_last, k, 6)
+            up[trc + k] = row(f_last, k, 7)
+        moves[1].wait()
+        for k in range(trc):
+            down[k] = row(f_first, k, 1)
+            down[trc + k] = row(f_first, k, 0)
+        moves[2].wait()
+        for d in range(6):
+            up[2 * trc + d] = row(t_last, d, 7)
+        moves[3].wait()
+        for d in range(6):
+            down[2 * trc + d] = row(t_first, d, 0)
+
+    out = ((2 * trc + 6, lev, LANES), F32)
+    return call(
         body,
-        grid=(1,),
-        out_shape=[out, out],
-        in_specs=[
-            pl.BlockSpec((trc * lev, 8, LANES), lambda i: (0, last, 0)),
-            pl.BlockSpec((trc * lev, 8, LANES), lambda i: (0, 0, 0)),
-            pl.BlockSpec((6 * lev, 8, LANES), lambda i: (0, last, 0)),
-            pl.BlockSpec((6 * lev, 8, LANES), lambda i: (0, 0, 0)),
-        ],
-        out_specs=[VMEM] * 2,
-        compiler_params=pltpu.CompilerParams(vmem_limit_bytes=8 << 20),
-        name="border_rows",
-    )(f3, f3, t3, t3)
+        [out, out],
+        [HBM, HBM],
+        [pltpu.VMEM((n, 8, LANES), F32) for n in (tiles, tiles, 6 * lev, 6 * lev)] + [pltpu.SemaphoreType.DMA((4,))],
+    )(field.reshape(tiles, rows, LANES), rates.reshape(6 * lev, rows, LANES))
 
 
 def border_cols(field, rates):
@@ -164,22 +170,24 @@
 
 
 def transport_kernel(trc, lev, rows, bands, band_ref, field, tv, w_in, e_in, my_east, my_west, b, a, my_up, my_down,
-                     lam, level0, row_sums, f1, cols, gw, ge):
+                     lam, level0, row_sums, f1, cols, ghost0, ghost1, mids, halves):
     high = rows + 2 * OFF
     lane = iota((8, LANES), 1)
     sub = iota((lev, LANES), 0)
     lane_l = iota((lev, LANES), 1)
-    f0 = field.reshape(trc * lev * rows, LANES)
     bf, af = (x.reshape((2 * trc + 6) * lev, LANES) for x in (b, a))
+    f1_flat = f1.reshape(trc * lev * high, LANES)
     south_mask, north_mask = masks(band_ref[0], bands)
     edge = iota((8, LANES), 0)
-    tvf = tv.reshape(6 * lev * rows, LANES)
-    lamf = lam.reshape(trc * lev * rows, LANES)
-    for which, (ref, mine, mask) in enumerate(zip((b, a), (my_down, my_up), masks(band_ref[0], bands))):
+
+    def centre(rate):
+        return 1.0 - rate[0] - rate[1] - rate[2] - rate[3] - rate[4] - rate[5]
+
+    for which, (ref, mine, mask) in enumerate(zip((b, a), (my_down, my_up), (south_mask, north_mask))):
         rate = [ref[2 * trc + d] for d in range(6)]
         rate[4] = jnp.where(sub < lev - 1, rate[4], 0.0)
         rate[5] = jnp.where(sub > 0, rate[5], 0.0)
-        mid = 1.0 - rate[0] - rate[1] - rate[2] - rate[3] - rate[4] - rate[5]
+        mid = centre(rate)
         west_corner = jnp.broadcast_to(w_in[pl.ds(2 * rows + which, 1), :], (lev, LANES))
         east_corner = jnp.broadcast_to(e_in[pl.ds(2 * rows + which, 1), :], (lev, LANES))
         for k in range(trc):
@@ -196,80 +204,101 @@
             g = (mid * c + rate[0] * east + rate[1] * west + rate[2] * north + rate[3] * south
                  + rate[4] * upper + rate[5] * lower)
             at = OFF - 1 if which == 0 else OFF + rows
-            f1[pl.ds(k * lev * high + at, lev, stride=high), :] = g * mask
+            f1_flat[pl.ds(k * lev * high + at, lev, stride=high), :] = g * mask
     level_of = lane % lev
-    for ref, mine, out, side in ((w_in, my_west, gw, 0), (e_in, my_east, ge, 1)):
-        cols[pl.ds(OFF, rows), :] = ref[pl.ds(0, rows), :]
-        cols[pl.ds(OFF - 1, 1), :] = ref[pl.ds(2 * rows, 1), :]
-        cols[pl.ds(OFF + rows, 1), :] = ref[pl.ds(2 * rows + 1, 1), :]
-        for r in range(0, rows, 8):
-            c = cols[pl.ds(OFF + r, 8), :]
-            north, south = cols[pl.ds(OFF + r + 1, 8), :], cols[pl.ds(OFF + r - 1, 8), :]
+    from_west, from_east = lane // 2, (lane + 1) // 2 % 64
+
+    def ghosts(west, east):
+        return jnp.where(lane % 2 == 0, jnp.take_along_axis(west, from_west, axis=1),
+                         jnp.take_along_axis(east, from_east, axis=1))
+
+    for side, ref in enumerate((w_in, e_in)):
+        cols[side, pl.ds(OFF, rows), :] = ref[pl.ds(0, rows), :]
+        cols[side, pl.ds(OFF - 1, 1), :] = ref[pl.ds(2 * rows, 1), :]
+        cols[side, pl.ds(OFF + rows, 1), :] = ref[pl.ds(2 * rows + 1, 1), :]
+    for r in range(0, rows, 8):
+        stepped = []
+        for side, (ref, mine) in enumerate(((w_in, my_west), (e_in, my_east))):
+            c = cols[side, pl.ds(OFF + r, 8), :]
+            north, south = cols[side, pl.ds(OFF + r + 1, 8), :], cols[side, pl.ds(OFF + r - 1, 8), :]
             far, own = pltpu.roll(c, 64, 1), mine[pl.ds(r, 8), :]
             east, west = (own, far) if side == 0 else (far, own)
             packed = ref[pl.ds(rows + r, 8), :]
             rate = [jnp.take_along_axis(packed, d * lev + level_of, axis=1) for d in range(6)]
             rate[4] = jnp.where(level_of < lev - 1, rate[4], 0.0)
             rate[5] = jnp.where(level_of > 0, rate[5], 0.0)
-            mid = 1.0 - rate[0] - rate[1] - rate[2] - rate[3] - rate[4] - rate[5]
             upper, lower = pltpu.roll(c, LANES - 1, 1), pltpu.roll(c, 1, 1)
-            out[pl.ds(r, 8), :] = (mid * c + rate[0] * east + rate[1] * west + rate[2] * north + rate[3] * south
-                                   + rate[4] * upper + rate[5] * lower)
-
-    def step(load, west_ghost, east_ghost, emit):
-        for l in range(lev):
-            for r in range(0, rows, 8):
-                rate = [tvf[pl.ds((d * lev + l) * rows + r, 8), :] for d in range(6)]
-                mid = 1.0 - rate[0] - rate[1] - rate[2] - rate[3]
-                if l < lev - 1:
-                    mid = mid - rate[4]
-                if l > 0:
-                    mid = mid - rate[5]
-                wg, eg = west_ghost[pl.ds(r, 8), :], east_ghost[pl.ds(r, 8), :]
-                for k in range(trc):
-                    m = k * lev + l
+            stepped.append(centre(rate) * c + rate[0] * east + rate[1] * west + rate[2] * north + rate[3] * south
+                           + rate[4] * upper + rate[5] * lower)
+        ghost0[pl.ds(r, 8), :] = ghosts(w_in[pl.ds(r, 8), :], e_in[pl.ds(r, 8), :])
+        ghost1[pl.ds(r, 8), :] = ghosts(*stepped)
+    for l in range(lev):
+        for r in range(0, rows, 8):
+            rate = [tv[d * lev + l, pl.ds(r, 8), :] for d in range(6)]
+            if l == lev - 1:
+                rate[4] = jnp.zeros_like(rate[4])
+            if l == 0:
+                rate[5] = jnp.zeros_like(rate[5])
+            mids[l, pl.ds(r, 8), :] = centre(rate)
+    row_sums[...] = jnp.zeros(row_sums.shape, F32)
+
+    def step(load, ghost, emit, after):
+        def tracer(k, carry):
+            for l in range(lev):
+                for r in range(0, rows, 8):
+                    rate = [tv[d * lev + l, pl.ds(r, 8), :] for d in range(6)]
                     c = load(k, l, r, 0)
-                    west = jnp.where(lane == 0, pltpu.roll(wg, (LANES - m) % LANES, 1), pltpu.roll(c, 1, 1))
-                    east = jnp.where(lane == LANES - 1, pltpu.roll(eg, LANES - 1 - m, 1), pltpu.roll(c, LANES - 1, 1))
-                    v = (mid * c + rate[0] * east + rate[1] * west
-                         + rate[2] * load(k, l, r, 1) + rate[3] * load(k, l, r, -1))
+                    g = pltpu.roll(ghost[pl.ds(r, 8), :], (LANES - 2 * (k * lev + l)) % LANES, 1)
+                    west = jnp.where(lane == 0, g, pltpu.roll(c, 1, 1))
+                    east = jnp.where(lane == LANES - 1, g, pltpu.roll(c, LANES - 1, 1))
+                    v = (mids[l, pl.ds(r, 8), :] * c + rate[2] * load(k, l, r, 1) + rate[3] * load(k, l, r, -1))
                     if l < lev - 1:
                         v = v + rate[4] * load(k, l + 1, r, 0)
                     if l > 0:
                         v = v + rate[5] * load(k, l - 1, r, 0)
-                    emit(k, l, r, v)
+                    emit(k, l, r, v + (rate[0] * east + rate[1] * west))
+            after(k)
+            return carry
+
+        lax.fori_loop(0, trc, tracer, 0)
 
     def load0(k, l, r, by):
-        at = (k * lev + l) * rows + r
+        m = k * lev + l
         if r + by < 0:
             ghost = bf[pl.ds((trc + k) * lev + l, 8, stride=0), :] * south_mask
-            return jnp.where(edge == 0, ghost, pltpu.roll(f0[pl.ds(at, 8), :], 1, 0))
+            return jnp.where(edge == 0, ghost, pltpu.roll(field[m, pl.ds(0, 8), :], 1, 0))
         if r + by + 8 > rows:
             ghost = af[pl.ds((trc + k) * lev + l, 8, stride=0), :] * north_mask
-            return jnp.where(edge == 7, ghost, pltpu.roll(f0[pl.ds(at, 8), :], 7, 0))
-        return f0[pl.ds(at + by, 8), :]
+            return jnp.where(edge == 7, ghost, pltpu.roll(field[m, pl.ds(rows - 8, 8), :], 7, 0))
+        return field[m, pl.ds(r + by, 8), :]
 
     def load1(k, l, r, by):
-        return f1[pl.ds((k * lev + l) * high + OFF + r + by, 8), :]
+        return f1[k * lev + l, pl.ds(OFF + r + by, 8), :]
 
     def emit1(k, l, r, v):
-        f1[pl.ds((k * lev + l) * high + OFF + r, 8), :] = v
-
-    sums = {}
+        f1[k * lev + l, pl.ds(OFF + r, 8), :] = v
 
     def emit2(k, l, r, v):
-        lamf[pl.ds((k * lev + l) * rows + r, 8), :] = v
+        lam[k * lev + l, pl.ds(r, 8), :] = v
         if l == 0:
             level0[pl.ds(r * trc + k, 8, stride=trc), :] = v
-        total = jnp.sum(v, axis=1, keepdims=True)
-        old = sums[r] if k else row_sums[pl.ds(r, 8), :]
-        sums[r] = jnp.where(lane == l * trc + k, total, old)
-        if k == trc - 1:
-            row_sums[pl.ds(r, 8), :] = sums[r]
-
-    row_sums[...] = jnp.zeros(row_sums.shape, F32)
-    step(load0, w_in, e_in, emit1)
-    step(load1, gw, ge, emit2)
+
+    def sums(k):
+        for l in range(lev):
+            for r in range(0, rows, 16):
+                v = lam[k * lev + l, pl.ds(r, 16), :]
+                hi = v.astype(BF16)
+                halves[pl.ds(l * rows + r, 16), pl.ds(0, LANES)] = hi
+                halves[pl.ds(l * rows + r, 16), pl.ds(LANES, LANES)] = (v - hi.astype(F32)).astype(BF16)
+        total = jnp.dot(halves[...], jnp.ones((2 * LANES, LANES), BF16), preferred_element_type=F32)
+        for r in range(0, rows, 8):
+            old = row_sums[pl.ds(r, 8), :]
+            for l in range(lev):
+                old = jnp.where(lane == l * trc + k, total[l * rows + r : l * rows + r + 8], old)
+            row_sums[pl.ds(r, 8), :] = old
+
+    step(load0, ghost0, emit1, lambda k: None)
+    step(load1, ghost1, emit2, sums)
 
 
 def transport(band, bands, field, rates, w_in, e_in, east, west, before, after, up, down, trc, lev, rows):
@@ -279,10 +308,12 @@
         [((trc * lev, rows, LANES), F32), ((rows * trc, LANES), F32), ((rows, LANES), F32)],
         [SMEM] + [VMEM] * 10,
         [
-            pltpu.VMEM((trc * lev * high, LANES), F32),
-            pltpu.VMEM((high, LANES), F32),
+            pltpu.VMEM((trc * lev, high, LANES), F32),
+            pltpu.VMEM((2, high, LANES), F32),
             pltpu.VMEM((rows, LANES), F32),
             pltpu.VMEM((rows, LANES), F32),
+            pltpu.VMEM((lev, rows, LANES), F32),
+            pltpu.VMEM((lev * rows, 2 * LANES), BF16),
         ],
     )(band, field.reshape(trc * lev, rows, LANES), rates.reshape(6 * lev, rows, LANES),
       w_in, e_in, east, west, before, after, up, down)
@@ -446,21 +477,25 @@
     return [(i, i ^ bit) for i in range(devices)]
 
 
-def append(parts):
-    rows, cols = sum(x.shape[0] for x in parts), parts[0].shape[1]
+def append(parts, cols):
+    rows = sum(x.shape[0] for x in parts)
 
     def body(*refs):
         at = 0
         for ref in refs[:-1]:
-            refs[-1][pl.ds(at, ref.shape[0]), :] = ref[...]
+            here = pl.ds(at, ref.shape[0])
+            refs[-1][here, pl.ds(0, ref.shape[1])] = ref[...]
+            if cols > ref.shape[1]:
+                refs[-1][here, pl.ds(ref.shape[1], cols - ref.shape[1])] = jnp.zeros(
+                    (ref.shape[0], cols - ref.shape[1]), ref.dtype)
             at += ref.shape[0]
 
     return call(body, [((rows, cols), parts[0].dtype)], [VMEM] * len(parts))(*parts)[0]
 
 
-def base_product(tile, mine, theirs, cov, turn):
+def base_product(tile, mine, theirs, cov, turn, cols):
     own_rows, regions = cov.shape
-    cols = mine.shape[1]
+    wide = mine.shape[1]
     half = len(turn) // 2
 
     def body(tile_ref, a, b, cov_ref, out, grad):
@@ -468,10 +503,10 @@
             src = a if j < half else b
             at = pl.multiple_of((tile_ref[0] ^ flip) * own_rows, own_rows)
             grad[pl.ds(at, own_rows), :] = src[pl.ds(j % half * own_rows, own_rows), :]
-        out[...] = jnp.dot(cov_ref[...], grad[...], preferred_element_type=F32)
+        out[...] = jnp.dot(cov_ref[...], grad[...], preferred_element_type=F32)[:, :cols]
 
     return call(
-        body, [((own_rows, cols), F32)], [SMEM] + [VMEM] * 3, [pltpu.VMEM((regions, cols), cov.dtype)]
+        body, [((own_rows, cols), F32)], [SMEM] + [VMEM] * 3, [pltpu.VMEM((regions, wide), cov.dtype)]
     )(tile, mine, theirs, cov)[0]
 
 
@@ -486,7 +521,8 @@
     east_to, west_to = ring(lons)
 
     lon_bits, bits = lons.bit_length() - 1, devices.bit_length() - 1
-    order = list(range(1, lon_bits)) + list(range(lon_bits + 1, bits)) + [0, lon_bits]
+    far = list(range(lon_bits + 1, bits))
+    order = list(range(lon_bits - 1, 0, -1)) + far[:1] + [0] + far[1:] + [lon_bits]
     turn = [0]
     for bit in order:
         turn = turn + [j ^ (1 << bit) for j in turn]
@@ -496,7 +532,8 @@
 
     have = grad_in
     for i in range(len(order) - 1):
-        have = append([have, exchange(i, have)])
+        wide = pl.cdiv(have.shape[1], LANES) * LANES if i == len(order) - 2 else have.shape[1]
+        have = append([have, exchange(i, have)], wide)
     theirs = exchange(len(order) - 1, have)
 
     up, down = border_rows(adjoint, transport_rates)
@@ -521,7 +558,7 @@
     zonal, copies = regional(parts, s1, zc, trc, devices, cols * lons)
     sums = lax.all_to_all(copies, AXES, 0, 0, tiled=True)
     adjoint_out = filtered(lam, zonal, half, trc, lev).reshape(adjoint.shape)
-    base = base_product(tile, have, theirs, covariance, turn)
+    base = base_product(tile, have, theirs, covariance, turn, grad_in.shape[1])
     precond = finish(week_index, sums, inv, covariance, base, trc)
     return adjoint_out, precond
 

time: 86.8 us -> 77.8 us (0.90)
  Pallas kernels: 24.5 us -> 17.9 us
  local copies, waits for them, and re-layouts: 4.6 us -> 1.84 us
    pallas_call x15, Pallas kernels: 24.5 us -> 17.9 us  [apply(): return run(*(place(x, spec) for x, spec in zip(args, in_specs)))]
    ppermute x1 -> x0, local copies, waits for them, and re-layouts: 1.45 us -> none  [exchange(): return lax.ppermute(x, AXES, partners(devices, 1 << order[i]))]
    pallas_call x1 -> x0, local copies, waits for them, and re-layouts: 1.29 us -> none  [apply(): run(*(pltpu.with_memory_space_constraint(x, pltpu.VMEM) if spec is VMEM a...]
  transfers between devices with their start and end apart: 13 -> 13, of which waited for: 8 -> 9; matrix products, arithmetic and copies ran while one was open for 2% -> 0% of each run, Pallas kernels for 25% -> 20%
where the time goes in v2:
time: 77.8 us; the launch traced here: 77.5 us
  waiting for transfers between devices  32 us (41%)
  starting transfers between devices  24.3 us (31%)
  Pallas kernels  17.9 us (23%)
  local copies, waits for them, and re-layouts  1.84 us (2%)
  between operations  1.47 us (2%)
    ppermute x5, waiting for transfers between devices, exchange(): return lax.ppermute(x, AXES, partners(devices, 1 << order[i]))  21.1 us
    pallas_call x15, Pallas kernels, apply(): return run(*(place(x, spec) for x, spec in zip(args, in_specs)))  17.9 us
    ppermute x5, starting transfers between devices, exchange(): return lax.ppermute(x, AXES, partners(devices, 1 << order[i]))  8.5 us
    all_to_all x1, waiting for transfers between devices, shards(): sums = lax.all_to_all(copies, AXES, 0, 0, tiled=True)  4.49 us
    ppermute x3, starting transfers between devices, shards(): lax.ppermute(row_sums, 'lon', partners(lons, k))  4.39 us
    ppermute x1, starting transfers between devices, shards(): e_in = lax.ppermute(west, 'lon', west_to)  3.78 us
    ppermute x3, waiting for transfers between devices, shards(): lax.ppermute(row_sums, 'lon', partners(lons, k))  3.21 us
    all_to_all x1, starting transfers between devices, shards(): sums = lax.all_to_all(copies, AXES, 0, 0, tiled=True)  2.58 us
  transfers between devices with their start and end apart: 13, of which 9 were waited for; matrix products, arithmetic and copies ran while one was open for 0% of the time, Pallas kernels for 20%

profile of v2, /device:TPU:0, one launch (start us, length us, event | category | flops | bytes accessed | tf_op | source)
XLA Modules:
  0.0 77.5 jit_solution(18246115635978728228)
XLA Ops:
  0.6 4.1 %collective-permute-start.7 = (bf16[64,416]{1,0:T(8,128)(2,1)}, bf16[64,416]{1,0:T(8,128)(2,1)S(1)}, u32[]{:S(2)}, u32[]{:S(2)}) collective-permute-start(bf16[64,416]{1,0:T(8,128)(2,1)} %refs_0_.1), channel_id=1, source_target_pairs={{0,2},{1,3},{2,0},{3,1},{4,6},{5,7},{6,4},{7,5},{8,10},{9,11},{10,... | collective-permute-start | bytes 159752 | tf_op jit(solution)/shard_map/ppermute | solution.py:531
  4.8 3.9 %collective-permute-done.7.refs_1_ = bf16[64,416]{1,0:T(8,128)(2,1)S(1)} collective-permute-done((bf16[64,416]{1,0:T(8,128)(2,1)}, bf16[64,416]{1,0:T(8,128)(2,1)S(1)}, u32[]{:S(2)}, u32[]{:S(2)}) %collective-permute-start.7) | collective-permute-done | bytes 53280 | tf_op jit(solution)/shard_map/ppermute | solution.py:531
  8.6 0.8 %copy-done.5 = bf16[64,416]{1,0:T(8,128)(2,1)S(1)} copy-done((bf16[64,416]{1,0:T(8,128)(2,1)S(1)}, bf16[64,416]{1,0:T(8,128)(2,1)}, u32[]{:S(2)}) %copy-start.5) | copy-done | bytes 53272
  9.5 1.8 %collective-permute-start.8 = (bf16[128,416]{1,0:T(8,128)(2,1)S(1)}, bf16[128,416]{1,0:T(8,128)(2,1)S(1)}, u32[]{:S(2)}, u32[]{:S(2)}) collective-permute-start(bf16[128,416]{1,0:T(8,128)(2,1)S(1)} %shard_map.113.refs_0_), channel_id=1, source_target_pairs={{0,8},{1,9},{2,10},{3,11},{4,12},{5,13},{6,14},{7,15},{8,0},{9,1},... | collective-permute-start | bytes 319496 | tf_op jit(solution)/shard_map/ppermute | solution.py:531
  11.2 3.3 %collective-permute-done.8.refs_1_ = bf16[128,416]{1,0:T(8,128)(2,1)S(1)} collective-permute-done((bf16[128,416]{1,0:T(8,128)(2,1)S(1)}, bf16[128,416]{1,0:T(8,128)(2,1)S(1)}, u32[]{:S(2)}, u32[]{:S(2)}) %collective-permute-start.8) | collective-permute-done | bytes 106528 | tf_op jit(solution)/shard_map/ppermute | solution.py:531
  14.5 0.7 collective-permute-start.9
  15.3 5.7 %collective-permute-done.9.refs_1_ = bf16[256,416]{1,0:T(8,128)(2,1)S(1)} collective-permute-done((bf16[256,416]{1,0:T(8,128)(2,1)S(1)}, bf16[256,416]{1,0:T(8,128)(2,1)S(1)}, u32[]{:S(2)}, u32[]{:S(2)}) %collective-permute-start.9) | collective-permute-done | bytes 213024 | tf_op jit(solution)/shard_map/ppermute | solution.py:531
  21.0 0.0 copy-start
  21.0 0.0 copy-start.1
  21.0 1.8 %collective-permute-start.10 = (bf16[512,416]{1,0:T(8,128)(2,1)S(1)}, bf16[512,416]{1,0:T(8,128)(2,1)S(1)}, u32[]{:S(2)}, u32[]{:S(2)}) collective-permute-start(bf16[512,416]{1,0:T(8,128)(2,1)S(1)} %shard_map.115.refs_0_), channel_id=1, source_target_pairs={{0,16},{1,17},{2,18},{3,19},{4,20},{5,21},{6,22},{7,23},{8,24},{9,... | collective-permute-start | bytes 1277960 | tf_op jit(solution)/shard_map/ppermute | solution.py:531
  22.8 8.3 %collective-permute-done.10.refs_1_ = bf16[512,416]{1,0:T(8,128)(2,1)S(1)} collective-permute-done((bf16[512,416]{1,0:T(8,128)(2,1)S(1)}, bf16[512,416]{1,0:T(8,128)(2,1)S(1)}, u32[]{:S(2)}, u32[]{:S(2)}) %collective-permute-start.10) | collective-permute-done | bytes 426016 | tf_op jit(solution)/shard_map/ppermute | solution.py:531
  31.1 0.1 shard_map.116.a
  31.2 0.1 collective-permute-start.11
  31.3 1.2 %shard_map.105 = (f32[22,8,128]{2,1,0:T(8,128)S(1)}, f32[22,8,128]{2,1,0:T(8,128)S(1)}) custom-call(f32[64,32,128]{2,1,0:T(8,128)} %bitcast.6, f32[48,32,128]{2,1,0:T(8,128)} %bitcast.9), custom_call_target="tpu_custom_call" | custom-call | tf_op jit(solution)/shard_map/pallas_call | solution.py:58
  32.5 0.5 collective-permute-start
  33.1 2.2 %collective-permute-start.1 = (f32[22,8,128]{2,1,0:T(8,128)S(1)}, f32[22,8,128]{2,1,0:T(8,128)S(1)}, u32[]{:S(2)}, u32[]{:S(2)}) collective-permute-start(f32[22,8,128]{2,1,0:T(8,128)S(1)} %get-tuple-element.20.my_down), channel_id=1, source_target_pairs={{4,0},{8,4},{12,8},{16,12},{20,16},{24,20},{28,24},{0,28},{5,1},{9... | collective-permute-start | bytes 270344 | tf_op jit(solution)/shard_map/ppermute | solution.py:541
  35.2 0.0 copy-done
  35.2 1.5 %shard_map.104 = (f32[72,128]{1,0:T(8,128)S(1)}, f32[72,128]{1,0:T(8,128)S(1)}) custom-call(f32[64,32,128]{2,1,0:T(8,128)S(1)} %bitcast.7, f32[48,32,128]{2,1,0:T(8,128)S(1)} %bitcast.10), custom_call_target="tpu_custom_call" | custom-call | tf_op jit(solution)/shard_map/pallas_call | solution.py:58
  36.8 0.7 collective-permute-done.b
  37.4 0.0 collective-permute-done.1.a
  37.4 0.1 shard_map.106
  37.5 2.3 %collective-permute-start.2 = (f32[72,128]{1,0:T(8,128)S(1)}, f32[72,128]{1,0:T(8,128)S(1)}, u32[]{:S(2)}, u32[]{:S(2)}) collective-permute-start(f32[72,128]{1,0:T(8,128)S(1)} %get-tuple-element.21.my_east), channel_id=1, source_target_pairs={{0,1},{1,2},{2,3},{3,0},{4,5},{5,6},{6,7},{7,4},{8,9},{9,10},{10,1... | collective-permute-start | bytes 110600 | tf_op jit(solution)/shard_map/ppermute | solution.py:544
  39.8 3.8 %collective-permute-start.3 = (f32[72,128]{1,0:T(8,128)S(1)}, f32[72,128]{1,0:T(8,128)S(1)}, u32[]{:S(2)}, u32[]{:S(2)}) collective-permute-start(f32[72,128]{1,0:T(8,128)S(1)} %get-tuple-element.22.my_west), channel_id=1, source_target_pairs={{1,0},{2,1},{3,2},{0,3},{5,4},{6,5},{7,6},{4,7},{9,8},{10,9},{11,1... | collective-permute-start | bytes 110600 | tf_op jit(solution)/shard_map/ppermute | solution.py:545
  43.6 2.2 %collective-permute-done.2.w_in = f32[72,128]{1,0:T(8,128)S(1)} collective-permute-done((f32[72,128]{1,0:T(8,128)S(1)}, f32[72,128]{1,0:T(8,128)S(1)}, u32[]{:S(2)}, u32[]{:S(2)}) %collective-permute-start.2) | collective-permute-done | bytes 36896 | tf_op jit(solution)/shard_map/ppermute | solution.py:544
  45.8 0.4 collective-permute-done.3.e_in
  46.2 4.7 %shard_map.107 = (f32[64,32,128]{2,1,0:T(8,128)S(1)}, f32[256,128]{1,0:T(8,128)S(1)}, f32[32,128]{1,0:T(8,128)S(1)}) custom-call(s32[1]{0:T(128)} %bitcast.band_ref, f32[64,32,128]{2,1,0:T(8,128)S(1)} %bitcast.8, f32[48,32,128]{2,1,0:T(8,128)S(1)} %bitcast.11, f32[72,128]{1,0:T(8,128)S(1)} %collective-permute-done.2.w_in, ...), custom_call_target="tpu_custom_call" | custom-call | tf_op jit(solution)/shard_map/pallas_call | solution.py:58
  50.9 0.0 copy-start.2
  50.9 1.0 %copy-done.2 = f32[64,32,128]{2,1,0:T(8,128)} copy-done((f32[64,32,128]{2,1,0:T(8,128)}, f32[64,32,128]{2,1,0:T(8,128)S(1)}, u32[]{:S(2)}) %copy-start.2) | copy-done | bytes 1048600
  51.9 1.0 %collective-permute-start.4 = (f32[32,128]{1,0:T(8,128)S(1)}, f32[32,128]{1,0:T(8,128)S(1)}, u32[]{:S(2)}, u32[]{:S(2)}) collective-permute-start(f32[32,128]{1,0:T(8,128)S(1)} %get-tuple-element.24.refs_0_), channel_id=1, source_target_pairs={{0,1},{1,0},{2,3},{3,2},{4,5},{5,4},{6,7},{7,6},{8,9},{9,8},{10,11... | collective-permute-start | bytes 49160 | tf_op jit(solution)/shard_map/ppermute | solution.py:552
  52.9 3.0 %collective-permute-start.5 = (f32[32,128]{1,0:T(8,128)S(1)}, f32[32,128]{1,0:T(8,128)S(1)}, u32[]{:S(2)}, u32[]{:S(2)}) collective-permute-start(f32[32,128]{1,0:T(8,128)S(1)} %get-tuple-element.24.refs_0_), channel_id=1, source_target_pairs={{0,2},{1,3},{2,0},{3,1},{4,6},{5,7},{6,4},{7,5},{8,10},{9,11},{10,... | collective-permute-start | bytes 49160 | tf_op jit(solution)/shard_map/ppermute | solution.py:552
  55.9 0.4 collective-permute-start.6
  56.3 0.0 copy-done.7
  56.3 1.1 %shard_map.108 = (bf16[256,4096]{1,0:T(8,128)(2,1)S(1)}, f32[32,256]{1,0:T(8,128)S(1)}, f32[32,128]{1,0:T(8,128)S(1)}, f32[32,128]{1,0:T(8,128)S(1)}) custom-call(s32[32,128]{1,0:T(8,128)S(1)} %copy-done.7, f32[32,128]{1,0:T(8,128)S(1)} %copy-done.8, s32[1,32]{1,0:T(1,128)S(1)} %bitcast.12), custom_call_target="tpu_custom_call" | custom-call | tf_op jit(solution)/shard_map/pallas_call | solution.py:58
  57.4 0.8 %shard_map.109.refs_4_ = f32[8,256]{1,0:T(8,128)S(1)} custom-call(f32[256,128]{1,0:T(8,128)S(1)} %get-tuple-element.25.l0, f32[32,128]{1,0:T(8,128)S(1)} %get-tuple-element.26.w, bf16[256,4096]{1,0:T(8,128)(2,1)S(1)} %get-tuple-element.27.hot_ref), custom_call_target="tpu_custom_call" | custom-call | tf_op jit(solution)/shard_map/pallas_call | solution.py:58
  58.2 0.0 copy-start.4
  58.2 0.0 collective-permute-done.4.refs_1_
  58.2 0.0 collective-permute-done.5.refs_2_
  58.2 3.2 %collective-permute-done.6.refs_3_ = f32[32,128]{1,0:T(8,128)S(1)} collective-permute-done((f32[32,128]{1,0:T(8,128)S(1)}, f32[32,128]{1,0:T(8,128)S(1)}, u32[]{:S(2)}, u32[]{:S(2)}) %collective-permute-start.6) | collective-permute-done | bytes 16416 | tf_op jit(solution)/shard_map/ppermute | solution.py:552
  61.4 0.9 %shard_map.110 = (f32[32,128]{1,0:T(8,128)S(1)}, f32[32,8,256]{2,1,0:T(8,128)}) custom-call(f32[32,128]{1,0:T(8,128)S(1)} %get-tuple-element.24.refs_0_, f32[32,128]{1,0:T(8,128)S(1)} %collective-permute-done.4.refs_1_, f32[32,128]{1,0:T(8,128)S(1)} %collective-permute-done.5.refs_2_, f32[32,128]{1,0:T(8,128)S(1)} %collective-permute-done.6.refs_3_, ...), custom_call_target="tpu_custom_call" | custom-call | tf_op jit(solution)/shard_map/pallas_call | solution.py:58
  62.3 2.6 %all-to-all-start = ((f32[32,8,256]{2,1,0:T(8,128)}), f32[32,8,256]{2,1,0:T(8,128)S(1)}, u32[]{:S(2)}, u32[]{:S(2)}) async-start(f32[32,8,256]{2,1,0:T(8,128)} %get-tuple-element.31), calls=%async_computation | async-start | bytes 524288 | tf_op jit(solution)/shard_map/all_to_all | solution.py:559
  64.9 0.0 copy-done.6
  64.9 1.7 %shard_map.112.inv_ref = s32[16,32,128]{2,1,0:T(8,128)S(1)} custom-call(s32[32,256]{1,0:T(8,128)S(1)} %copy-done.6), custom_call_target="tpu_custom_call" | custom-call | tf_op jit(solution)/shard_map/pallas_call | solution.py:58
  67.3 0.0 copy-done.3
  67.3 1.5 %shard_map.111 = f32[64,32,128]{2,1,0:T(8,128)} custom-call(f32[64,32,128]{2,1,0:T(8,128)S(1)} %copy-done.3, f32[32,128]{1,0:T(8,128)S(1)} %get-tuple-element.29.z_ref, f32[32,128]{1,0:T(8,128)S(1)} %get-tuple-element.30.h_ref), custom_call_target="tpu_custom_call" | custom-call | tf_op jit(solution)/shard_map/pallas_call | solution.py:58
  68.8 0.0 collective-permute-done.11.b
  68.8 1.8 %shard_map.117.base_ref = f32[64,416]{1,0:T(8,128)S(1)} custom-call(s32[1]{0:T(128)S(6)} %add.7.tile_ref, bf16[1024,512]{1,0:T(8,128)(2,1)S(1)} %shard_map.116.a, bf16[1024,512]{1,0:T(8,128)(2,1)} %collective-permute-done.11.b, bf16[64,2048]{1,0:T(8,128)(2,1)S(1)} %copy-done.4), custom_call_target="tpu_custom_call" | custom-call | tf_op jit(solution)/shard_map/pallas_call | solution.py:58
  70.7 4.5 %all-to-all-done.s_ref = f32[32,8,256]{2,1,0:T(8,128)S(1)} async-done(((f32[32,8,256]{2,1,0:T(8,128)}), f32[32,8,256]{2,1,0:T(8,128)S(1)}, u32[]{:S(2)}, u32[]{:S(2)}) %all-to-all-start) | async-done | bytes 262176 | tf_op jit(solution)/shard_map/all_to_all | solution.py:559
  75.2 2.4 %shard_map.118 = f32[64,416]{1,0:T(8,128)} custom-call(s32[1]{0:T(128)S(6)} %copy.11.week_ref, f32[32,8,256]{2,1,0:T(8,128)S(1)} %all-to-all-done.s_ref, s32[16,32,128]{2,1,0:T(8,128)S(1)} %shard_map.112.inv_ref, bf16[64,2048]{1,0:T(8,128)(2,1)S(1)} %copy-done.4, f32[64,416]{1,0:T(8,128)S(1)} %shard_map.117.base_ref), custom_call_target="tpu_custom_call" | custom-call | tf_op jit(solution)/shard_map/pallas_call | solution.py:58
  (13 shorter events, 0.1 us)
Async XLA Ops:
  0.6 8.0 %collective-permute-start.7 = (bf16[64,416]{1,0:T(8,128)(2,1)}, bf16[64,416]{1,0:T(8,128)(2,1)S(1)}, u32[]{:S(2)}, u32[]{:S(2)}) collective-permute-start(bf16[64,416]{1,0:T(8,128)(2,1)} %refs_0_.1), channel_id=1, source_target_pairs={{0,2},{1,3},{2,0},{3,1},{4,6},{5,7},{6,4},{7,5},{8,10},{9,11},{10,... | collective-permute-start | bytes 159752 | tf_op jit(solution)/shard_map/ppermute | solution.py:531
  8.6 0.8 %copy-start.5 = (bf16[64,416]{1,0:T(8,128)(2,1)S(1)}, bf16[64,416]{1,0:T(8,128)(2,1)}, u32[]{:S(2)}) copy-start(bf16[64,416]{1,0:T(8,128)(2,1)} %refs_0_.1) | copy-start | bytes 159748
  9.5 5.0 %collective-permute-start.8 = (bf16[128,416]{1,0:T(8,128)(2,1)S(1)}, bf16[128,416]{1,0:T(8,128)(2,1)S(1)}, u32[]{:S(2)}, u32[]{:S(2)}) collective-permute-start(bf16[128,416]{1,0:T(8,128)(2,1)S(1)} %shard_map.113.refs_0_), channel_id=1, source_target_pairs={{0,8},{1,9},{2,10},{3,11},{4,12},{5,13},{6,14},{7,15},{8,0},{9,1},... | collective-permute-start | bytes 319496 | tf_op jit(solution)/shard_map/ppermute | solution.py:531
  14.5 6.4 %collective-permute-start.9 = (bf16[256,416]{1,0:T(8,128)(2,1)S(1)}, bf16[256,416]{1,0:T(8,128)(2,1)S(1)}, u32[]{:S(2)}, u32[]{:S(2)}) collective-permute-start(bf16[256,416]{1,0:T(8,128)(2,1)S(1)} %shard_map.114.refs_0_), channel_id=1, source_target_pairs={{0,1},{1,0},{2,3},{3,2},{4,5},{5,4},{6,7},{7,6},{8,9},{9,8},{10,11... | collective-permute-start | bytes 638984 | tf_op jit(solution)/shard_map/ppermute | solution.py:531
  21.0 14.2 %copy-start = (f32[8,8,32,128]{3,2,1,0:T(8,128)S(1)}, f32[8,8,32,128]{3,2,1,0:T(8,128)}, u32[]{:S(2)}) copy-start(f32[8,8,32,128]{3,2,1,0:T(8,128)} %param.9) | copy-start | bytes 3145732
  21.0 14.2 %copy-start.1 = (f32[6,8,32,128]{3,2,1,0:T(8,128)S(1)}, f32[6,8,32,128]{3,2,1,0:T(8,128)}, u32[]{:S(2)}) copy-start(f32[6,8,32,128]{3,2,1,0:T(8,128)} %param.10) | copy-start | bytes 2359300
  21.0 10.1 %collective-permute-start.10 = (bf16[512,416]{1,0:T(8,128)(2,1)S(1)}, bf16[512,416]{1,0:T(8,128)(2,1)S(1)}, u32[]{:S(2)}, u32[]{:S(2)}) collective-permute-start(bf16[512,416]{1,0:T(8,128)(2,1)S(1)} %shard_map.115.refs_0_), channel_id=1, source_target_pairs={{0,16},{1,17},{2,18},{3,19},{4,20},{5,21},{6,22},{7,23},{8,24},{9,... | collective-permute-start | bytes 1277960 | tf_op jit(solution)/shard_map/ppermute | solution.py:531
  31.2 37.6 %collective-permute-start.11 = (bf16[1024,512]{1,0:T(8,128)(2,1)S(1)}, bf16[1024,512]{1,0:T(8,128)(2,1)}, u32[]{:S(2)}, u32[]{:S(2)}) collective-permute-start(bf16[1024,512]{1,0:T(8,128)(2,1)S(1)} %shard_map.116.a), channel_id=1, source_target_pairs={{0,4},{1,5},{2,6},{3,7},{4,0},{5,1},{6,2},{7,3},{8,12},{9,13},{10,... | collective-permute-start | bytes 3145736 | tf_op jit(solution)/shard_map/ppermute | solution.py:531
  32.5 4.9 %collective-permute-start = (f32[22,8,128]{2,1,0:T(8,128)S(1)}, f32[22,8,128]{2,1,0:T(8,128)S(1)}, u32[]{:S(2)}, u32[]{:S(2)}) collective-permute-start(f32[22,8,128]{2,1,0:T(8,128)S(1)} %get-tuple-element.19.my_up), channel_id=1, source_target_pairs={{0,4},{4,8},{8,12},{12,16},{16,20},{20,24},{24,28},{28,0},{1,5},{5... | collective-permute-start | bytes 270344 | tf_op jit(solution)/shard_map/ppermute | solution.py:540
  33.0 23.2 %copy-start.7 = (s32[32,128]{1,0:T(8,128)S(1)}, s32[32,128]{1,0:T(8,128)}, u32[]{:S(2)}) copy-start(s32[32,128]{1,0:T(8,128)} %rl.1) | copy-start | bytes 49156
  33.0 23.2 %copy-start.8 = (f32[32,128]{1,0:T(8,128)S(1)}, f32[32,128]{1,0:T(8,128)}, u32[]{:S(2)}) copy-start(f32[32,128]{1,0:T(8,128)} %w_ref.1) | copy-start | bytes 49156
  33.0 23.2 %copy-start.9 = (s32[32]{0:T(128)S(1)}, s32[32]{0:T(128)}, u32[]{:S(2)}) copy-start(s32[32]{0:T(128)} %param.14) | copy-start | bytes 388
  33.1 4.4 %collective-permute-start.1 = (f32[22,8,128]{2,1,0:T(8,128)S(1)}, f32[22,8,128]{2,1,0:T(8,128)S(1)}, u32[]{:S(2)}, u32[]{:S(2)}) collective-permute-start(f32[22,8,128]{2,1,0:T(8,128)S(1)} %get-tuple-element.20.my_down), channel_id=1, source_target_pairs={{4,0},{8,4},{12,8},{16,12},{20,16},{24,20},{28,24},{0,28},{5,1},{9... | collective-permute-start | bytes 270344 | tf_op jit(solution)/shard_map/ppermute | solution.py:541
  37.5 8.3 %collective-permute-start.2 = (f32[72,128]{1,0:T(8,128)S(1)}, f32[72,128]{1,0:T(8,128)S(1)}, u32[]{:S(2)}, u32[]{:S(2)}) collective-permute-start(f32[72,128]{1,0:T(8,128)S(1)} %get-tuple-element.21.my_east), channel_id=1, source_target_pairs={{0,1},{1,2},{2,3},{3,0},{4,5},{5,6},{6,7},{7,4},{8,9},{9,10},{10,1... | collective-permute-start | bytes 110600 | tf_op jit(solution)/shard_map/ppermute | solution.py:544
  39.8 25.1 %copy-start.6 = (s32[32,256]{1,0:T(8,128)S(1)}, s32[32,256]{1,0:T(8,128)}, u32[]{:S(2)}) copy-start(s32[32,256]{1,0:T(8,128)} %tr.1) | copy-start | bytes 98308
  39.8 6.4 %collective-permute-start.3 = (f32[72,128]{1,0:T(8,128)S(1)}, f32[72,128]{1,0:T(8,128)S(1)}, u32[]{:S(2)}, u32[]{:S(2)}) collective-permute-start(f32[72,128]{1,0:T(8,128)S(1)} %get-tuple-element.22.my_west), channel_id=1, source_target_pairs={{1,0},{2,1},{3,2},{0,3},{5,4},{6,5},{7,6},{4,7},{9,8},{10,9},{11,1... | collective-permute-start | bytes 110600 | tf_op jit(solution)/shard_map/ppermute | solution.py:545
  50.9 1.0 %copy-start.2 = (f32[64,32,128]{2,1,0:T(8,128)}, f32[64,32,128]{2,1,0:T(8,128)S(1)}, u32[]{:S(2)}) copy-start(f32[64,32,128]{2,1,0:T(8,128)S(1)} %get-tuple-element.23.l_ref) | copy-start | bytes 3145732
  51.9 15.5 %copy-start.3 = (f32[64,32,128]{2,1,0:T(8,128)S(1)}, f32[64,32,128]{2,1,0:T(8,128)}, u32[]{:S(2)}) copy-start(f32[64,32,128]{2,1,0:T(8,128)} %copy-done.2) | copy-start | bytes 3145732
  51.9 6.3 %collective-permute-start.4 = (f32[32,128]{1,0:T(8,128)S(1)}, f32[32,128]{1,0:T(8,128)S(1)}, u32[]{:S(2)}, u32[]{:S(2)}) collective-permute-start(f32[32,128]{1,0:T(8,128)S(1)} %get-tuple-element.24.refs_0_), channel_id=1, source_target_pairs={{0,1},{1,0},{2,3},{3,2},{4,5},{5,4},{6,7},{7,6},{8,9},{9,8},{10,11... | collective-permute-start | bytes 49160 | tf_op jit(solution)/shard_map/ppermute | solution.py:552
  52.9 5.3 %collective-permute-start.5 = (f32[32,128]{1,0:T(8,128)S(1)}, f32[32,128]{1,0:T(8,128)S(1)}, u32[]{:S(2)}, u32[]{:S(2)}) collective-permute-start(f32[32,128]{1,0:T(8,128)S(1)} %get-tuple-element.24.refs_0_), channel_id=1, source_target_pairs={{0,2},{1,3},{2,0},{3,1},{4,6},{5,7},{6,4},{7,5},{8,10},{9,11},{10,... | collective-permute-start | bytes 49160 | tf_op jit(solution)/shard_map/ppermute | solution.py:552
  55.9 5.5 %collective-permute-start.6 = (f32[32,128]{1,0:T(8,128)S(1)}, f32[32,128]{1,0:T(8,128)S(1)}, u32[]{:S(2)}, u32[]{:S(2)}) collective-permute-start(f32[32,128]{1,0:T(8,128)S(1)} %get-tuple-element.24.refs_0_), channel_id=1, source_target_pairs={{0,3},{1,2},{2,1},{3,0},{4,7},{5,6},{6,5},{7,4},{8,11},{9,10},{10,... | collective-permute-start | bytes 49160 | tf_op jit(solution)/shard_map/ppermute | solution.py:552
  58.2 10.6 %copy-start.4 = (bf16[64,2048]{1,0:T(8,128)(2,1)S(1)}, bf16[64,2048]{1,0:T(8,128)(2,1)}, u32[]{:S(2)}) copy-start(bf16[64,2048]{1,0:T(8,128)(2,1)} %cov_ref.3) | copy-start | bytes 786436
  62.3 12.8 %all-to-all-start = ((f32[32,8,256]{2,1,0:T(8,128)}), f32[32,8,256]{2,1,0:T(8,128)S(1)}, u32[]{:S(2)}, u32[]{:S(2)}) async-start(f32[32,8,256]{2,1,0:T(8,128)} %get-tuple-element.31), calls=%async_computation | async-start | bytes 524288 | tf_op jit(solution)/shard_map/all_to_all | solution.py:559

commit v3 on v2

--- a/solution.py
+++ b/solution.py
@@ -145,16 +145,16 @@
     return south, north
 
 
-def corners(east, west, before, after, band, bands):
+def corners(east, west, before, after, bands):
     rows = (east.shape[0] - 8) // 2
     lev = before.shape[1]
     trc = (before.shape[0] - 6) // 2
 
-    def body(band_ref, east_in, west_in, b, a, e_ref, w_ref):
+    def body(east_in, west_in, b, a, e_ref, w_ref):
         lane, sub = iota((lev, LANES), 1), iota((lev, LANES), 0)
         e_ref[...] = east_in[...]
         w_ref[...] = west_in[...]
-        for which, (ref, mask) in enumerate(zip((b, a), masks(band_ref[0], bands))):
+        for which, (ref, mask) in enumerate(zip((b, a), masks(lax.axis_index("lat"), bands))):
             to_e = jnp.zeros((lev, LANES), F32)
             to_w = jnp.zeros((lev, LANES), F32)
             for k in range(trc):
@@ -165,11 +165,11 @@
             e_ref[pl.ds(2 * rows + which, 1), :] = jnp.sum(to_e, axis=0, keepdims=True)
             w_ref[pl.ds(2 * rows + which, 1), :] = jnp.sum(to_w, axis=0, keepdims=True)
 
-    return call(body, [(x.shape, F32) for x in (east, west)], [SMEM] + [VMEM] * 4)(
-        band, east, west, before, after)
-
-
-def transport_kernel(trc, lev, rows, bands, band_ref, field, tv, w_in, e_in, my_east, my_west, b, a, my_up, my_down,
+    return call(body, [(x.shape, F32) for x in (east, west)], [VMEM] * 4)(
+        east, west, before, after)
+
+
+def transport_kernel(trc, lev, rows, bands, field, tv, w_in, e_in, my_east, my_west, b, a, my_up, my_down,
                      lam, level0, row_sums, f1, cols, ghost0, ghost1, mids, halves):
     high = rows + 2 * OFF
     lane = iota((8, LANES), 1)
@@ -177,7 +177,7 @@
     lane_l = iota((lev, LANES), 1)
     bf, af = (x.reshape((2 * trc + 6) * lev, LANES) for x in (b, a))
     f1_flat = f1.reshape(trc * lev * high, LANES)
-    south_mask, north_mask = masks(band_ref[0], bands)
+    south_mask, north_mask = masks(lax.axis_index("lat"), bands)
     edge = iota((8, LANES), 0)
 
     def centre(rate):
@@ -240,7 +240,6 @@
             if l == 0:
                 rate[5] = jnp.zeros_like(rate[5])
             mids[l, pl.ds(r, 8), :] = centre(rate)
-    row_sums[...] = jnp.zeros(row_sums.shape, F32)
 
     def step(load, ghost, emit, after):
         def tracer(k, carry):
@@ -283,43 +282,51 @@
         if l == 0:
             level0[pl.ds(r * trc + k, 8, stride=trc), :] = v
 
-    def sums(k):
+    def halve(k):
         for l in range(lev):
             for r in range(0, rows, 16):
                 v = lam[k * lev + l, pl.ds(r, 16), :]
                 hi = v.astype(BF16)
-                halves[pl.ds(l * rows + r, 16), pl.ds(0, LANES)] = hi
-                halves[pl.ds(l * rows + r, 16), pl.ds(LANES, LANES)] = (v - hi.astype(F32)).astype(BF16)
-        total = jnp.dot(halves[...], jnp.ones((2 * LANES, LANES), BF16), preferred_element_type=F32)
-        for r in range(0, rows, 8):
-            old = row_sums[pl.ds(r, 8), :]
-            for l in range(lev):
-                old = jnp.where(lane == l * trc + k, total[l * rows + r : l * rows + r + 8], old)
-            row_sums[pl.ds(r, 8), :] = old
+                halves[k, pl.ds(l * rows + r, 16), pl.ds(0, LANES)] = hi
+                halves[k, pl.ds(l * rows + r, 16), pl.ds(LANES, LANES)] = (v - hi.astype(F32)).astype(BF16)
 
     step(load0, ghost0, emit1, lambda k: None)
-    step(load1, ghost1, emit2, sums)
-
-
-def transport(band, bands, field, rates, w_in, e_in, east, west, before, after, up, down, trc, lev, rows):
+    step(load1, ghost1, emit2, halve)
+    total = [jnp.zeros((8, LANES), F32) for _ in range(0, rows, 8)]
+    ones = jnp.ones((2 * LANES, LANES), BF16)
+    for k in range(trc):
+        sums = jnp.dot(halves[k], ones, preferred_element_type=F32)
+        for l in range(lev):
+            for i in range(rows // 8):
+                at = l * rows + 8 * i
+                total[i] = jnp.where(lane == l * trc + k, sums[at : at + 8], total[i])
+    for i in range(rows // 8):
+        row_sums[pl.ds(8 * i, 8), :] = total[i]
+
+
+def transport(bands, field, rates, w_in, e_in, east, west, before, after, up, down, trc, lev, rows):
     high = rows + 2 * OFF
     return call(
         functools.partial(transport_kernel, trc, lev, rows, bands),
         [((trc * lev, rows, LANES), F32), ((rows * trc, LANES), F32), ((rows, LANES), F32)],
-        [SMEM] + [VMEM] * 10,
+        [VMEM] * 10,
         [
             pltpu.VMEM((trc * lev, high, LANES), F32),
             pltpu.VMEM((2, high, LANES), F32),
             pltpu.VMEM((rows, LANES), F32),
             pltpu.VMEM((rows, LANES), F32),
             pltpu.VMEM((lev, rows, LANES), F32),
-            pltpu.VMEM((lev * rows, 2 * LANES), BF16),
+            pltpu.VMEM((trc, lev * rows, 2 * LANES), BF16),
         ],
-    )(band, field.reshape(trc * lev, rows, LANES), rates.reshape(6 * lev, rows, LANES),
+    )(field.reshape(trc * lev, rows, LANES), rates.reshape(6 * lev, rows, LANES),
       w_in, e_in, east, west, before, after, up, down)
 
 
-def tables(region_local, cell_weight, polar_rows, local):
+def numbered(row, each, blocks):
+    return (row & (blocks - 1)) * each + (row >> (blocks.bit_length() - 1))
+
+
+def tables(region_local, cell_weight, polar_rows, local, blocks):
     rows, cols = region_local.shape
 
     def body(rl, w_ref, p_ref, hot, zc, half, w1, wz):
@@ -332,18 +339,23 @@
         w1[...] = w * (1.0 - hp)
         w1z = w * hp
         row_id = iota((rows, cols), 0)
-        entry = iota((local, cols), 0)
+        entry = numbered(iota((local, cols), 0), local // blocks, blocks)
         for r in range(rows):
             hot[:, pl.ds(r * cols, cols)] = (rl[pl.ds(r, 1), :] == entry).astype(F32).astype(BF16)
             parts = split3(jnp.where(row_id == r, w1z, 0.0))
             for i in range(3):
                 wz[pl.ds(i * rows, rows), pl.ds(r * cols, cols)] = parts[i].astype(BF16)
         z = lax.dot_general(wz[...], hot[...], (((1,), (1,)), ((), ())), preferred_element_type=F32)
-        zc[...] = z[:rows] + z[rows : 2 * rows] + z[2 * rows :]
+        z = z[:rows] + z[rows : 2 * rows] + z[2 * rows :]
+        hi, mid, lo = split3(jnp.concatenate([z, jnp.zeros((LANES - rows, local), F32)], axis=0))
+        for i, piece in enumerate((hi, mid, lo)):
+            turned = jnp.transpose(piece)[:, :rows].astype(BF16)
+            for at in ((0, 3, 5), (1, 4), (2,))[i]:
+                zc[:, pl.ds(at * rows, rows)] = turned
 
     return call(
         body,
-        [((local, rows * cols), BF16), ((rows, local), F32), ((rows, cols), F32), ((rows, cols), F32)],
+        [((local, rows * cols), BF16), ((local, 6 * rows), BF16), ((rows, cols), F32), ((rows, cols), F32)],
         [VMEM] * 3,
         [pltpu.VMEM((3 * rows, rows * cols), BF16)],
     )(region_local, cell_weight, polar_rows.reshape(1, rows))
@@ -352,28 +364,30 @@
 def places(tile_regions, own_rows):
     count, local = tile_regions.shape
     regions = own_rows * count
-    per = local // count
-    owners = LANES // own_rows
-
-    def body(tr, inv):
-        lane = iota((8, LANES), 1)
-
-        def block(i, carry):
-            t = pl.multiple_of(i * 8, 8)
-            for q in range(regions // LANES):
-                first = q * owners * per
-                src = tr[pl.ds(t, 8), pl.ds(first // LANES * LANES, LANES)]
-                start = first % LANES + lane // own_rows * per
-                found = jnp.full((8, LANES), -1, jnp.int32)
-                for e in range(per):
-                    got = jnp.take_along_axis(src, start + e, axis=1)
-                    found = jnp.where(got == q * LANES + lane, start + e, found)
-                inv[q, pl.ds(t, 8), :] = found
+    blocks = regions // LANES
+    each = local // blocks
+    width = count * each
+    group = LANES // each
+
+    def body(tr, out):
+        lane, sub = iota((group, LANES), 1), iota((group, LANES), 0)
+        region = iota((LANES, LANES), 0)
+
+        def block(q, carry):
+            first = q * each
+            src_at = pl.multiple_of(first // LANES * LANES, LANES)
+            from_lane = first % LANES + lane % each
+            for g in range(width // LANES):
+                src = tr[pl.ds(g * group, group), pl.ds(src_at, LANES)]
+                got = jnp.take_along_axis(src, from_lane, axis=1)
+                row = jnp.sum(jnp.where(lane // each == sub, got, 0), axis=0, keepdims=True)
+                out[pl.ds(pl.multiple_of(q * LANES, LANES), LANES), pl.ds(g * LANES, LANES)] = (
+                    (row == q * LANES + region).astype(F32).astype(BF16))
             return carry
 
-        lax.fori_loop(0, count // 8, block, 0)
-
-    return call(body, [((regions // LANES, count, LANES), jnp.int32)], [VMEM])(tile_regions)[0]
+        lax.fori_loop(0, blocks, block, 0)
+
+    return call(body, [((regions, width), BF16)], [VMEM])(tile_regions)[0]
 
 
 def local_sums(level0, w1, hot):
@@ -389,29 +403,41 @@
             lhs[pl.ds(0, 2 * trc), at] = jnp.concatenate([hi, mid], axis=0).astype(BF16)
             lhs[pl.ds(2 * trc, 2 * trc), at] = jnp.concatenate([lo, jnp.zeros_like(lo)], axis=0).astype(BF16)
         s = lax.dot_general(lhs[...], hot_ref[...], (((1,), (1,)), ((), ())), preferred_element_type=F32)
-        out[...] = s[:trc] + s[trc : 2 * trc] + s[2 * trc : 3 * trc]
-
-    return call(body, [((trc, local), F32)], [VMEM] * 3, [pltpu.VMEM((4 * trc, rows * cols), BF16)])(level0, w1, hot)[0]
-
-
-def regional(parts, s1, zc, trc, devices, columns):
+        s = s[:trc] + s[trc : 2 * trc] + s[2 * trc : 3 * trc]
+        out[...] = jnp.transpose(jnp.concatenate([s, jnp.zeros((LANES - trc, local), F32)], axis=0))
+
+    return call(
+        body, [((local, LANES), F32)], [VMEM] * 3, [pltpu.VMEM((4 * trc, rows * cols), BF16)]
+    )(level0, w1, hot)[0]
+
+
+def regional(parts, s1, zc, trc, devices, columns, blocks):
     rows, _ = parts[0].shape
-    local = s1.shape[1]
+    local = s1.shape[0]
+    each, width = local // blocks, blocks * trc
 
     def body(*refs):
-        ins, (s_ref, zc_ref, zonal, out) = refs[: len(parts)], refs[len(parts) :]
+        ins, (s_ref, zc_ref, zonal, out, mixed) = refs[: len(parts)], refs[len(parts) :]
         z = ins[0][...]
         for ref in ins[1:]:
             z = z + ref[...]
         z = z / columns
         zonal[...] = z
-        s = s_ref[...] + lax.dot_general(
-            z[:, :trc], zc_ref[...], (((0,), (0,)), ((), ())), precision=lax.Precision.HIGHEST,
-            preferred_element_type=F32)
-        for d in range(devices):
-            out[d] = s
-
-    return call(body, [((rows, LANES), F32), ((devices, trc, local), F32)], [VMEM] * (len(parts) + 2))(*parts, s1, zc)
+        hi, mid, lo = split3(z)
+        pieces = jnp.concatenate([x.astype(BF16) for x in (hi, hi, hi, mid, mid, lo)], axis=0)
+        more = jnp.dot(zc_ref[...], pieces, preferred_element_type=F32)
+        mixed[...] = s_ref[...] + jnp.where(iota((local, LANES), 1) < trc, more, 0.0)
+        for c in range(0, width, LANES):
+            total = jnp.zeros((each, LANES), F32)
+            for q in range(c // trc, (c + LANES) // trc):
+                total = total + pltpu.roll(mixed[pl.ds(q, each, stride=blocks), :], q * trc % LANES, 1)
+            for d in range(devices):
+                out[d, :, pl.ds(c, LANES)] = total
+
+    return call(
+        body, [((rows, LANES), F32), ((devices, each, width), F32)], [VMEM] * (len(parts) + 2),
+        [pltpu.VMEM((local, LANES), F32)]
+    )(*parts, s1, zc)
 
 
 def filtered(lam, zonal, half, trc, lev):
@@ -428,44 +454,37 @@
     return call(body, [(lam.shape, F32)], [VMEM] * 3, keep=False)(lam, zonal, half)[0]
 
 
-def finish(week, sums, inv, cov, base, trc):
-    count, _, local = sums.shape
-    own_rows, regions = cov.shape
+def finish(week, sums, hot, cov, base, trc):
+    own_rows, _ = cov.shape
     cols = base.shape[1]
-    per = local // count
-    owners = LANES // own_rows
-
-    def body(week_ref, s_ref, inv_ref, cov_ref, base_ref, out, fresh):
-        def block(q, carry):
-            src_at = q * owners * per // LANES * LANES
-            src_at = src_at if isinstance(q, int) else pl.multiple_of(src_at, LANES)
-            total = [jnp.zeros((trc, LANES), F32) for _ in range(4)]
-            for t in range(count):
-                idx = inv_ref[q, pl.ds(t, trc, stride=0), :]
-                got = jnp.take_along_axis(s_ref[t, :, pl.ds(src_at, LANES)], jnp.maximum(idx, 0), axis=1)
-                total[t % 4] = total[t % 4] + jnp.where(idx >= 0, got, 0.0)
-            fresh[q] = total[0] + total[1] + (total[2] + total[3])
-            return carry
-
-        blocks = regions // LANES
-        if blocks <= 16:
-            for q in range(blocks):
-                block(q, 0)
-        else:
-            lax.fori_loop(0, blocks, block, 0)
-        fresh_rows = jnp.concatenate([fresh[q] for q in range(blocks)], axis=1)
-        wide = jnp.concatenate([fresh_rows, jnp.zeros((LANES - trc, regions), F32)], axis=0).astype(BF16)
-        added = lax.dot_general(cov_ref[...], wide, (((1,), (1,)), ((), ())), preferred_element_type=F32)
-        start = week_ref[0] * trc
-        added = pltpu.roll(added, start % LANES, 1)
+    width = sums.shape[1]
+    span = LANES // trc * LANES
+
+    def body(week_ref, s_ref, hot_ref, cov_ref, base_ref, out):
+        added = jnp.zeros((own_rows, LANES), F32)
+        for c in range(0, width, LANES):
+            parts = [x.astype(BF16) for x in split3(jnp.transpose(s_ref[:, pl.ds(c, LANES)]))]
+            fresh = []
+            for q in range(0, LANES // trc, 2):
+                rows = slice(q * trc, (q + 2) * trc)
+                both = lax.dot_general(
+                    jnp.concatenate([x[rows] for x in parts], axis=0),
+                    hot_ref[pl.ds((c // trc + q) * LANES, 2 * LANES), :],
+                    (((1,), (1,)), ((), ())), preferred_element_type=F32)
+                both = both[: 2 * trc] + both[2 * trc : 4 * trc] + both[4 * trc :]
+                fresh += [both[:trc, :LANES], both[trc:, LANES:]]
+            fresh = jnp.concatenate(fresh, axis=1)
+            fresh = jnp.concatenate([fresh] * (LANES // trc), axis=0).astype(BF16)
+            added = added + lax.dot_general(
+                cov_ref[:, pl.ds(c // trc * LANES, span)], fresh, (((1,), (1,)), ((), ())),
+                preferred_element_type=F32)
         for c in range(0, cols, LANES):
-            width = min(LANES, cols - c)
-            here = jnp.where(start // LANES == c // LANES, added[:, :width], 0.0)
-            out[:, pl.ds(c, width)] = base_ref[:, pl.ds(c, width)] + here
-
-    return call(
-        body, [((own_rows, cols), F32)], [SMEM] + [VMEM] * 4, [pltpu.VMEM((regions // LANES, trc, LANES), F32)], keep=False
-    )(week, sums, inv, cov, base)[0]
+            w = min(LANES, cols - c)
+            here = (c + iota((own_rows, LANES), 1)) // trc == week_ref[0]
+            out[:, pl.ds(c, w)] = base_ref[:, pl.ds(c, w)] + jnp.where(here, added, 0.0)[:, :w]
+
+    return call(body, [((own_rows, cols), F32)], [SMEM] + [VMEM] * 4, keep=False)(
+        week, sums, hot, cov, base)[0]
 
 
 def ring(size):
@@ -493,30 +512,29 @@
     return call(body, [((rows, cols), parts[0].dtype)], [VMEM] * len(parts))(*parts)[0]
 
 
-def base_product(tile, mine, theirs, cov, turn, cols):
+def base_product(mine, theirs, cov, turn, cols):
     own_rows, regions = cov.shape
     wide = mine.shape[1]
     half = len(turn) // 2
 
-    def body(tile_ref, a, b, cov_ref, out, grad):
+    def body(a, b, cov_ref, out, grad):
+        tile = lax.axis_index("lat") * lax.axis_size("lon") + lax.axis_index("lon")
         for j, flip in enumerate(turn):
             src = a if j < half else b
-            at = pl.multiple_of((tile_ref[0] ^ flip) * own_rows, own_rows)
+            at = pl.multiple_of((tile ^ flip) * own_rows, own_rows)
             grad[pl.ds(at, own_rows), :] = src[pl.ds(j % half * own_rows, own_rows), :]
         out[...] = jnp.dot(cov_ref[...], grad[...], preferred_element_type=F32)[:, :cols]
 
     return call(
-        body, [((own_rows, cols), F32)], [SMEM] + [VMEM] * 3, [pltpu.VMEM((regions, wide), cov.dtype)]
-    )(tile, mine, theirs, cov)[0]
+        body, [((own_rows, cols), F32)], [VMEM] * 3, [pltpu.VMEM((regions, wide), cov.dtype)]
+    )(mine, theirs, cov)[0]
 
 
 def shards(adjoint, transport_rates, cell_weight, region_local, tile_regions, polar_rows, week_index, grad_in, covariance):
     trc, lev, rows, cols = adjoint.shape
-    own_rows, _ = covariance.shape
+    own_rows, regions = covariance.shape
     lats, lons = lax.axis_size("lat"), lax.axis_size("lon")
     devices = lats * lons
-    band = lax.axis_index("lat").astype(jnp.int32).reshape(1)
-    tile = band * lons + lax.axis_index("lon").astype(jnp.int32)
     north_to, south_to = ring(lats)
     east_to, west_to = ring(lons)
 
@@ -540,13 +558,14 @@
     before = lax.ppermute(up, "lat", north_to)
     after = lax.ppermute(down, "lat", south_to)
     east, west = border_cols(adjoint, transport_rates)
-    east, west = corners(east, west, before, after, band, lats)
+    east, west = corners(east, west, before, after, lats)
     w_in = lax.ppermute(east, "lon", east_to)
     e_in = lax.ppermute(west, "lon", west_to)
-    hot, zc, half, w1 = tables(region_local, cell_weight, polar_rows, tile_regions.shape[1])
-    inv = places(tile_regions, own_rows)
+    blocks = regions // LANES
+    hot, zc, half, w1 = tables(region_local, cell_weight, polar_rows, tile_regions.shape[1], blocks)
+    where = places(tile_regions, own_rows)
     lam, level0, row_sums = transport(
-        band, lats, adjoint, transport_rates, w_in, e_in, east, west, before, after, up, down, trc, lev, rows)
+        lats, adjoint, transport_rates, w_in, e_in, east, west, before, after, up, down, trc, lev, rows)
 
     if lons <= 4:
         parts = [row_sums] + [lax.ppermute(row_sums, "lon", partners(lons, k)) for k in range(1, lons)]
@@ -555,11 +574,12 @@
             jnp.broadcast_to(row_sums[None], (lons,) + row_sums.shape), "lon", 0, 0, tiled=True)
         parts = [jnp.sum(got, axis=0)]
     s1 = local_sums(level0, w1, hot)
-    zonal, copies = regional(parts, s1, zc, trc, devices, cols * lons)
+    zonal, copies = regional(parts, s1, zc, trc, devices, cols * lons, blocks)
     sums = lax.all_to_all(copies, AXES, 0, 0, tiled=True)
+    sums = sums.reshape(-1, sums.shape[2])
     adjoint_out = filtered(lam, zonal, half, trc, lev).reshape(adjoint.shape)
-    base = base_product(tile, have, theirs, covariance, turn, grad_in.shape[1])
-    precond = finish(week_index, sums, inv, covariance, base, trc)
+    base = base_product(have, theirs, covariance, turn, grad_in.shape[1])
+    precond = finish(week_index, sums, where, covariance, base, trc)
     return adjoint_out, precond
 
 

time: 77.8 us -> 78.1 us (level)
  waiting for transfers between devices: 32 us -> 30.3 us
  local copies, waits for them, and re-layouts: 1.84 us -> 3.06 us
    all_to_all x1, waiting for transfers between devices: 4.49 us -> 3.14 us  [shards(): sums = lax.all_to_all(copies, AXES, 0, 0, tiled=True)]
    unnamed x20, local copies, waits for them, and re-layouts: 1.84 us -> 3.06 us
where the time goes in v3:
time: 78.1 us; the launch traced here: 77.8 us
  waiting for transfers between devices  30.3 us (39%)
  starting transfers between devices  25 us (32%)
  Pallas kernels  18 us (23%)
  local copies, waits for them, and re-layouts  3.06 us (4%)
  between operations  1.44 us (2%)
    ppermute x5, waiting for transfers between devices, exchange(): return lax.ppermute(x, AXES, partners(devices, 1 << order[i]))  21.1 us
    pallas_call x15, Pallas kernels, apply(): return run(*(place(x, spec) for x, spec in zip(args, in_specs)))  18 us
    ppermute x5, starting transfers between devices, exchange(): return lax.ppermute(x, AXES, partners(devices, 1 << order[i]))  8.5 us
    ppermute x3, starting transfers between devices, shards(): lax.ppermute(row_sums, 'lon', partners(lons, k))  4.39 us
    ppermute x1, starting transfers between devices, shards(): e_in = lax.ppermute(west, 'lon', west_to)  3.77 us
    all_to_all x1, starting transfers between devices, shards(): sums = lax.all_to_all(copies, AXES, 0, 0, tiled=True)  3.3 us
    all_to_all x1, waiting for transfers between devices, shards(): sums = lax.all_to_all(copies, AXES, 0, 0, tiled=True)  3.14 us
    unnamed x20, local copies, waits for them, and re-layouts  3.06 us
  transfers between devices with their start and end apart: 13, of which 9 were waited for; matrix products, arithmetic and copies ran while one was open for 0% of the time, Pallas kernels for 20%

profile of v3, /device:TPU:0, one launch (start us, length us, event | category | flops | bytes accessed | tf_op | source)
XLA Modules:
  0.0 77.8 jit_solution(3312236924287059273)
XLA Ops:
  0.6 4.1 %collective-permute-start.7 = (bf16[64,416]{1,0:T(8,128)(2,1)}, bf16[64,416]{1,0:T(8,128)(2,1)S(1)}, u32[]{:S(2)}, u32[]{:S(2)}) collective-permute-start(bf16[64,416]{1,0:T(8,128)(2,1)} %refs_0_.1), channel_id=1, source_target_pairs={{0,2},{1,3},{2,0},{3,1},{4,6},{5,7},{6,4},{7,5},{8,10},{9,11},{10,... | collective-permute-start | bytes 159752 | tf_op jit(solution)/shard_map/ppermute | solution.py:549
  4.8 3.9 %collective-permute-done.7.refs_1_ = bf16[64,416]{1,0:T(8,128)(2,1)S(1)} collective-permute-done((bf16[64,416]{1,0:T(8,128)(2,1)}, bf16[64,416]{1,0:T(8,128)(2,1)S(1)}, u32[]{:S(2)}, u32[]{:S(2)}) %collective-permute-start.7) | collective-permute-done | bytes 53280 | tf_op jit(solution)/shard_map/ppermute | solution.py:549
  8.6 0.8 %copy-done.5 = bf16[64,416]{1,0:T(8,128)(2,1)S(1)} copy-done((bf16[64,416]{1,0:T(8,128)(2,1)S(1)}, bf16[64,416]{1,0:T(8,128)(2,1)}, u32[]{:S(2)}) %copy-start.5) | copy-done | bytes 53272
  9.5 1.8 %collective-permute-start.8 = (bf16[128,416]{1,0:T(8,128)(2,1)S(1)}, bf16[128,416]{1,0:T(8,128)(2,1)S(1)}, u32[]{:S(2)}, u32[]{:S(2)}) collective-permute-start(bf16[128,416]{1,0:T(8,128)(2,1)S(1)} %shard_map.113.refs_0_), channel_id=1, source_target_pairs={{0,8},{1,9},{2,10},{3,11},{4,12},{5,13},{6,14},{7,15},{8,0},{9,1},... | collective-permute-start | bytes 319496 | tf_op jit(solution)/shard_map/ppermute | solution.py:549
  11.2 3.3 %collective-permute-done.8.refs_1_ = bf16[128,416]{1,0:T(8,128)(2,1)S(1)} collective-permute-done((bf16[128,416]{1,0:T(8,128)(2,1)S(1)}, bf16[128,416]{1,0:T(8,128)(2,1)S(1)}, u32[]{:S(2)}, u32[]{:S(2)}) %collective-permute-start.8) | collective-permute-done | bytes 106528 | tf_op jit(solution)/shard_map/ppermute | solution.py:549
  14.5 0.7 collective-permute-start.9
  15.3 5.7 %collective-permute-done.9.refs_1_ = bf16[256,416]{1,0:T(8,128)(2,1)S(1)} collective-permute-done((bf16[256,416]{1,0:T(8,128)(2,1)S(1)}, bf16[256,416]{1,0:T(8,128)(2,1)S(1)}, u32[]{:S(2)}, u32[]{:S(2)}) %collective-permute-start.9) | collective-permute-done | bytes 213024 | tf_op jit(solution)/shard_map/ppermute | solution.py:549
  21.0 0.0 copy-start
  21.0 0.0 copy-start.1
  21.0 1.8 %collective-permute-start.10 = (bf16[512,416]{1,0:T(8,128)(2,1)S(1)}, bf16[512,416]{1,0:T(8,128)(2,1)S(1)}, u32[]{:S(2)}, u32[]{:S(2)}) collective-permute-start(bf16[512,416]{1,0:T(8,128)(2,1)S(1)} %shard_map.115.refs_0_), channel_id=1, source_target_pairs={{0,16},{1,17},{2,18},{3,19},{4,20},{5,21},{6,22},{7,23},{8,24},{9,... | collective-permute-start | bytes 1277960 | tf_op jit(solution)/shard_map/ppermute | solution.py:549
  22.8 8.3 %collective-permute-done.10.refs_1_ = bf16[512,416]{1,0:T(8,128)(2,1)S(1)} collective-permute-done((bf16[512,416]{1,0:T(8,128)(2,1)S(1)}, bf16[512,416]{1,0:T(8,128)(2,1)S(1)}, u32[]{:S(2)}, u32[]{:S(2)}) %collective-permute-start.10) | collective-permute-done | bytes 426016 | tf_op jit(solution)/shard_map/ppermute | solution.py:549
  31.1 0.1 shard_map.116.a
  31.2 0.1 collective-permute-start.11
  31.3 1.2 %shard_map.105 = (f32[22,8,128]{2,1,0:T(8,128)S(1)}, f32[22,8,128]{2,1,0:T(8,128)S(1)}) custom-call(f32[64,32,128]{2,1,0:T(8,128)} %bitcast.5, f32[48,32,128]{2,1,0:T(8,128)} %bitcast.8), custom_call_target="tpu_custom_call" | custom-call | tf_op jit(solution)/shard_map/pallas_call | solution.py:58
  32.5 0.5 collective-permute-start
  33.1 2.2 %collective-permute-start.1 = (f32[22,8,128]{2,1,0:T(8,128)S(1)}, f32[22,8,128]{2,1,0:T(8,128)S(1)}, u32[]{:S(2)}, u32[]{:S(2)}) collective-permute-start(f32[22,8,128]{2,1,0:T(8,128)S(1)} %get-tuple-element.20.my_down), channel_id=1, source_target_pairs={{4,0},{8,4},{12,8},{16,12},{20,16},{24,20},{28,24},{0,28},{5,1},{9... | collective-permute-start | bytes 270344 | tf_op jit(solution)/shard_map/ppermute | solution.py:559
  35.2 0.0 copy-done
  35.2 1.5 %shard_map.104 = (f32[72,128]{1,0:T(8,128)S(1)}, f32[72,128]{1,0:T(8,128)S(1)}) custom-call(f32[64,32,128]{2,1,0:T(8,128)S(1)} %bitcast.6, f32[48,32,128]{2,1,0:T(8,128)S(1)} %bitcast.9), custom_call_target="tpu_custom_call" | custom-call | tf_op jit(solution)/shard_map/pallas_call | solution.py:58
  36.7 0.7 collective-permute-done.b
  37.4 0.0 collective-permute-done.1.a
  37.4 0.1 shard_map.106
  37.5 2.3 %collective-permute-start.2 = (f32[72,128]{1,0:T(8,128)S(1)}, f32[72,128]{1,0:T(8,128)S(1)}, u32[]{:S(2)}, u32[]{:S(2)}) collective-permute-start(f32[72,128]{1,0:T(8,128)S(1)} %get-tuple-element.21.my_east), channel_id=1, source_target_pairs={{0,1},{1,2},{2,3},{3,0},{4,5},{5,6},{6,7},{7,4},{8,9},{9,10},{10,1... | collective-permute-start | bytes 110600 | tf_op jit(solution)/shard_map/ppermute | solution.py:562
  39.9 3.8 %collective-permute-start.3 = (f32[72,128]{1,0:T(8,128)S(1)}, f32[72,128]{1,0:T(8,128)S(1)}, u32[]{:S(2)}, u32[]{:S(2)}) collective-permute-start(f32[72,128]{1,0:T(8,128)S(1)} %get-tuple-element.22.my_west), channel_id=1, source_target_pairs={{1,0},{2,1},{3,2},{0,3},{5,4},{6,5},{7,6},{4,7},{9,8},{10,9},{11,1... | collective-permute-start | bytes 110600 | tf_op jit(solution)/shard_map/ppermute | solution.py:563
  43.6 2.2 %collective-permute-done.2.w_in = f32[72,128]{1,0:T(8,128)S(1)} collective-permute-done((f32[72,128]{1,0:T(8,128)S(1)}, f32[72,128]{1,0:T(8,128)S(1)}, u32[]{:S(2)}, u32[]{:S(2)}) %collective-permute-start.2) | collective-permute-done | bytes 36896 | tf_op jit(solution)/shard_map/ppermute | solution.py:562
  45.8 0.4 collective-permute-done.3.e_in
  46.2 3.9 %shard_map.107 = (f32[64,32,128]{2,1,0:T(8,128)S(1)}, f32[256,128]{1,0:T(8,128)S(1)}, f32[32,128]{1,0:T(8,128)S(1)}) custom-call(f32[64,32,128]{2,1,0:T(8,128)S(1)} %bitcast.7, f32[48,32,128]{2,1,0:T(8,128)S(1)} %bitcast.10, f32[72,128]{1,0:T(8,128)S(1)} %collective-permute-done.2.w_in, f32[72,128]{1,0:T(8,128)S(1)} %collective-permute-done.3.e_in, ...), custom_call_target="tpu_custom_call" | custom-call | tf_op jit(solution)/shard_map/pallas_call | solution.py:58
  50.1 0.0 copy-start.3
  50.2 1.0 %copy-done.3 = f32[64,32,128]{2,1,0:T(8,128)} copy-done((f32[64,32,128]{2,1,0:T(8,128)}, f32[64,32,128]{2,1,0:T(8,128)S(1)}, u32[]{:S(2)}) %copy-start.3) | copy-done | bytes 1048600
  51.1 1.0 %collective-permute-start.4 = (f32[32,128]{1,0:T(8,128)S(1)}, f32[32,128]{1,0:T(8,128)S(1)}, u32[]{:S(2)}, u32[]{:S(2)}) collective-permute-start(f32[32,128]{1,0:T(8,128)S(1)} %get-tuple-element.24.refs_0_), channel_id=1, source_target_pairs={{0,1},{1,0},{2,3},{3,2},{4,5},{5,4},{6,7},{7,6},{8,9},{9,8},{10,11... | collective-permute-start | bytes 49160 | tf_op jit(solution)/shard_map/ppermute | solution.py:571
  52.2 3.0 %collective-permute-start.5 = (f32[32,128]{1,0:T(8,128)S(1)}, f32[32,128]{1,0:T(8,128)S(1)}, u32[]{:S(2)}, u32[]{:S(2)}) collective-permute-start(f32[32,128]{1,0:T(8,128)S(1)} %get-tuple-element.24.refs_0_), channel_id=1, source_target_pairs={{0,2},{1,3},{2,0},{3,1},{4,6},{5,7},{6,4},{7,5},{8,10},{9,11},{10,... | collective-permute-start | bytes 49160 | tf_op jit(solution)/shard_map/ppermute | solution.py:571
  55.1 0.4 collective-permute-start.6
  55.5 1.4 %shard_map.108 = (bf16[256,4096]{1,0:T(8,128)(2,1)S(1)}, bf16[256,192]{1,0:T(8,128)(2,1)S(1)}, f32[32,128]{1,0:T(8,128)S(1)}, f32[32,128]{1,0:T(8,128)S(1)}) custom-call(s32[32,128]{1,0:T(8,128)S(1)} %copy-done.7, f32[32,128]{1,0:T(8,128)S(1)} %copy-done.8, s32[1,32]{1,0:T(1,128)S(1)} %bitcast.11), custom_call_target="tpu_custom_call" | custom-call | tf_op jit(solution)/shard_map/pallas_call | solution.py:58
  56.9 0.9 %shard_map.109.refs_4_ = f32[256,128]{1,0:T(8,128)S(1)} custom-call(f32[256,128]{1,0:T(8,128)S(1)} %get-tuple-element.25.l0, f32[32,128]{1,0:T(8,128)S(1)} %get-tuple-element.26.w, bf16[256,4096]{1,0:T(8,128)(2,1)S(1)} %get-tuple-element.27.hot_ref), custom_call_target="tpu_custom_call" | custom-call | tf_op jit(solution)/shard_map/pallas_call | solution.py:58
  57.8 0.0 collective-permute-done.4.refs_1_
  57.8 0.0 collective-permute-done.5.refs_2_
  57.9 2.8 %collective-permute-done.6.refs_3_ = f32[32,128]{1,0:T(8,128)S(1)} collective-permute-done((f32[32,128]{1,0:T(8,128)S(1)}, f32[32,128]{1,0:T(8,128)S(1)}, u32[]{:S(2)}, u32[]{:S(2)}) %collective-permute-start.6) | collective-permute-done | bytes 16416 | tf_op jit(solution)/shard_map/ppermute | solution.py:571
  60.7 1.0 %shard_map.110 = (f32[32,128]{1,0:T(8,128)S(1)}, f32[32,16,128]{2,1,0:T(8,128)}) custom-call(f32[32,128]{1,0:T(8,128)S(1)} %get-tuple-element.24.refs_0_, f32[32,128]{1,0:T(8,128)S(1)} %collective-permute-done.4.refs_1_, f32[32,128]{1,0:T(8,128)S(1)} %collective-permute-done.5.refs_2_, f32[32,128]{1,0:T(8,128)S(1)} %collective-permute-done.6.refs_3_, ...), custom_call_target="tpu_custom_call" | custom-call | tf_op jit(solution)/shard_map/pallas_call | solution.py:58
  61.7 3.3 %all-to-all-start = ((f32[32,16,128]{2,1,0:T(8,128)}), f32[32,16,128]{2,1,0:T(8,128)}, u32[]{:S(2)}, u32[]{:S(2)}) async-start(f32[32,16,128]{2,1,0:T(8,128)} %get-tuple-element.31), calls=%async_computation | async-start | bytes 524288 | tf_op jit(solution)/shard_map/all_to_all | solution.py:578
  65.0 0.0 copy-start.2
  65.0 1.8 %shard_map.112.hot_ref = bf16[2048,512]{1,0:T(8,128)(2,1)S(1)} custom-call(s32[32,256]{1,0:T(8,128)S(1)} %copy-done.6), custom_call_target="tpu_custom_call" | custom-call | tf_op jit(solution)/shard_map/pallas_call | solution.py:58
  67.5 0.0 copy-start.4
  67.5 1.2 %copy-done.4 = f32[64,32,128]{2,1,0:T(8,128)S(1)} copy-done((f32[64,32,128]{2,1,0:T(8,128)S(1)}, f32[64,32,128]{2,1,0:T(8,128)}, u32[]{:S(2)}) %copy-start.4) | copy-done | bytes 1048600
  68.7 1.5 %shard_map.111 = f32[64,32,128]{2,1,0:T(8,128)} custom-call(f32[64,32,128]{2,1,0:T(8,128)S(1)} %copy-done.4, f32[32,128]{1,0:T(8,128)S(1)} %get-tuple-element.29.z_ref, f32[32,128]{1,0:T(8,128)S(1)} %get-tuple-element.30.h_ref), custom_call_target="tpu_custom_call" | custom-call | tf_op jit(solution)/shard_map/pallas_call | solution.py:58
  70.2 0.0 collective-permute-done.11.b
  70.2 0.0 copy-done.2
  70.2 1.8 %shard_map.117.base_ref = f32[64,416]{1,0:T(8,128)S(1)} custom-call(bf16[1024,512]{1,0:T(8,128)(2,1)S(1)} %shard_map.116.a, bf16[1024,512]{1,0:T(8,128)(2,1)} %collective-permute-done.11.b, bf16[64,2048]{1,0:T(8,128)(2,1)S(1)} %copy-done.2), custom_call_target="tpu_custom_call" | custom-call | tf_op jit(solution)/shard_map/pallas_call | solution.py:58
  72.0 3.1 %all-to-all-done = f32[32,16,128]{2,1,0:T(8,128)} async-done(((f32[32,16,128]{2,1,0:T(8,128)}), f32[32,16,128]{2,1,0:T(8,128)}, u32[]{:S(2)}, u32[]{:S(2)}) %all-to-all-start) | async-done | bytes 262176 | tf_op jit(solution)/shard_map/all_to_all | solution.py:578
  75.2 2.6 %shard_map.118 = f32[64,416]{1,0:T(8,128)} custom-call(s32[1]{0:T(128)S(6)} %copy.11.week_ref, f32[512,128]{1,0:T(8,128)} %bitcast.4.s_ref, bf16[2048,512]{1,0:T(8,128)(2,1)S(1)} %shard_map.112.hot_ref, bf16[64,2048]{1,0:T(8,128)(2,1)S(1)} %copy-done.2, f32[64,416]{1,0:T(8,128)S(1)} %shard_map.117.base_ref), custom_call_target="tpu_custom_call" | custom-call | tf_op jit(solution)/shard_map/pallas_call | solution.py:58
  (13 shorter events, 0.1 us)
Async XLA Ops:
  0.6 8.0 %collective-permute-start.7 = (bf16[64,416]{1,0:T(8,128)(2,1)}, bf16[64,416]{1,0:T(8,128)(2,1)S(1)}, u32[]{:S(2)}, u32[]{:S(2)}) collective-permute-start(bf16[64,416]{1,0:T(8,128)(2,1)} %refs_0_.1), channel_id=1, source_target_pairs={{0,2},{1,3},{2,0},{3,1},{4,6},{5,7},{6,4},{7,5},{8,10},{9,11},{10,... | collective-permute-start | bytes 159752 | tf_op jit(solution)/shard_map/ppermute | solution.py:549
  8.6 0.8 %copy-start.5 = (bf16[64,416]{1,0:T(8,128)(2,1)S(1)}, bf16[64,416]{1,0:T(8,128)(2,1)}, u32[]{:S(2)}) copy-start(bf16[64,416]{1,0:T(8,128)(2,1)} %refs_0_.1) | copy-start | bytes 159748
  9.5 5.0 %collective-permute-start.8 = (bf16[128,416]{1,0:T(8,128)(2,1)S(1)}, bf16[128,416]{1,0:T(8,128)(2,1)S(1)}, u32[]{:S(2)}, u32[]{:S(2)}) collective-permute-start(bf16[128,416]{1,0:T(8,128)(2,1)S(1)} %shard_map.113.refs_0_), channel_id=1, source_target_pairs={{0,8},{1,9},{2,10},{3,11},{4,12},{5,13},{6,14},{7,15},{8,0},{9,1},... | collective-permute-start | bytes 319496 | tf_op jit(solution)/shard_map/ppermute | solution.py:549
  14.5 6.4 %collective-permute-start.9 = (bf16[256,416]{1,0:T(8,128)(2,1)S(1)}, bf16[256,416]{1,0:T(8,128)(2,1)S(1)}, u32[]{:S(2)}, u32[]{:S(2)}) collective-permute-start(bf16[256,416]{1,0:T(8,128)(2,1)S(1)} %shard_map.114.refs_0_), channel_id=1, source_target_pairs={{0,1},{1,0},{2,3},{3,2},{4,5},{5,4},{6,7},{7,6},{8,9},{9,8},{10,11... | collective-permute-start | bytes 638984 | tf_op jit(solution)/shard_map/ppermute | solution.py:549
  21.0 14.2 %copy-start = (f32[8,8,32,128]{3,2,1,0:T(8,128)S(1)}, f32[8,8,32,128]{3,2,1,0:T(8,128)}, u32[]{:S(2)}) copy-start(f32[8,8,32,128]{3,2,1,0:T(8,128)} %param.9) | copy-start | bytes 3145732
  21.0 14.2 %copy-start.1 = (f32[6,8,32,128]{3,2,1,0:T(8,128)S(1)}, f32[6,8,32,128]{3,2,1,0:T(8,128)}, u32[]{:S(2)}) copy-start(f32[6,8,32,128]{3,2,1,0:T(8,128)} %param.10) | copy-start | bytes 2359300
  21.0 10.1 %collective-permute-start.10 = (bf16[512,416]{1,0:T(8,128)(2,1)S(1)}, bf16[512,416]{1,0:T(8,128)(2,1)S(1)}, u32[]{:S(2)}, u32[]{:S(2)}) collective-permute-start(bf16[512,416]{1,0:T(8,128)(2,1)S(1)} %shard_map.115.refs_0_), channel_id=1, source_target_pairs={{0,16},{1,17},{2,18},{3,19},{4,20},{5,21},{6,22},{7,23},{8,24},{9,... | collective-permute-start | bytes 1277960 | tf_op jit(solution)/shard_map/ppermute | solution.py:549
  31.2 39.0 %collective-permute-start.11 = (bf16[1024,512]{1,0:T(8,128)(2,1)S(1)}, bf16[1024,512]{1,0:T(8,128)(2,1)}, u32[]{:S(2)}, u32[]{:S(2)}) collective-permute-start(bf16[1024,512]{1,0:T(8,128)(2,1)S(1)} %shard_map.116.a), channel_id=1, source_target_pairs={{0,4},{1,5},{2,6},{3,7},{4,0},{5,1},{6,2},{7,3},{8,12},{9,13},{10,... | collective-permute-start | bytes 3145736 | tf_op jit(solution)/shard_map/ppermute | solution.py:549
  32.5 4.9 %collective-permute-start = (f32[22,8,128]{2,1,0:T(8,128)S(1)}, f32[22,8,128]{2,1,0:T(8,128)S(1)}, u32[]{:S(2)}, u32[]{:S(2)}) collective-permute-start(f32[22,8,128]{2,1,0:T(8,128)S(1)} %get-tuple-element.19.my_up), channel_id=1, source_target_pairs={{0,4},{4,8},{8,12},{12,16},{16,20},{20,24},{24,28},{28,0},{1,5},{5... | collective-permute-start | bytes 270344 | tf_op jit(solution)/shard_map/ppermute | solution.py:558
  33.0 22.5 %copy-start.7 = (s32[32,128]{1,0:T(8,128)S(1)}, s32[32,128]{1,0:T(8,128)}, u32[]{:S(2)}) copy-start(s32[32,128]{1,0:T(8,128)} %rl.1) | copy-start | bytes 49156
  33.0 22.5 %copy-start.8 = (f32[32,128]{1,0:T(8,128)S(1)}, f32[32,128]{1,0:T(8,128)}, u32[]{:S(2)}) copy-start(f32[32,128]{1,0:T(8,128)} %w_ref.1) | copy-start | bytes 49156
  33.0 22.5 %copy-start.9 = (s32[32]{0:T(128)S(1)}, s32[32]{0:T(128)}, u32[]{:S(2)}) copy-start(s32[32]{0:T(128)} %param.14) | copy-start | bytes 388
  33.1 4.4 %collective-permute-start.1 = (f32[22,8,128]{2,1,0:T(8,128)S(1)}, f32[22,8,128]{2,1,0:T(8,128)S(1)}, u32[]{:S(2)}, u32[]{:S(2)}) collective-permute-start(f32[22,8,128]{2,1,0:T(8,128)S(1)} %get-tuple-element.20.my_down), channel_id=1, source_target_pairs={{4,0},{8,4},{12,8},{16,12},{20,16},{24,20},{28,24},{0,28},{5,1},{9... | collective-permute-start | bytes 270344 | tf_op jit(solution)/shard_map/ppermute | solution.py:559
  37.5 8.3 %collective-permute-start.2 = (f32[72,128]{1,0:T(8,128)S(1)}, f32[72,128]{1,0:T(8,128)S(1)}, u32[]{:S(2)}, u32[]{:S(2)}) collective-permute-start(f32[72,128]{1,0:T(8,128)S(1)} %get-tuple-element.21.my_east), channel_id=1, source_target_pairs={{0,1},{1,2},{2,3},{3,0},{4,5},{5,6},{6,7},{7,4},{8,9},{9,10},{10,1... | collective-permute-start | bytes 110600 | tf_op jit(solution)/shard_map/ppermute | solution.py:562
  39.9 6.4 %collective-permute-start.3 = (f32[72,128]{1,0:T(8,128)S(1)}, f32[72,128]{1,0:T(8,128)S(1)}, u32[]{:S(2)}, u32[]{:S(2)}) collective-permute-start(f32[72,128]{1,0:T(8,128)S(1)} %get-tuple-element.22.my_west), channel_id=1, source_target_pairs={{1,0},{2,1},{3,2},{0,3},{5,4},{6,5},{7,6},{4,7},{9,8},{10,9},{11,1... | collective-permute-start | bytes 110600 | tf_op jit(solution)/shard_map/ppermute | solution.py:563
  50.1 1.0 %copy-start.3 = (f32[64,32,128]{2,1,0:T(8,128)}, f32[64,32,128]{2,1,0:T(8,128)S(1)}, u32[]{:S(2)}) copy-start(f32[64,32,128]{2,1,0:T(8,128)S(1)} %get-tuple-element.23.l_ref) | copy-start | bytes 3145732
  51.1 13.9 %copy-start.6 = (s32[32,256]{1,0:T(8,128)S(1)}, s32[32,256]{1,0:T(8,128)}, u32[]{:S(2)}) copy-start(s32[32,256]{1,0:T(8,128)} %tr.1) | copy-start | bytes 98308
  51.1 6.7 %collective-permute-start.4 = (f32[32,128]{1,0:T(8,128)S(1)}, f32[32,128]{1,0:T(8,128)S(1)}, u32[]{:S(2)}, u32[]{:S(2)}) collective-permute-start(f32[32,128]{1,0:T(8,128)S(1)} %get-tuple-element.24.refs_0_), channel_id=1, source_target_pairs={{0,1},{1,0},{2,3},{3,2},{4,5},{5,4},{6,7},{7,6},{8,9},{9,8},{10,11... | collective-permute-start | bytes 49160 | tf_op jit(solution)/shard_map/ppermute | solution.py:571
  52.2 5.7 %collective-permute-start.5 = (f32[32,128]{1,0:T(8,128)S(1)}, f32[32,128]{1,0:T(8,128)S(1)}, u32[]{:S(2)}, u32[]{:S(2)}) collective-permute-start(f32[32,128]{1,0:T(8,128)S(1)} %get-tuple-element.24.refs_0_), channel_id=1, source_target_pairs={{0,2},{1,3},{2,0},{3,1},{4,6},{5,7},{6,4},{7,5},{8,10},{9,11},{10,... | collective-permute-start | bytes 49160 | tf_op jit(solution)/shard_map/ppermute | solution.py:571
  55.1 5.5 %collective-permute-start.6 = (f32[32,128]{1,0:T(8,128)S(1)}, f32[32,128]{1,0:T(8,128)S(1)}, u32[]{:S(2)}, u32[]{:S(2)}) collective-permute-start(f32[32,128]{1,0:T(8,128)S(1)} %get-tuple-element.24.refs_0_), channel_id=1, source_target_pairs={{0,3},{1,2},{2,1},{3,0},{4,7},{5,6},{6,5},{7,4},{8,11},{9,10},{10,... | collective-permute-start | bytes 49160 | tf_op jit(solution)/shard_map/ppermute | solution.py:571
  61.7 13.5 %all-to-all-start = ((f32[32,16,128]{2,1,0:T(8,128)}), f32[32,16,128]{2,1,0:T(8,128)}, u32[]{:S(2)}, u32[]{:S(2)}) async-start(f32[32,16,128]{2,1,0:T(8,128)} %get-tuple-element.31), calls=%async_computation | async-start | bytes 524288 | tf_op jit(solution)/shard_map/all_to_all | solution.py:578
  65.0 5.2 %copy-start.2 = (bf16[64,2048]{1,0:T(8,128)(2,1)S(1)}, bf16[64,2048]{1,0:T(8,128)(2,1)}, u32[]{:S(2)}) copy-start(bf16[64,2048]{1,0:T(8,128)(2,1)} %cov_ref.3) | copy-start | bytes 786436
  67.5 1.2 %copy-start.4 = (f32[64,32,128]{2,1,0:T(8,128)S(1)}, f32[64,32,128]{2,1,0:T(8,128)}, u32[]{:S(2)}) copy-start(f32[64,32,128]{2,1,0:T(8,128)} %copy-done.3) | copy-start | bytes 3145732

commit v4 on v3

--- a/solution.py
+++ b/solution.py
@@ -73,9 +73,9 @@
 
     def body(f, t, up, down, f_last, f_first, t_last, t_first, sem):
         moves = [
-            pltpu.make_async_copy(src.at[:, pl.ds(at, 8), :], dst, sem.at[i])
+            pltpu.make_async_copy(src.at[:, pl.ds(at, 2), :], dst.at[:, pl.ds(0, 2), :], sem.at[i])
             for i, (src, at, dst) in enumerate(
-                ((f, rows - 8, f_last), (f, 0, f_first), (t, rows - 8, t_last), (t, 0, t_first)))
+                ((f, rows - 2, f_last), (f, 0, f_first), (t, rows - 2, t_last), (t, 0, t_first)))
         ]
         for move in moves:
             move.start()
@@ -85,15 +85,15 @@
 
         moves[0].wait()
         for k in range(trc):
-            up[k] = row(f_last, k, 6)
-            up[trc + k] = row(f_last, k, 7)
+            up[k] = row(f_last, k, 0)
+            up[trc + k] = row(f_last, k, 1)
         moves[1].wait()
         for k in range(trc):
             down[k] = row(f_first, k, 1)
             down[trc + k] = row(f_first, k, 0)
         moves[2].wait()
         for d in range(6):
-            up[2 * trc + d] = row(t_last, d, 7)
+            up[2 * trc + d] = row(t_last, d, 1)
         moves[3].wait()
         for d in range(6):
             down[2 * trc + d] = row(t_first, d, 0)
@@ -169,42 +169,95 @@
         east, west, before, after)
 
 
-def transport_kernel(trc, lev, rows, bands, field, tv, w_in, e_in, my_east, my_west, b, a, my_up, my_down,
-                     lam, level0, row_sums, f1, cols, ghost0, ghost1, mids, halves):
+def centre(rate):
+    return 1.0 - rate[0] - rate[1] - rate[2] - rate[3] - rate[4] - rate[5]
+
+
+def edge_rates(ref, trc, lev):
+    sub = iota((lev, LANES), 0)
+    rate = [ref[2 * trc + d] for d in range(6)]
+    rate[4] = jnp.where(sub < lev - 1, rate[4], 0.0)
+    rate[5] = jnp.where(sub > 0, rate[5], 0.0)
+    return rate, centre(rate)
+
+
+def stencil(load, mids, tv, lev, rows, emit):
+    for l in range(lev):
+        for r in range(0, rows, 8):
+            rate = [tv[d * lev + l, pl.ds(r, 8), :] for d in range(6)]
+            c = load(l, r, 0)
+            west, east = pltpu.roll(c, 1, 1), pltpu.roll(c, LANES - 1, 1)
+            v = mids[l, pl.ds(r, 8), :] * c + rate[2] * load(l, r, 1) + rate[3] * load(l, r, -1)
+            if l < lev - 1:
+                v = v + rate[4] * load(l + 1, r, 0)
+            if l > 0:
+                v = v + rate[5] * load(l - 1, r, 0)
+            emit(l, r, v, rate, west, east)
+
+
+def first_step(bands, field, rates, before, after, up, down, trc, lev, rows):
+    high = rows + 2 * OFF
+    tiles = trc * lev
+
+    def body(f, tv, b, a, my_up, my_down, f1, mids):
+        lane, edge = iota((8, LANES), 1), iota((8, LANES), 0)
+        lane_l = iota((lev, LANES), 1)
+        flat = f1.reshape(tiles * high, LANES)
+        bf, af = (x.reshape((2 * trc + 6) * lev, LANES) for x in (b, a))
+        south_mask, north_mask = masks(lax.axis_index("lat"), bands)
+        for which, (ref, mine, mask) in enumerate(zip((b, a), (my_down, my_up), (south_mask, north_mask))):
+            rate, mid = edge_rates(ref, trc, lev)
+            for k in range(trc):
+                c = ref[trc + k]
+                far, own = ref[k], mine[trc + k]
+                north, south = (own, far) if which == 0 else (far, own)
+                east = jnp.where(lane_l == LANES - 1, 0.0, pltpu.roll(c, LANES - 1, 1))
+                west = jnp.where(lane_l == 0, 0.0, pltpu.roll(c, 1, 1))
+                g = (mid * c + rate[0] * east + rate[1] * west + rate[2] * north + rate[3] * south
+                     + rate[4] * pltpu.roll(c, lev - 1, 0) + rate[5] * pltpu.roll(c, 1, 0))
+                at = OFF - 1 if which == 0 else OFF + rows
+                flat[pl.ds(k * lev * high + at, lev, stride=high), :] = g * mask
+        for l in range(lev):
+            for r in range(0, rows, 8):
+                rate = [tv[d * lev + l, pl.ds(r, 8), :] for d in range(6)]
+                if l == lev - 1:
+                    rate[4] = jnp.zeros_like(rate[4])
+                if l == 0:
+                    rate[5] = jnp.zeros_like(rate[5])
+                mids[l, pl.ds(r, 8), :] = centre(rate)
+
+        def tracer(k, carry):
+            def load(l, r, by):
+                m = k * lev + l
+                if r + by < 0:
+                    ghost = bf[pl.ds((trc + k) * lev + l, 8, stride=0), :] * south_mask
+                    return jnp.where(edge == 0, ghost, pltpu.roll(f[m, pl.ds(0, 8), :], 1, 0))
+                if r + by + 8 > rows:
+                    ghost = af[pl.ds((trc + k) * lev + l, 8, stride=0), :] * north_mask
+                    return jnp.where(edge == 7, ghost, pltpu.roll(f[m, pl.ds(rows - 8, 8), :], 7, 0))
+                return f[m, pl.ds(r + by, 8), :]
+
+            def emit(l, r, v, rate, west, east):
+                f1[k * lev + l, pl.ds(OFF + r, 8), :] = v + (
+                    rate[0] * jnp.where(lane == LANES - 1, 0.0, east) + rate[1] * jnp.where(lane == 0, 0.0, west))
+
+            stencil(load, mids, tv, lev, rows, emit)
+            return carry
+
+        lax.fori_loop(0, trc, tracer, 0)
+
+    return call(body, [((tiles, high, LANES), F32), ((lev, rows, LANES), F32)], [VMEM] * 6)(
+        field.reshape(tiles, rows, LANES), rates.reshape(6 * lev, rows, LANES), before, after, up, down)
+
+
+def transport_kernel(trc, lev, rows, bands, f1, mids, tv, w_in, e_in, my_east, my_west, b, a,
+                     lam, level0, row_sums, whole, cols, ghost0, ghost1, halves):
     high = rows + 2 * OFF
     lane = iota((8, LANES), 1)
     sub = iota((lev, LANES), 0)
     lane_l = iota((lev, LANES), 1)
-    bf, af = (x.reshape((2 * trc + 6) * lev, LANES) for x in (b, a))
     f1_flat = f1.reshape(trc * lev * high, LANES)
-    south_mask, north_mask = masks(lax.axis_index("lat"), bands)
-    edge = iota((8, LANES), 0)
-
-    def centre(rate):
-        return 1.0 - rate[0] - rate[1] - rate[2] - rate[3] - rate[4] - rate[5]
-
-    for which, (ref, mine, mask) in enumerate(zip((b, a), (my_down, my_up), (south_mask, north_mask))):
-        rate = [ref[2 * trc + d] for d in range(6)]
-        rate[4] = jnp.where(sub < lev - 1, rate[4], 0.0)
-        rate[5] = jnp.where(sub > 0, rate[5], 0.0)
-        mid = centre(rate)
-        west_corner = jnp.broadcast_to(w_in[pl.ds(2 * rows + which, 1), :], (lev, LANES))
-        east_corner = jnp.broadcast_to(e_in[pl.ds(2 * rows + which, 1), :], (lev, LANES))
-        for k in range(trc):
-            c = ref[trc + k]
-            far, own = ref[k], mine[trc + k]
-            north, south = (own, far) if which == 0 else (far, own)
-            here = lane_l == k * lev + sub
-            wc = jnp.sum(jnp.where(here, west_corner, 0.0), axis=1, keepdims=True)
-            ec = jnp.sum(jnp.where(here, east_corner, 0.0), axis=1, keepdims=True)
-            east = jnp.where(lane_l == LANES - 1, ec, pltpu.roll(c, LANES - 1, 1))
-            west = jnp.where(lane_l == 0, wc, pltpu.roll(c, 1, 1))
-            upper = pltpu.roll(c, lev - 1, 0)
-            lower = pltpu.roll(c, 1, 0)
-            g = (mid * c + rate[0] * east + rate[1] * west + rate[2] * north + rate[3] * south
-                 + rate[4] * upper + rate[5] * lower)
-            at = OFF - 1 if which == 0 else OFF + rows
-            f1_flat[pl.ds(k * lev * high + at, lev, stride=high), :] = g * mask
+    whole_flat = whole.reshape(lev * high, LANES)
     level_of = lane % lev
     from_west, from_east = lane // 2, (lane + 1) // 2 % 64
 
@@ -232,66 +285,46 @@
                            + rate[4] * upper + rate[5] * lower)
         ghost0[pl.ds(r, 8), :] = ghosts(w_in[pl.ds(r, 8), :], e_in[pl.ds(r, 8), :])
         ghost1[pl.ds(r, 8), :] = ghosts(*stepped)
-    for l in range(lev):
-        for r in range(0, rows, 8):
-            rate = [tv[d * lev + l, pl.ds(r, 8), :] for d in range(6)]
-            if l == lev - 1:
-                rate[4] = jnp.zeros_like(rate[4])
+    side_masks = masks(lax.axis_index("lat"), bands)
+
+    def tracer(k, carry):
+        def beside(ghost, l, r):
+            return pltpu.roll(ghost[pl.ds(r, 8), :], (LANES - 2 * (k * lev + l)) % LANES, 1)
+
+        def ends(at, west, east):
+            return jnp.where(at == 0, west, jnp.where(at == LANES - 1, east, 0.0))
+
+        for which, (ref, mask) in enumerate(zip((b, a), side_masks)):
+            at = OFF - 1 if which == 0 else OFF + rows
+            corner = [jnp.take_along_axis(
+                jnp.broadcast_to(x[pl.ds(2 * rows + which, 1), :], (lev, LANES)), k * lev + sub, axis=1)
+                for x in (w_in, e_in)]
+            more = ends(lane_l, ref[2 * trc + 1] * corner[0], ref[2 * trc] * corner[1])
+            whole_flat[pl.ds(at, lev, stride=high), :] = (
+                f1_flat[pl.ds(k * lev * high + at, lev, stride=high), :] + more * mask)
+        for l in range(lev):
+            for r in range(0, rows, 8):
+                g = beside(ghost0, l, r)
+                whole[l, pl.ds(OFF + r, 8), :] = f1[k * lev + l, pl.ds(OFF + r, 8), :] + ends(
+                    lane, tv[lev + l, pl.ds(r, 8), :] * g, tv[l, pl.ds(r, 8), :] * g)
+
+        def emit(l, r, v, rate, west, east):
+            g = beside(ghost1, l, r)
+            v = v + (rate[0] * jnp.where(lane == LANES - 1, g, east) + rate[1] * jnp.where(lane == 0, g, west))
+            lam[k * lev + l, pl.ds(r, 8), :] = v
             if l == 0:
-                rate[5] = jnp.zeros_like(rate[5])
-            mids[l, pl.ds(r, 8), :] = centre(rate)
-
-    def step(load, ghost, emit, after):
-        def tracer(k, carry):
-            for l in range(lev):
-                for r in range(0, rows, 8):
-                    rate = [tv[d * lev + l, pl.ds(r, 8), :] for d in range(6)]
-                    c = load(k, l, r, 0)
-                    g = pltpu.roll(ghost[pl.ds(r, 8), :], (LANES - 2 * (k * lev + l)) % LANES, 1)
-                    west = jnp.where(lane == 0, g, pltpu.roll(c, 1, 1))
-                    east = jnp.where(lane == LANES - 1, g, pltpu.roll(c, LANES - 1, 1))
-                    v = (mids[l, pl.ds(r, 8), :] * c + rate[2] * load(k, l, r, 1) + rate[3] * load(k, l, r, -1))
-                    if l < lev - 1:
-                        v = v + rate[4] * load(k, l + 1, r, 0)
-                    if l > 0:
-                        v = v + rate[5] * load(k, l - 1, r, 0)
-                    emit(k, l, r, v + (rate[0] * east + rate[1] * west))
-            after(k)
-            return carry
-
-        lax.fori_loop(0, trc, tracer, 0)
-
-    def load0(k, l, r, by):
-        m = k * lev + l
-        if r + by < 0:
-            ghost = bf[pl.ds((trc + k) * lev + l, 8, stride=0), :] * south_mask
-            return jnp.where(edge == 0, ghost, pltpu.roll(field[m, pl.ds(0, 8), :], 1, 0))
-        if r + by + 8 > rows:
-            ghost = af[pl.ds((trc + k) * lev + l, 8, stride=0), :] * north_mask
-            return jnp.where(edge == 7, ghost, pltpu.roll(field[m, pl.ds(rows - 8, 8), :], 7, 0))
-        return field[m, pl.ds(r + by, 8), :]
-
-    def load1(k, l, r, by):
-        return f1[k * lev + l, pl.ds(OFF + r + by, 8), :]
-
-    def emit1(k, l, r, v):
-        f1[k * lev + l, pl.ds(OFF + r, 8), :] = v
-
-    def emit2(k, l, r, v):
-        lam[k * lev + l, pl.ds(r, 8), :] = v
-        if l == 0:
-            level0[pl.ds(r * trc + k, 8, stride=trc), :] = v
-
-    def halve(k):
+                level0[pl.ds(r * trc + k, 8, stride=trc), :] = v
+
+        stencil(lambda l, r, by: whole[l, pl.ds(OFF + r + by, 8), :], mids, tv, lev, rows, emit)
         for l in range(lev):
             for r in range(0, rows, 16):
                 v = lam[k * lev + l, pl.ds(r, 16), :]
                 hi = v.astype(BF16)
                 halves[k, pl.ds(l * rows + r, 16), pl.ds(0, LANES)] = hi
                 halves[k, pl.ds(l * rows + r, 16), pl.ds(LANES, LANES)] = (v - hi.astype(F32)).astype(BF16)
-
-    step(load0, ghost0, emit1, lambda k: None)
-    step(load1, ghost1, emit2, halve)
+        return carry
+
+    lax.fori_loop(0, trc, tracer, 0)
     total = [jnp.zeros((8, LANES), F32) for _ in range(0, rows, 8)]
     ones = jnp.ones((2 * LANES, LANES), BF16)
     for k in range(trc):
@@ -304,22 +337,20 @@
         row_sums[pl.ds(8 * i, 8), :] = total[i]
 
 
-def transport(bands, field, rates, w_in, e_in, east, west, before, after, up, down, trc, lev, rows):
+def transport(bands, f1, mids, rates, w_in, e_in, east, west, before, after, trc, lev, rows):
     high = rows + 2 * OFF
     return call(
         functools.partial(transport_kernel, trc, lev, rows, bands),
         [((trc * lev, rows, LANES), F32), ((rows * trc, LANES), F32), ((rows, LANES), F32)],
-        [VMEM] * 10,
+        [VMEM] * 9,
         [
-            pltpu.VMEM((trc * lev, high, LANES), F32),
+            pltpu.VMEM((lev, high, LANES), F32),
             pltpu.VMEM((2, high, LANES), F32),
             pltpu.VMEM((rows, LANES), F32),
             pltpu.VMEM((rows, LANES), F32),
-            pltpu.VMEM((lev, rows, LANES), F32),
             pltpu.VMEM((trc, lev * rows, 2 * LANES), BF16),
         ],
-    )(field.reshape(trc * lev, rows, LANES), rates.reshape(6 * lev, rows, LANES),
-      w_in, e_in, east, west, before, after, up, down)
+    )(f1, mids, rates.reshape(6 * lev, rows, LANES), w_in, e_in, east, west, before, after)
 
 
 def numbered(row, each, blocks):
@@ -337,14 +368,13 @@
         half[...] = hp
         w = w_ref[...]
         w1[...] = w * (1.0 - hp)
-        w1z = w * hp
+        w1z = split3(w * hp)
         row_id = iota((rows, cols), 0)
         entry = numbered(iota((local, cols), 0), local // blocks, blocks)
         for r in range(rows):
             hot[:, pl.ds(r * cols, cols)] = (rl[pl.ds(r, 1), :] == entry).astype(F32).astype(BF16)
-            parts = split3(jnp.where(row_id == r, w1z, 0.0))
             for i in range(3):
-                wz[pl.ds(i * rows, rows), pl.ds(r * cols, cols)] = parts[i].astype(BF16)
+                wz[pl.ds(i * rows, rows), pl.ds(r * cols, cols)] = jnp.where(row_id == r, w1z[i], 0.0).astype(BF16)
         z = lax.dot_general(wz[...], hot[...], (((1,), (1,)), ((), ())), preferred_element_type=F32)
         z = z[:rows] + z[rows : 2 * rows] + z[2 * rows :]
         hi, mid, lo = split3(jnp.concatenate([z, jnp.zeros((LANES - rows, local), F32)], axis=0))
@@ -564,8 +594,9 @@
     blocks = regions // LANES
     hot, zc, half, w1 = tables(region_local, cell_weight, polar_rows, tile_regions.shape[1], blocks)
     where = places(tile_regions, own_rows)
+    f1, mids = first_step(lats, adjoint, transport_rates, before, after, up, down, trc, lev, rows)
     lam, level0, row_sums = transport(
-        lats, adjoint, transport_rates, w_in, e_in, east, west, before, after, up, down, trc, lev, rows)
+        lats, f1, mids, transport_rates, w_in, e_in, east, west, before, after, trc, lev, rows)
 
     if lons <= 4:
         parts = [row_sums] + [lax.ppermute(row_sums, "lon", partners(lons, k)) for k in range(1, lons)]

time: 78.1 us -> 76.8 us (0.983)
  waiting for transfers between devices: 30.3 us -> 29.1 us
    ppermute x1, waiting for transfers between devices: 2.22 us -> 0.89 us  [shards(): w_in = lax.ppermute(east, 'lon', east_to)]
    pallas_call x15 -> x16, Pallas kernels: 18 us -> 17.8 us  [apply(): return run(*(place(x, spec) for x, spec in zip(args, in_specs)))]
where the time goes in v4:
time: 76.8 us; the launch traced here: 76.4 us
  waiting for transfers between devices  29.1 us (38%)
  starting transfers between devices  25 us (33%)
  Pallas kernels  17.8 us (23%)
  local copies, waits for them, and re-layouts  3.06 us (4%)
  between operations  1.45 us (2%)
    ppermute x5, waiting for transfers between devices, exchange(): return lax.ppermute(x, AXES, partners(devices, 1 << order[i]))  21.1 us
    pallas_call x16, Pallas kernels, apply(): return run(*(place(x, spec) for x, spec in zip(args, in_specs)))  17.8 us
    ppermute x5, starting transfers between devices, exchange(): return lax.ppermute(x, AXES, partners(devices, 1 << order[i]))  8.5 us
    ppermute x3, starting transfers between devices, shards(): lax.ppermute(row_sums, 'lon', partners(lons, k))  4.39 us
    ppermute x1, starting transfers between devices, shards(): e_in = lax.ppermute(west, 'lon', west_to)  3.8 us
    all_to_all x1, starting transfers between devices, shards(): sums = lax.all_to_all(copies, AXES, 0, 0, tiled=True)  3.3 us
    all_to_all x1, waiting for transfers between devices, shards(): sums = lax.all_to_all(copies, AXES, 0, 0, tiled=True)  3.14 us
    unnamed x20, local copies, waits for them, and re-layouts  3.06 us
  transfers between devices with their start and end apart: 13, of which 9 were waited for; matrix products, arithmetic and copies ran while one was open for 0% of the time, Pallas kernels for 20%

profile of v4, /device:TPU:0, one launch (start us, length us, event | category | flops | bytes accessed | tf_op | source)
XLA Modules:
  0.0 76.4 jit_solution(829488475429965203)
XLA Ops:
  0.6 4.1 %collective-permute-start.7 = (bf16[64,416]{1,0:T(8,128)(2,1)}, bf16[64,416]{1,0:T(8,128)(2,1)S(1)}, u32[]{:S(2)}, u32[]{:S(2)}) collective-permute-start(bf16[64,416]{1,0:T(8,128)(2,1)} %refs_0_.1), channel_id=1, source_target_pairs={{0,2},{1,3},{2,0},{3,1},{4,6},{5,7},{6,4},{7,5},{8,10},{9,11},{10,... | collective-permute-start | bytes 159752 | tf_op jit(solution)/shard_map/ppermute | solution.py:579
  4.8 3.9 %collective-permute-done.7.refs_1_ = bf16[64,416]{1,0:T(8,128)(2,1)S(1)} collective-permute-done((bf16[64,416]{1,0:T(8,128)(2,1)}, bf16[64,416]{1,0:T(8,128)(2,1)S(1)}, u32[]{:S(2)}, u32[]{:S(2)}) %collective-permute-start.7) | collective-permute-done | bytes 53280 | tf_op jit(solution)/shard_map/ppermute | solution.py:579
  8.6 0.8 %copy-done.5 = bf16[64,416]{1,0:T(8,128)(2,1)S(1)} copy-done((bf16[64,416]{1,0:T(8,128)(2,1)S(1)}, bf16[64,416]{1,0:T(8,128)(2,1)}, u32[]{:S(2)}) %copy-start.5) | copy-done | bytes 53272
  9.5 1.8 %collective-permute-start.8 = (bf16[128,416]{1,0:T(8,128)(2,1)S(1)}, bf16[128,416]{1,0:T(8,128)(2,1)S(1)}, u32[]{:S(2)}, u32[]{:S(2)}) collective-permute-start(bf16[128,416]{1,0:T(8,128)(2,1)S(1)} %shard_map.114.refs_0_), channel_id=1, source_target_pairs={{0,8},{1,9},{2,10},{3,11},{4,12},{5,13},{6,14},{7,15},{8,0},{9,1},... | collective-permute-start | bytes 319496 | tf_op jit(solution)/shard_map/ppermute | solution.py:579
  11.2 3.3 %collective-permute-done.8.refs_1_ = bf16[128,416]{1,0:T(8,128)(2,1)S(1)} collective-permute-done((bf16[128,416]{1,0:T(8,128)(2,1)S(1)}, bf16[128,416]{1,0:T(8,128)(2,1)S(1)}, u32[]{:S(2)}, u32[]{:S(2)}) %collective-permute-start.8) | collective-permute-done | bytes 106528 | tf_op jit(solution)/shard_map/ppermute | solution.py:579
  14.5 0.7 collective-permute-start.9
  15.3 5.7 %collective-permute-done.9.refs_1_ = bf16[256,416]{1,0:T(8,128)(2,1)S(1)} collective-permute-done((bf16[256,416]{1,0:T(8,128)(2,1)S(1)}, bf16[256,416]{1,0:T(8,128)(2,1)S(1)}, u32[]{:S(2)}, u32[]{:S(2)}) %collective-permute-start.9) | collective-permute-done | bytes 213024 | tf_op jit(solution)/shard_map/ppermute | solution.py:579
  21.0 0.0 copy-start
  21.0 0.0 copy-start.1
  21.0 1.8 %collective-permute-start.10 = (bf16[512,416]{1,0:T(8,128)(2,1)S(1)}, bf16[512,416]{1,0:T(8,128)(2,1)S(1)}, u32[]{:S(2)}, u32[]{:S(2)}) collective-permute-start(bf16[512,416]{1,0:T(8,128)(2,1)S(1)} %shard_map.116.refs_0_), channel_id=1, source_target_pairs={{0,16},{1,17},{2,18},{3,19},{4,20},{5,21},{6,22},{7,23},{8,24},{9,... | collective-permute-start | bytes 1277960 | tf_op jit(solution)/shard_map/ppermute | solution.py:579
  22.8 8.3 %collective-permute-done.10.refs_1_ = bf16[512,416]{1,0:T(8,128)(2,1)S(1)} collective-permute-done((bf16[512,416]{1,0:T(8,128)(2,1)S(1)}, bf16[512,416]{1,0:T(8,128)(2,1)S(1)}, u32[]{:S(2)}, u32[]{:S(2)}) %collective-permute-start.10) | collective-permute-done | bytes 426016 | tf_op jit(solution)/shard_map/ppermute | solution.py:579
  31.1 0.1 shard_map.117.a
  31.2 0.1 collective-permute-start.11
  31.3 0.9 %shard_map.104 = (f32[22,8,128]{2,1,0:T(8,128)S(1)}, f32[22,8,128]{2,1,0:T(8,128)S(1)}) custom-call(f32[64,32,128]{2,1,0:T(8,128)} %bitcast.9, f32[48,32,128]{2,1,0:T(8,128)} %bitcast.5), custom_call_target="tpu_custom_call" | custom-call | tf_op jit(solution)/shard_map/pallas_call | solution.py:58
  32.2 0.5 collective-permute-start
  32.8 2.2 %collective-permute-start.1 = (f32[22,8,128]{2,1,0:T(8,128)S(1)}, f32[22,8,128]{2,1,0:T(8,128)S(1)}, u32[]{:S(2)}, u32[]{:S(2)}) collective-permute-start(f32[22,8,128]{2,1,0:T(8,128)S(1)} %get-tuple-element.20.my_down), channel_id=1, source_target_pairs={{4,0},{8,4},{12,8},{16,12},{20,16},{24,20},{28,24},{0,28},{5,1},{9... | collective-permute-start | bytes 270344 | tf_op jit(solution)/shard_map/ppermute | solution.py:589
  34.9 0.0 copy-done
  34.9 1.5 %shard_map.106 = (f32[72,128]{1,0:T(8,128)S(1)}, f32[72,128]{1,0:T(8,128)S(1)}) custom-call(f32[64,32,128]{2,1,0:T(8,128)S(1)} %bitcast.10, f32[48,32,128]{2,1,0:T(8,128)S(1)} %bitcast.6), custom_call_target="tpu_custom_call" | custom-call | tf_op jit(solution)/shard_map/pallas_call | solution.py:58
  36.5 0.7 collective-permute-done.b
  37.2 0.0 collective-permute-done.1.a
  37.2 0.1 shard_map.107
  37.3 2.3 %collective-permute-start.2 = (f32[72,128]{1,0:T(8,128)S(1)}, f32[72,128]{1,0:T(8,128)S(1)}, u32[]{:S(2)}, u32[]{:S(2)}) collective-permute-start(f32[72,128]{1,0:T(8,128)S(1)} %get-tuple-element.25.my_east), channel_id=1, source_target_pairs={{0,1},{1,2},{2,3},{3,0},{4,5},{5,6},{6,7},{7,4},{8,9},{9,10},{10,1... | collective-permute-start | bytes 110600 | tf_op jit(solution)/shard_map/ppermute | solution.py:592
  39.6 3.8 %collective-permute-start.3 = (f32[72,128]{1,0:T(8,128)S(1)}, f32[72,128]{1,0:T(8,128)S(1)}, u32[]{:S(2)}, u32[]{:S(2)}) collective-permute-start(f32[72,128]{1,0:T(8,128)S(1)} %get-tuple-element.26.my_west), channel_id=1, source_target_pairs={{1,0},{2,1},{3,2},{0,3},{5,4},{6,5},{7,6},{4,7},{9,8},{10,9},{11,1... | collective-permute-start | bytes 110600 | tf_op jit(solution)/shard_map/ppermute | solution.py:593
  43.4 1.3 %shard_map.105 = (f32[64,48,128]{2,1,0:T(8,128)S(1)}, f32[8,32,128]{2,1,0:T(8,128)S(1)}) custom-call(f32[64,32,128]{2,1,0:T(8,128)S(1)} %bitcast.11, f32[48,32,128]{2,1,0:T(8,128)S(1)} %bitcast.7, f32[22,8,128]{2,1,0:T(8,128)S(1)} %collective-permute-done.b, f32[22,8,128]{2,1,0:T(8,128)S(1)} %collective-permute-done.1.a, ...), custom_call_target="tpu_custom_call" | custom-call | tf_op jit(solution)/shard_map/pallas_call | solution.py:58
  44.7 0.9 %collective-permute-done.2.w_in = f32[72,128]{1,0:T(8,128)S(1)} collective-permute-done((f32[72,128]{1,0:T(8,128)S(1)}, f32[72,128]{1,0:T(8,128)S(1)}, u32[]{:S(2)}, u32[]{:S(2)}) %collective-permute-start.2) | collective-permute-done | bytes 36896 | tf_op jit(solution)/shard_map/ppermute | solution.py:592
  45.6 0.4 collective-permute-done.3.e_in
  46.0 2.7 %shard_map.108 = (f32[64,32,128]{2,1,0:T(8,128)S(1)}, f32[256,128]{1,0:T(8,128)S(1)}, f32[32,128]{1,0:T(8,128)S(1)}) custom-call(f32[64,48,128]{2,1,0:T(8,128)S(1)} %get-tuple-element.21.f1, f32[8,32,128]{2,1,0:T(8,128)S(1)} %get-tuple-element.22.mids, f32[48,32,128]{2,1,0:T(8,128)S(1)} %bitcast.8, f32[72,128]{1,0:T(8,128)S(1)} %collective-permute-done.2.w_in, ...), custom_call_target="tpu_custom_call" | custom-call | tf_op jit(solution)/shard_map/pallas_call | solution.py:58
  48.7 0.0 copy-start.3
  48.7 1.0 %copy-done.3 = f32[64,32,128]{2,1,0:T(8,128)} copy-done((f32[64,32,128]{2,1,0:T(8,128)}, f32[64,32,128]{2,1,0:T(8,128)S(1)}, u32[]{:S(2)}) %copy-start.3) | copy-done | bytes 1048600
  49.7 1.0 %collective-permute-start.4 = (f32[32,128]{1,0:T(8,128)S(1)}, f32[32,128]{1,0:T(8,128)S(1)}, u32[]{:S(2)}, u32[]{:S(2)}) collective-permute-start(f32[32,128]{1,0:T(8,128)S(1)} %get-tuple-element.28.refs_0_), channel_id=1, source_target_pairs={{0,1},{1,0},{2,3},{3,2},{4,5},{5,4},{6,7},{7,6},{8,9},{9,8},{10,11... | collective-permute-start | bytes 49160 | tf_op jit(solution)/shard_map/ppermute | solution.py:602
  50.7 3.0 %collective-permute-start.5 = (f32[32,128]{1,0:T(8,128)S(1)}, f32[32,128]{1,0:T(8,128)S(1)}, u32[]{:S(2)}, u32[]{:S(2)}) collective-permute-start(f32[32,128]{1,0:T(8,128)S(1)} %get-tuple-element.28.refs_0_), channel_id=1, source_target_pairs={{0,2},{1,3},{2,0},{3,1},{4,6},{5,7},{6,4},{7,5},{8,10},{9,11},{10,... | collective-permute-start | bytes 49160 | tf_op jit(solution)/shard_map/ppermute | solution.py:602
  53.7 0.4 collective-permute-start.6
  54.1 1.4 %shard_map.109 = (bf16[256,4096]{1,0:T(8,128)(2,1)S(1)}, bf16[256,192]{1,0:T(8,128)(2,1)S(1)}, f32[32,128]{1,0:T(8,128)S(1)}, f32[32,128]{1,0:T(8,128)S(1)}) custom-call(s32[32,128]{1,0:T(8,128)S(1)} %copy-done.7, f32[32,128]{1,0:T(8,128)S(1)} %copy-done.8, s32[1,32]{1,0:T(1,128)S(1)} %bitcast.12), custom_call_target="tpu_custom_call" | custom-call | tf_op jit(solution)/shard_map/pallas_call | solution.py:58
  55.4 0.9 %shard_map.110.refs_4_ = f32[256,128]{1,0:T(8,128)S(1)} custom-call(f32[256,128]{1,0:T(8,128)S(1)} %get-tuple-element.29.l0, f32[32,128]{1,0:T(8,128)S(1)} %get-tuple-element.30.w, bf16[256,4096]{1,0:T(8,128)(2,1)S(1)} %get-tuple-element.31.hot_ref), custom_call_target="tpu_custom_call" | custom-call | tf_op jit(solution)/shard_map/pallas_call | solution.py:58
  56.4 0.0 collective-permute-done.4.refs_1_
  56.4 0.0 collective-permute-done.5.refs_2_
  56.4 2.9 %collective-permute-done.6.refs_3_ = f32[32,128]{1,0:T(8,128)S(1)} collective-permute-done((f32[32,128]{1,0:T(8,128)S(1)}, f32[32,128]{1,0:T(8,128)S(1)}, u32[]{:S(2)}, u32[]{:S(2)}) %collective-permute-start.6) | collective-permute-done | bytes 16416 | tf_op jit(solution)/shard_map/ppermute | solution.py:602
  59.2 1.0 %shard_map.111 = (f32[32,128]{1,0:T(8,128)S(1)}, f32[32,16,128]{2,1,0:T(8,128)}) custom-call(f32[32,128]{1,0:T(8,128)S(1)} %get-tuple-element.28.refs_0_, f32[32,128]{1,0:T(8,128)S(1)} %collective-permute-done.4.refs_1_, f32[32,128]{1,0:T(8,128)S(1)} %collective-permute-done.5.refs_2_, f32[32,128]{1,0:T(8,128)S(1)} %collective-permute-done.6.refs_3_, ...), custom_call_target="tpu_custom_call" | custom-call | tf_op jit(solution)/shard_map/pallas_call | solution.py:58
  60.3 3.3 %all-to-all-start = ((f32[32,16,128]{2,1,0:T(8,128)}), f32[32,16,128]{2,1,0:T(8,128)}, u32[]{:S(2)}, u32[]{:S(2)}) async-start(f32[32,16,128]{2,1,0:T(8,128)} %get-tuple-element.35), calls=%async_computation | async-start | bytes 524288 | tf_op jit(solution)/shard_map/all_to_all | solution.py:609
  63.6 0.0 copy-start.2
  63.6 1.8 %shard_map.113.hot_ref = bf16[2048,512]{1,0:T(8,128)(2,1)S(1)} custom-call(s32[32,256]{1,0:T(8,128)S(1)} %copy-done.6), custom_call_target="tpu_custom_call" | custom-call | tf_op jit(solution)/shard_map/pallas_call | solution.py:58
  66.1 0.0 copy-start.4
  66.1 1.2 %copy-done.4 = f32[64,32,128]{2,1,0:T(8,128)S(1)} copy-done((f32[64,32,128]{2,1,0:T(8,128)S(1)}, f32[64,32,128]{2,1,0:T(8,128)}, u32[]{:S(2)}) %copy-start.4) | copy-done | bytes 1048600
  67.3 1.5 %shard_map.112 = f32[64,32,128]{2,1,0:T(8,128)} custom-call(f32[64,32,128]{2,1,0:T(8,128)S(1)} %copy-done.4, f32[32,128]{1,0:T(8,128)S(1)} %get-tuple-element.33.z_ref, f32[32,128]{1,0:T(8,128)S(1)} %get-tuple-element.34.h_ref), custom_call_target="tpu_custom_call" | custom-call | tf_op jit(solution)/shard_map/pallas_call | solution.py:58
  68.8 0.0 collective-permute-done.11.b
  68.8 1.8 %shard_map.118.base_ref = f32[64,416]{1,0:T(8,128)S(1)} custom-call(bf16[1024,512]{1,0:T(8,128)(2,1)S(1)} %shard_map.117.a, bf16[1024,512]{1,0:T(8,128)(2,1)} %collective-permute-done.11.b, bf16[64,2048]{1,0:T(8,128)(2,1)S(1)} %copy-done.2), custom_call_target="tpu_custom_call" | custom-call | tf_op jit(solution)/shard_map/pallas_call | solution.py:58
  70.6 3.1 %all-to-all-done = f32[32,16,128]{2,1,0:T(8,128)} async-done(((f32[32,16,128]{2,1,0:T(8,128)}), f32[32,16,128]{2,1,0:T(8,128)}, u32[]{:S(2)}, u32[]{:S(2)}) %all-to-all-start) | async-done | bytes 262176 | tf_op jit(solution)/shard_map/all_to_all | solution.py:609
  73.8 2.6 %shard_map.119 = f32[64,416]{1,0:T(8,128)} custom-call(s32[1]{0:T(128)S(6)} %copy.11.week_ref, f32[512,128]{1,0:T(8,128)} %bitcast.4.s_ref, bf16[2048,512]{1,0:T(8,128)(2,1)S(1)} %shard_map.113.hot_ref, bf16[64,2048]{1,0:T(8,128)(2,1)S(1)} %copy-done.2, f32[64,416]{1,0:T(8,128)S(1)} %shard_map.118.base_ref), custom_call_target="tpu_custom_call" | custom-call | tf_op jit(solution)/shard_map/pallas_call | solution.py:58
  (14 shorter events, 0.1 us)
Async XLA Ops:
  0.6 8.0 %collective-permute-start.7 = (bf16[64,416]{1,0:T(8,128)(2,1)}, bf16[64,416]{1,0:T(8,128)(2,1)S(1)}, u32[]{:S(2)}, u32[]{:S(2)}) collective-permute-start(bf16[64,416]{1,0:T(8,128)(2,1)} %refs_0_.1), channel_id=1, source_target_pairs={{0,2},{1,3},{2,0},{3,1},{4,6},{5,7},{6,4},{7,5},{8,10},{9,11},{10,... | collective-permute-start | bytes 159752 | tf_op jit(solution)/shard_map/ppermute | solution.py:579
  8.6 0.8 %copy-start.5 = (bf16[64,416]{1,0:T(8,128)(2,1)S(1)}, bf16[64,416]{1,0:T(8,128)(2,1)}, u32[]{:S(2)}) copy-start(bf16[64,416]{1,0:T(8,128)(2,1)} %refs_0_.1) | copy-start | bytes 159748
  9.5 5.0 %collective-permute-start.8 = (bf16[128,416]{1,0:T(8,128)(2,1)S(1)}, bf16[128,416]{1,0:T(8,128)(2,1)S(1)}, u32[]{:S(2)}, u32[]{:S(2)}) collective-permute-start(bf16[128,416]{1,0:T(8,128)(2,1)S(1)} %shard_map.114.refs_0_), channel_id=1, source_target_pairs={{0,8},{1,9},{2,10},{3,11},{4,12},{5,13},{6,14},{7,15},{8,0},{9,1},... | collective-permute-start | bytes 319496 | tf_op jit(solution)/shard_map/ppermute | solution.py:579
  14.5 6.4 %collective-permute-start.9 = (bf16[256,416]{1,0:T(8,128)(2,1)S(1)}, bf16[256,416]{1,0:T(8,128)(2,1)S(1)}, u32[]{:S(2)}, u32[]{:S(2)}) collective-permute-start(bf16[256,416]{1,0:T(8,128)(2,1)S(1)} %shard_map.115.refs_0_), channel_id=1, source_target_pairs={{0,1},{1,0},{2,3},{3,2},{4,5},{5,4},{6,7},{7,6},{8,9},{9,8},{10,11... | collective-permute-start | bytes 638984 | tf_op jit(solution)/shard_map/ppermute | solution.py:579
  21.0 13.9 %copy-start = (f32[6,8,32,128]{3,2,1,0:T(8,128)S(1)}, f32[6,8,32,128]{3,2,1,0:T(8,128)}, u32[]{:S(2)}) copy-start(f32[6,8,32,128]{3,2,1,0:T(8,128)} %param.10) | copy-start | bytes 2359300
  21.0 13.9 %copy-start.1 = (f32[8,8,32,128]{3,2,1,0:T(8,128)S(1)}, f32[8,8,32,128]{3,2,1,0:T(8,128)}, u32[]{:S(2)}) copy-start(f32[8,8,32,128]{3,2,1,0:T(8,128)} %param.9) | copy-start | bytes 3145732
  21.0 10.1 %collective-permute-start.10 = (bf16[512,416]{1,0:T(8,128)(2,1)S(1)}, bf16[512,416]{1,0:T(8,128)(2,1)S(1)}, u32[]{:S(2)}, u32[]{:S(2)}) collective-permute-start(bf16[512,416]{1,0:T(8,128)(2,1)S(1)} %shard_map.116.refs_0_), channel_id=1, source_target_pairs={{0,16},{1,17},{2,18},{3,19},{4,20},{5,21},{6,22},{7,23},{8,24},{9,... | collective-permute-start | bytes 1277960 | tf_op jit(solution)/shard_map/ppermute | solution.py:579
  31.2 37.6 %collective-permute-start.11 = (bf16[1024,512]{1,0:T(8,128)(2,1)S(1)}, bf16[1024,512]{1,0:T(8,128)(2,1)}, u32[]{:S(2)}, u32[]{:S(2)}) collective-permute-start(bf16[1024,512]{1,0:T(8,128)(2,1)S(1)} %shard_map.117.a), channel_id=1, source_target_pairs={{0,4},{1,5},{2,6},{3,7},{4,0},{5,1},{6,2},{7,3},{8,12},{9,13},{10,... | collective-permute-start | bytes 3145736 | tf_op jit(solution)/shard_map/ppermute | solution.py:579
  32.2 4.9 %collective-permute-start = (f32[22,8,128]{2,1,0:T(8,128)S(1)}, f32[22,8,128]{2,1,0:T(8,128)S(1)}, u32[]{:S(2)}, u32[]{:S(2)}) collective-permute-start(f32[22,8,128]{2,1,0:T(8,128)S(1)} %get-tuple-element.19.my_up), channel_id=1, source_target_pairs={{0,4},{4,8},{8,12},{12,16},{16,20},{20,24},{24,28},{28,0},{1,5},{5... | collective-permute-start | bytes 270344 | tf_op jit(solution)/shard_map/ppermute | solution.py:588
  32.8 4.4 %collective-permute-start.1 = (f32[22,8,128]{2,1,0:T(8,128)S(1)}, f32[22,8,128]{2,1,0:T(8,128)S(1)}, u32[]{:S(2)}, u32[]{:S(2)}) collective-permute-start(f32[22,8,128]{2,1,0:T(8,128)S(1)} %get-tuple-element.20.my_down), channel_id=1, source_target_pairs={{4,0},{8,4},{12,8},{16,12},{20,16},{24,20},{28,24},{0,28},{5,1},{9... | collective-permute-start | bytes 270344 | tf_op jit(solution)/shard_map/ppermute | solution.py:589
  37.3 8.3 %collective-permute-start.2 = (f32[72,128]{1,0:T(8,128)S(1)}, f32[72,128]{1,0:T(8,128)S(1)}, u32[]{:S(2)}, u32[]{:S(2)}) collective-permute-start(f32[72,128]{1,0:T(8,128)S(1)} %get-tuple-element.25.my_east), channel_id=1, source_target_pairs={{0,1},{1,2},{2,3},{3,0},{4,5},{5,6},{6,7},{7,4},{8,9},{9,10},{10,1... | collective-permute-start | bytes 110600 | tf_op jit(solution)/shard_map/ppermute | solution.py:592
  39.6 14.5 %copy-start.7 = (s32[32,128]{1,0:T(8,128)S(1)}, s32[32,128]{1,0:T(8,128)}, u32[]{:S(2)}) copy-start(s32[32,128]{1,0:T(8,128)} %rl.1) | copy-start | bytes 49156
  39.6 14.5 %copy-start.8 = (f32[32,128]{1,0:T(8,128)S(1)}, f32[32,128]{1,0:T(8,128)}, u32[]{:S(2)}) copy-start(f32[32,128]{1,0:T(8,128)} %w_ref.1) | copy-start | bytes 49156
  39.6 14.5 %copy-start.9 = (s32[32]{0:T(128)S(1)}, s32[32]{0:T(128)}, u32[]{:S(2)}) copy-start(s32[32]{0:T(128)} %param.14) | copy-start | bytes 388
  39.6 6.4 %collective-permute-start.3 = (f32[72,128]{1,0:T(8,128)S(1)}, f32[72,128]{1,0:T(8,128)S(1)}, u32[]{:S(2)}, u32[]{:S(2)}) collective-permute-start(f32[72,128]{1,0:T(8,128)S(1)} %get-tuple-element.26.my_west), channel_id=1, source_target_pairs={{1,0},{2,1},{3,2},{0,3},{5,4},{6,5},{7,6},{4,7},{9,8},{10,9},{11,1... | collective-permute-start | bytes 110600 | tf_op jit(solution)/shard_map/ppermute | solution.py:593
  48.7 1.0 %copy-start.3 = (f32[64,32,128]{2,1,0:T(8,128)}, f32[64,32,128]{2,1,0:T(8,128)S(1)}, u32[]{:S(2)}) copy-start(f32[64,32,128]{2,1,0:T(8,128)S(1)} %get-tuple-element.27.l_ref) | copy-start | bytes 3145732
  49.7 13.9 %copy-start.6 = (s32[32,256]{1,0:T(8,128)S(1)}, s32[32,256]{1,0:T(8,128)}, u32[]{:S(2)}) copy-start(s32[32,256]{1,0:T(8,128)} %tr.1) | copy-start | bytes 98308
  49.7 6.7 %collective-permute-start.4 = (f32[32,128]{1,0:T(8,128)S(1)}, f32[32,128]{1,0:T(8,128)S(1)}, u32[]{:S(2)}, u32[]{:S(2)}) collective-permute-start(f32[32,128]{1,0:T(8,128)S(1)} %get-tuple-element.28.refs_0_), channel_id=1, source_target_pairs={{0,1},{1,0},{2,3},{3,2},{4,5},{5,4},{6,7},{7,6},{8,9},{9,8},{10,11... | collective-permute-start | bytes 49160 | tf_op jit(solution)/shard_map/ppermute | solution.py:602
  50.7 5.7 %collective-permute-start.5 = (f32[32,128]{1,0:T(8,128)S(1)}, f32[32,128]{1,0:T(8,128)S(1)}, u32[]{:S(2)}, u32[]{:S(2)}) collective-permute-start(f32[32,128]{1,0:T(8,128)S(1)} %get-tuple-element.28.refs_0_), channel_id=1, source_target_pairs={{0,2},{1,3},{2,0},{3,1},{4,6},{5,7},{6,4},{7,5},{8,10},{9,11},{10,... | collective-permute-start | bytes 49160 | tf_op jit(solution)/shard_map/ppermute | solution.py:602
  53.7 5.5 %collective-permute-start.6 = (f32[32,128]{1,0:T(8,128)S(1)}, f32[32,128]{1,0:T(8,128)S(1)}, u32[]{:S(2)}, u32[]{:S(2)}) collective-permute-start(f32[32,128]{1,0:T(8,128)S(1)} %get-tuple-element.28.refs_0_), channel_id=1, source_target_pairs={{0,3},{1,2},{2,1},{3,0},{4,7},{5,6},{6,5},{7,4},{8,11},{9,10},{10,... | collective-permute-start | bytes 49160 | tf_op jit(solution)/shard_map/ppermute | solution.py:602
  60.3 13.5 %all-to-all-start = ((f32[32,16,128]{2,1,0:T(8,128)}), f32[32,16,128]{2,1,0:T(8,128)}, u32[]{:S(2)}, u32[]{:S(2)}) async-start(f32[32,16,128]{2,1,0:T(8,128)} %get-tuple-element.35), calls=%async_computation | async-start | bytes 524288 | tf_op jit(solution)/shard_map/all_to_all | solution.py:609
  63.6 5.2 %copy-start.2 = (bf16[64,2048]{1,0:T(8,128)(2,1)S(1)}, bf16[64,2048]{1,0:T(8,128)(2,1)}, u32[]{:S(2)}) copy-start(bf16[64,2048]{1,0:T(8,128)(2,1)} %cov_ref.3) | copy-start | bytes 786436
  66.1 1.2 %copy-start.4 = (f32[64,32,128]{2,1,0:T(8,128)S(1)}, f32[64,32,128]{2,1,0:T(8,128)}, u32[]{:S(2)}) copy-start(f32[64,32,128]{2,1,0:T(8,128)} %copy-done.3) | copy-start | bytes 3145732

commit v5 on v4

--- a/solution.py
+++ b/solution.py
@@ -45,7 +45,7 @@
             out_specs=[VMEM] * len(outs),
             scratch_shapes=list(scratch),
             input_output_aliases=aliases or {},
-            compiler_params=pltpu.CompilerParams(vmem_limit_bytes=own + (6 << 20)),
+            compiler_params=pltpu.CompilerParams(vmem_limit_bytes=own + (own // 2 if own > BIG else 0) + (6 << 20)),
         )
 
         def place(x, spec):
@@ -484,13 +484,13 @@
     return call(body, [(lam.shape, F32)], [VMEM] * 3, keep=False)(lam, zonal, half)[0]
 
 
-def finish(week, sums, hot, cov, base, trc):
+def finish(week, sums, hot, cov, base, more, trc):
     own_rows, _ = cov.shape
     cols = base.shape[1]
     width = sums.shape[1]
     span = LANES // trc * LANES
 
-    def body(week_ref, s_ref, hot_ref, cov_ref, base_ref, out):
+    def body(week_ref, s_ref, hot_ref, cov_ref, base_ref, more_ref, out):
         added = jnp.zeros((own_rows, LANES), F32)
         for c in range(0, width, LANES):
             parts = [x.astype(BF16) for x in split3(jnp.transpose(s_ref[:, pl.ds(c, LANES)]))]
@@ -511,10 +511,10 @@
         for c in range(0, cols, LANES):
             w = min(LANES, cols - c)
             here = (c + iota((own_rows, LANES), 1)) // trc == week_ref[0]
-            out[:, pl.ds(c, w)] = base_ref[:, pl.ds(c, w)] + jnp.where(here, added, 0.0)[:, :w]
-
-    return call(body, [((own_rows, cols), F32)], [SMEM] + [VMEM] * 4, keep=False)(
-        week, sums, hot, cov, base)[0]
+            out[:, pl.ds(c, w)] = base_ref[:, pl.ds(c, w)] + more_ref[:, pl.ds(c, w)] + jnp.where(here, added, 0.0)[:, :w]
+
+    return call(body, [((own_rows, cols), F32)], [SMEM] + [VMEM] * 5, keep=False)(
+        week, sums, hot, cov, base, more)[0]
 
 
 def ring(size):
@@ -542,22 +542,41 @@
     return call(body, [((rows, cols), parts[0].dtype)], [VMEM] * len(parts))(*parts)[0]
 
 
-def base_product(mine, theirs, cov, turn, cols):
+def upper_half():
+    tile = lax.axis_index("lat") * lax.axis_size("lon") + lax.axis_index("lon")
+    return tile // (lax.axis_size("lat") * lax.axis_size("lon") // 2)
+
+
+def far_columns(cov):
+    own_rows, regions = cov.shape
+    half = regions // 2
+
+    def body(cov_ref, out):
+        out[...] = cov_ref[:, pl.ds(pl.multiple_of((1 - upper_half()) * half, half), half)]
+
+    return call(body, [((own_rows, half), cov.dtype)], [VMEM])(cov)[0]
+
+
+def base_product(mine, theirs, cov, far, turn, cols):
     own_rows, regions = cov.shape
     wide = mine.shape[1]
-    half = len(turn) // 2
-
-    def body(a, b, cov_ref, out, grad):
+    half = regions // 2
+    count = len(turn)
+
+    def body(a, b, cov_ref, far_ref, out, other, grad):
         tile = lax.axis_index("lat") * lax.axis_size("lon") + lax.axis_index("lon")
         for j, flip in enumerate(turn):
-            src = a if j < half else b
-            at = pl.multiple_of((tile ^ flip) * own_rows, own_rows)
-            grad[pl.ds(at, own_rows), :] = src[pl.ds(j % half * own_rows, own_rows), :]
-        out[...] = jnp.dot(cov_ref[...], grad[...], preferred_element_type=F32)[:, :cols]
+            src = a if j < count // 2 else b
+            at = pl.multiple_of(((tile ^ flip) & (count - 1)) * own_rows, own_rows)
+            grad[pl.ds(at, own_rows), :] = src[pl.ds(j % (count // 2) * own_rows, own_rows), :]
+        near = cov_ref[:, pl.ds(pl.multiple_of(upper_half() * half, half), half)]
+        both = jnp.dot(jnp.concatenate([near, far_ref[...]], axis=0), grad[...], preferred_element_type=F32)
+        out[...] = both[:own_rows, :cols]
+        other[...] = both[own_rows:, :cols]
 
     return call(
-        body, [((own_rows, cols), F32)], [VMEM] * 3, [pltpu.VMEM((regions, wide), cov.dtype)]
-    )(mine, theirs, cov)[0]
+        body, [((own_rows, cols), F32)] * 2, [VMEM] * 4, [pltpu.VMEM((half, wide), cov.dtype)]
+    )(mine, theirs, cov, far)
 
 
 def shards(adjoint, transport_rates, cell_weight, region_local, tile_regions, polar_rows, week_index, grad_in, covariance):
@@ -570,7 +589,8 @@
 
     lon_bits, bits = lons.bit_length() - 1, devices.bit_length() - 1
     far = list(range(lon_bits + 1, bits))
-    order = list(range(lon_bits - 1, 0, -1)) + far[:1] + [0] + far[1:] + [lon_bits]
+    order = list(range(lon_bits - 1, 0, -1)) + far[:1] + [0] + far[1:-1] + [lon_bits]
+    top = partners(devices, devices // 2)
     turn = [0]
     for bit in order:
         turn = turn + [j ^ (1 << bit) for j in turn]
@@ -609,8 +629,10 @@
     sums = lax.all_to_all(copies, AXES, 0, 0, tiled=True)
     sums = sums.reshape(-1, sums.shape[2])
     adjoint_out = filtered(lam, zonal, half, trc, lev).reshape(adjoint.shape)
-    base = base_product(have, theirs, covariance, turn, grad_in.shape[1])
-    precond = finish(week_index, sums, where, covariance, base, trc)
+    far_cov = lax.ppermute(far_columns(covariance), AXES, top)
+    base, other = base_product(have, theirs, covariance, far_cov, turn, grad_in.shape[1])
+    more = lax.ppermute(other, AXES, top)
+    precond = finish(week_index, sums, where, covariance, base, more, trc)
     return adjoint_out, precond
 
 

time: 76.8 us -> 62.1 us (0.81)
  waiting for transfers between devices: 29.1 us -> 18.9 us
  Pallas kernels: 17.8 us -> 15.3 us
  local copies, waits for them, and re-layouts: 3.06 us -> 1.84 us
  starting transfers between devices: 25 us -> 24.2 us
    ppermute x5 -> x4, waiting for transfers between devices: 21.1 us -> 9.18 us  [exchange(): return lax.ppermute(x, AXES, partners(devices, 1 << order[i]))]
    ppermute x0 -> x2, waiting for transfers between devices: none -> 5.87 us  [the longest x1 5.87 us: shards(): far_cov = lax.ppermute(far_columns(covariance), AXES, top)]
    ppermute x0 -> x2, starting transfers between devices: none -> 3.28 us  [the longest x1 1.83 us: shards(): far_cov = lax.ppermute(far_columns(covariance), AXES, top)]
    all_to_all x1, waiting for transfers between devices: 3.14 us -> 0.01 us  [shards(): sums = lax.all_to_all(copies, AXES, 0, 0, tiled=True)]
    pallas_call x16, Pallas kernels: 17.8 us -> 15.3 us  [apply(): return run(*(place(x, spec) for x, spec in zip(args, in_specs)))]
    ppermute x5 -> x4, starting transfers between devices: 8.5 us -> 6.7 us  [exchange(): return lax.ppermute(x, AXES, partners(devices, 1 << order[i]))]
    ppermute x1, starting transfers between devices: 2.31 us -> 0.96 us  [shards(): w_in = lax.ppermute(east, 'lon', east_to)]
    unnamed x20, local copies, waits for them, and re-layouts: 3.06 us -> 1.84 us
  transfers between devices with their start and end apart: 13 -> 14, of which waited for: 9 -> 6; matrix products, arithmetic and copies ran while one was open for 0% -> 0% of each run, Pallas kernels for 20% -> 22%
where the time goes in v5:
time: 62.1 us; the launch traced here: 61.8 us
  starting transfers between devices  24.2 us (39%)
  waiting for transfers between devices  18.9 us (30%)
  Pallas kernels  15.3 us (25%)
  local copies, waits for them, and re-layouts  1.84 us (3%)
  between operations  1.49 us (2%)
    pallas_call x16, Pallas kernels, apply(): return run(*(place(x, spec) for x, spec in zip(args, in_specs)))  15.3 us
    ppermute x4, waiting for transfers between devices, exchange(): return lax.ppermute(x, AXES, partners(devices, 1 << order[i]))  9.18 us
    ppermute x4, starting transfers between devices, exchange(): return lax.ppermute(x, AXES, partners(devices, 1 << order[i]))  6.7 us
    ppermute x1, waiting for transfers between devices, shards(): far_cov = lax.ppermute(far_columns(covariance), AXES, top)  5.87 us
    ppermute x3, starting transfers between devices, shards(): lax.ppermute(row_sums, 'lon', partners(lons, k))  4.39 us
    ppermute x1, starting transfers between devices, shards(): e_in = lax.ppermute(west, 'lon', west_to)  3.36 us
    ppermute x3, waiting for transfers between devices, shards(): lax.ppermute(row_sums, 'lon', partners(lons, k))  3.09 us
    all_to_all x1, starting transfers between devices, shards(): sums = lax.all_to_all(copies, AXES, 0, 0, tiled=True)  2.85 us
  transfers between devices with their start and end apart: 14, of which 6 were waited for; matrix products, arithmetic and copies ran while one was open for 0% of the time, Pallas kernels for 22%

profile of v5, /device:TPU:0, one launch (start us, length us, event | category | flops | bytes accessed | tf_op | source)
XLA Modules:
  0.0 61.8 jit_solution(11817690844675554518)
XLA Ops:
  0.6 0.0 copy-start
  0.6 0.0 copy-start.1
  0.7 4.1 %collective-permute-start.7 = (bf16[64,416]{1,0:T(8,128)(2,1)}, bf16[64,416]{1,0:T(8,128)(2,1)S(1)}, u32[]{:S(2)}, u32[]{:S(2)}) collective-permute-start(bf16[64,416]{1,0:T(8,128)(2,1)} %refs_0_.1), channel_id=1, source_target_pairs={{0,2},{1,3},{2,0},{3,1},{4,6},{5,7},{6,4},{7,5},{8,10},{9,11},{10,... | collective-permute-start | bytes 159752 | tf_op jit(solution)/shard_map/ppermute | solution.py:599
  4.8 3.9 %collective-permute-done.7.refs_1_ = bf16[64,416]{1,0:T(8,128)(2,1)S(1)} collective-permute-done((bf16[64,416]{1,0:T(8,128)(2,1)}, bf16[64,416]{1,0:T(8,128)(2,1)S(1)}, u32[]{:S(2)}, u32[]{:S(2)}) %collective-permute-start.7) | collective-permute-done | bytes 53280 | tf_op jit(solution)/shard_map/ppermute | solution.py:599
  8.6 0.8 %copy-done.5 = bf16[64,416]{1,0:T(8,128)(2,1)S(1)} copy-done((bf16[64,416]{1,0:T(8,128)(2,1)S(1)}, bf16[64,416]{1,0:T(8,128)(2,1)}, u32[]{:S(2)}) %copy-start.5) | copy-done | bytes 53272
  9.5 1.8 %collective-permute-start.8 = (bf16[128,416]{1,0:T(8,128)(2,1)S(1)}, bf16[128,416]{1,0:T(8,128)(2,1)S(1)}, u32[]{:S(2)}, u32[]{:S(2)}) collective-permute-start(bf16[128,416]{1,0:T(8,128)(2,1)S(1)} %shard_map.114.refs_0_), channel_id=1, source_target_pairs={{0,8},{1,9},{2,10},{3,11},{4,12},{5,13},{6,14},{7,15},{8,0},{9,1},... | collective-permute-start | bytes 319496 | tf_op jit(solution)/shard_map/ppermute | solution.py:599
  11.3 3.3 %collective-permute-done.8.refs_1_ = bf16[128,416]{1,0:T(8,128)(2,1)S(1)} collective-permute-done((bf16[128,416]{1,0:T(8,128)(2,1)S(1)}, bf16[128,416]{1,0:T(8,128)(2,1)S(1)}, u32[]{:S(2)}, u32[]{:S(2)}) %collective-permute-start.8) | collective-permute-done | bytes 106528 | tf_op jit(solution)/shard_map/ppermute | solution.py:599
  14.6 0.7 %collective-permute-start.9 = (bf16[256,416]{1,0:T(8,128)(2,1)S(1)}, bf16[256,416]{1,0:T(8,128)(2,1)S(1)}, u32[]{:S(2)}, u32[]{:S(2)}) collective-permute-start(bf16[256,416]{1,0:T(8,128)(2,1)S(1)} %shard_map.115.refs_0_), channel_id=1, source_target_pairs={{0,1},{1,0},{2,3},{3,2},{4,5},{5,4},{6,7},{7,6},{8,9},{9,8},{10,11... | collective-permute-start | bytes 638984 | tf_op jit(solution)/shard_map/ppermute | solution.py:599
  15.3 0.9 %shard_map.104 = (f32[22,8,128]{2,1,0:T(8,128)S(1)}, f32[22,8,128]{2,1,0:T(8,128)S(1)}) custom-call(f32[64,32,128]{2,1,0:T(8,128)} %bitcast.9, f32[48,32,128]{2,1,0:T(8,128)} %bitcast.5), custom_call_target="tpu_custom_call" | custom-call | tf_op jit(solution)/shard_map/pallas_call | solution.py:58
  16.2 0.1 collective-permute-start
  16.3 2.6 %collective-permute-start.1 = (f32[22,8,128]{2,1,0:T(8,128)S(1)}, f32[22,8,128]{2,1,0:T(8,128)S(1)}, u32[]{:S(2)}, u32[]{:S(2)}) collective-permute-start(f32[22,8,128]{2,1,0:T(8,128)S(1)} %get-tuple-element.22.my_down), channel_id=1, source_target_pairs={{4,0},{8,4},{12,8},{16,12},{20,16},{24,20},{28,24},{0,28},{5,1},{9... | collective-permute-start | bytes 270344 | tf_op jit(solution)/shard_map/ppermute | solution.py:609
  18.9 2.1 %collective-permute-done.9.refs_1_ = bf16[256,416]{1,0:T(8,128)(2,1)S(1)} collective-permute-done((bf16[256,416]{1,0:T(8,128)(2,1)S(1)}, bf16[256,416]{1,0:T(8,128)(2,1)S(1)}, u32[]{:S(2)}, u32[]{:S(2)}) %collective-permute-start.9) | collective-permute-done | bytes 213024 | tf_op jit(solution)/shard_map/ppermute | solution.py:599
  21.0 0.1 shard_map.116.a
  21.0 0.1 collective-permute-start.10
  21.1 1.5 %shard_map.106 = (f32[72,128]{1,0:T(8,128)S(1)}, f32[72,128]{1,0:T(8,128)S(1)}) custom-call(f32[64,32,128]{2,1,0:T(8,128)S(1)} %bitcast.10, f32[48,32,128]{2,1,0:T(8,128)S(1)} %bitcast.6), custom_call_target="tpu_custom_call" | custom-call | tf_op jit(solution)/shard_map/pallas_call | solution.py:58
  22.7 0.0 collective-permute-done.b
  22.7 0.0 collective-permute-done.1.a
  22.7 0.1 shard_map.107
  22.8 1.0 %collective-permute-start.2 = (f32[72,128]{1,0:T(8,128)S(1)}, f32[72,128]{1,0:T(8,128)S(1)}, u32[]{:S(2)}, u32[]{:S(2)}) collective-permute-start(f32[72,128]{1,0:T(8,128)S(1)} %get-tuple-element.27.my_east), channel_id=1, source_target_pairs={{0,1},{1,2},{2,3},{3,0},{4,5},{5,6},{6,7},{7,4},{8,9},{9,10},{10,1... | collective-permute-start | bytes 110600 | tf_op jit(solution)/shard_map/ppermute | solution.py:612
  23.8 3.4 %collective-permute-start.3 = (f32[72,128]{1,0:T(8,128)S(1)}, f32[72,128]{1,0:T(8,128)S(1)}, u32[]{:S(2)}, u32[]{:S(2)}) collective-permute-start(f32[72,128]{1,0:T(8,128)S(1)} %get-tuple-element.28.my_west), channel_id=1, source_target_pairs={{1,0},{2,1},{3,2},{0,3},{5,4},{6,5},{7,6},{4,7},{9,8},{10,9},{11,1... | collective-permute-start | bytes 110600 | tf_op jit(solution)/shard_map/ppermute | solution.py:613
  27.2 1.3 %shard_map.105 = (f32[64,48,128]{2,1,0:T(8,128)S(1)}, f32[8,32,128]{2,1,0:T(8,128)S(1)}) custom-call(f32[64,32,128]{2,1,0:T(8,128)S(1)} %bitcast.11, f32[48,32,128]{2,1,0:T(8,128)S(1)} %bitcast.7, f32[22,8,128]{2,1,0:T(8,128)S(1)} %collective-permute-done.b, f32[22,8,128]{2,1,0:T(8,128)S(1)} %collective-permute-done.1.a, ...), custom_call_target="tpu_custom_call" | custom-call | tf_op jit(solution)/shard_map/pallas_call | solution.py:58
  28.4 0.8 %collective-permute-done.2.w_in = f32[72,128]{1,0:T(8,128)S(1)} collective-permute-done((f32[72,128]{1,0:T(8,128)S(1)}, f32[72,128]{1,0:T(8,128)S(1)}, u32[]{:S(2)}, u32[]{:S(2)}) %collective-permute-start.2) | collective-permute-done | bytes 36896 | tf_op jit(solution)/shard_map/ppermute | solution.py:612
  29.2 0.0 collective-permute-done.3.e_in
  29.2 2.7 %shard_map.108 = (f32[64,32,128]{2,1,0:T(8,128)S(1)}, f32[256,128]{1,0:T(8,128)S(1)}, f32[32,128]{1,0:T(8,128)S(1)}) custom-call(f32[64,48,128]{2,1,0:T(8,128)S(1)} %get-tuple-element.23.f1, f32[8,32,128]{2,1,0:T(8,128)S(1)} %get-tuple-element.24.mids, f32[48,32,128]{2,1,0:T(8,128)S(1)} %bitcast.8, f32[72,128]{1,0:T(8,128)S(1)} %collective-permute-done.2.w_in, ...), custom_call_target="tpu_custom_call" | custom-call | tf_op jit(solution)/shard_map/pallas_call | solution.py:58
  32.0 0.0 copy-start.3
  32.0 1.0 %copy-done.3 = f32[64,32,128]{2,1,0:T(8,128)} copy-done((f32[64,32,128]{2,1,0:T(8,128)}, f32[64,32,128]{2,1,0:T(8,128)S(1)}, u32[]{:S(2)}) %copy-start.3) | copy-done | bytes 1048600
  32.9 1.3 %collective-permute-start.4 = (f32[32,128]{1,0:T(8,128)S(1)}, f32[32,128]{1,0:T(8,128)S(1)}, u32[]{:S(2)}, u32[]{:S(2)}) collective-permute-start(f32[32,128]{1,0:T(8,128)S(1)} %get-tuple-element.30.refs_0_), channel_id=1, source_target_pairs={{0,1},{1,0},{2,3},{3,2},{4,5},{5,4},{6,7},{7,6},{8,9},{9,8},{10,11... | collective-permute-start | bytes 49160 | tf_op jit(solution)/shard_map/ppermute | solution.py:622
  34.2 2.9 %collective-permute-start.5 = (f32[32,128]{1,0:T(8,128)S(1)}, f32[32,128]{1,0:T(8,128)S(1)}, u32[]{:S(2)}, u32[]{:S(2)}) collective-permute-start(f32[32,128]{1,0:T(8,128)S(1)} %get-tuple-element.30.refs_0_), channel_id=1, source_target_pairs={{0,2},{1,3},{2,0},{3,1},{4,6},{5,7},{6,4},{7,5},{8,10},{9,11},{10,... | collective-permute-start | bytes 49160 | tf_op jit(solution)/shard_map/ppermute | solution.py:622
  37.2 0.1 collective-permute-start.6
  37.3 1.4 %shard_map.109 = (bf16[256,4096]{1,0:T(8,128)(2,1)S(1)}, bf16[256,192]{1,0:T(8,128)(2,1)S(1)}, f32[32,128]{1,0:T(8,128)S(1)}, f32[32,128]{1,0:T(8,128)S(1)}) custom-call(s32[32,128]{1,0:T(8,128)S(1)} %copy-done.7, f32[32,128]{1,0:T(8,128)S(1)} %copy-done.8, s32[1,32]{1,0:T(1,128)S(1)} %bitcast.13), custom_call_target="tpu_custom_call" | custom-call | tf_op jit(solution)/shard_map/pallas_call | solution.py:58
  38.7 0.0 copy-start.6
  38.7 0.9 %shard_map.110.refs_4_ = f32[256,128]{1,0:T(8,128)S(1)} custom-call(f32[256,128]{1,0:T(8,128)S(1)} %get-tuple-element.31.l0, f32[32,128]{1,0:T(8,128)S(1)} %get-tuple-element.32.w, bf16[256,4096]{1,0:T(8,128)(2,1)S(1)} %get-tuple-element.33.hot_ref), custom_call_target="tpu_custom_call" | custom-call | tf_op jit(solution)/shard_map/pallas_call | solution.py:58
  39.6 0.0 collective-permute-done.4.refs_1_
  39.6 0.0 collective-permute-done.5.refs_2_
  39.6 3.1 %collective-permute-done.6.refs_3_ = f32[32,128]{1,0:T(8,128)S(1)} collective-permute-done((f32[32,128]{1,0:T(8,128)S(1)}, f32[32,128]{1,0:T(8,128)S(1)}, u32[]{:S(2)}, u32[]{:S(2)}) %collective-permute-start.6) | collective-permute-done | bytes 16416 | tf_op jit(solution)/shard_map/ppermute | solution.py:622
  42.7 1.0 %shard_map.111 = (f32[32,128]{1,0:T(8,128)S(1)}, f32[32,16,128]{2,1,0:T(8,128)}) custom-call(f32[32,128]{1,0:T(8,128)S(1)} %get-tuple-element.30.refs_0_, f32[32,128]{1,0:T(8,128)S(1)} %collective-permute-done.4.refs_1_, f32[32,128]{1,0:T(8,128)S(1)} %collective-permute-done.5.refs_2_, f32[32,128]{1,0:T(8,128)S(1)} %collective-permute-done.6.refs_3_, ...), custom_call_target="tpu_custom_call" | custom-call | tf_op jit(solution)/shard_map/pallas_call | solution.py:58
  43.7 2.9 %all-to-all-start = ((f32[32,16,128]{2,1,0:T(8,128)}), f32[32,16,128]{2,1,0:T(8,128)S(1)}, u32[]{:S(2)}, u32[]{:S(2)}) async-start(f32[32,16,128]{2,1,0:T(8,128)} %get-tuple-element.37), calls=%async_computation | async-start | bytes 524288 | tf_op jit(solution)/shard_map/all_to_all | solution.py:629
  46.6 0.0 copy-start.4
  46.7 1.8 %collective-permute-start.11 = (bf16[64,1024]{1,0:T(8,128)(2,1)S(1)}, bf16[64,1024]{1,0:T(8,128)(2,1)S(1)}, u32[]{:S(2)}, u32[]{:S(2)}) collective-permute-start(bf16[64,1024]{1,0:T(8,128)(2,1)S(1)} %shard_map.117), channel_id=1, source_target_pairs={{0,16},{1,17},{2,18},{3,19},{4,20},{5,21},{6,22},{7,23},{8,24},{9,... | collective-permute-start | bytes 393224 | tf_op jit(solution)/shard_map/ppermute | solution.py:632
  48.5 5.9 %collective-permute-done.11.far_ref = bf16[64,1024]{1,0:T(8,128)(2,1)S(1)} collective-permute-done((bf16[64,1024]{1,0:T(8,128)(2,1)S(1)}, bf16[64,1024]{1,0:T(8,128)(2,1)S(1)}, u32[]{:S(2)}, u32[]{:S(2)}) %collective-permute-start.11) | collective-permute-done | bytes 131104 | tf_op jit(solution)/shard_map/ppermute | solution.py:632
  54.4 0.0 collective-permute-done.10.b
  54.4 0.4 shard_map.118
  54.8 1.4 %collective-permute-start.12 = (f32[64,416]{1,0:T(8,128)S(1)}, f32[64,416]{1,0:T(8,128)S(1)}, u32[]{:S(2)}, u32[]{:S(2)}) collective-permute-start(f32[64,416]{1,0:T(8,128)S(1)} %get-tuple-element.39), channel_id=1, source_target_pairs={{0,16},{1,17},{2,18},{3,19},{4,20},{5,21},{6,22},{7,23},{8,24},{9,... | collective-permute-start | bytes 319496 | tf_op jit(solution)/shard_map/ppermute | solution.py:634
  56.2 1.8 %shard_map.113.hot_ref = bf16[2048,512]{1,0:T(8,128)(2,1)S(1)} custom-call(s32[32,256]{1,0:T(8,128)S(1)} %copy-done.6), custom_call_target="tpu_custom_call" | custom-call | tf_op jit(solution)/shard_map/pallas_call | solution.py:58
  58.7 1.5 %shard_map.112 = f32[64,32,128]{2,1,0:T(8,128)} custom-call(f32[64,32,128]{2,1,0:T(8,128)S(1)} %copy-done.4, f32[32,128]{1,0:T(8,128)S(1)} %get-tuple-element.35.z_ref, f32[32,128]{1,0:T(8,128)S(1)} %get-tuple-element.36.h_ref), custom_call_target="tpu_custom_call" | custom-call | tf_op jit(solution)/shard_map/pallas_call | solution.py:58
  60.2 0.0 all-to-all-done
  60.2 0.0 collective-permute-done.12.more_ref
  60.2 1.7 %shard_map.119 = f32[64,416]{1,0:T(8,128)} custom-call(s32[1]{0:T(128)S(6)} %copy.11.week_ref, f32[512,128]{1,0:T(8,128)S(1)} %bitcast.12, bf16[2048,512]{1,0:T(8,128)(2,1)S(1)} %shard_map.113.hot_ref, bf16[64,2048]{1,0:T(8,128)(2,1)S(1)} %copy-done.2, f32[64,416]{1,0:T(8,128)S(1)} %get-tuple-element.38.base_ref, f32[64,416]{1,0:T(8,128)S(1)} %collective-permute-done.12.more_ref), custom_call_target="tpu_custom_call" | custom-call | tf_op jit(solution)/shard_map/pallas_call | solution.py:58
  (16 shorter events, 0.1 us)
Async XLA Ops:
  0.6 20.5 %copy-start = (f32[6,8,32,128]{3,2,1,0:T(8,128)S(1)}, f32[6,8,32,128]{3,2,1,0:T(8,128)}, u32[]{:S(2)}) copy-start(f32[6,8,32,128]{3,2,1,0:T(8,128)} %param.10) | copy-start | bytes 2359300
  0.6 20.5 %copy-start.1 = (f32[8,8,32,128]{3,2,1,0:T(8,128)S(1)}, f32[8,8,32,128]{3,2,1,0:T(8,128)}, u32[]{:S(2)}) copy-start(f32[8,8,32,128]{3,2,1,0:T(8,128)} %param.9) | copy-start | bytes 3145732
  0.7 8.0 %collective-permute-start.7 = (bf16[64,416]{1,0:T(8,128)(2,1)}, bf16[64,416]{1,0:T(8,128)(2,1)S(1)}, u32[]{:S(2)}, u32[]{:S(2)}) collective-permute-start(bf16[64,416]{1,0:T(8,128)(2,1)} %refs_0_.1), channel_id=1, source_target_pairs={{0,2},{1,3},{2,0},{3,1},{4,6},{5,7},{6,4},{7,5},{8,10},{9,11},{10,... | collective-permute-start | bytes 159752 | tf_op jit(solution)/shard_map/ppermute | solution.py:599
  8.6 0.8 %copy-start.5 = (bf16[64,416]{1,0:T(8,128)(2,1)S(1)}, bf16[64,416]{1,0:T(8,128)(2,1)}, u32[]{:S(2)}) copy-start(bf16[64,416]{1,0:T(8,128)(2,1)} %refs_0_.1) | copy-start | bytes 159748
  9.5 5.0 %collective-permute-start.8 = (bf16[128,416]{1,0:T(8,128)(2,1)S(1)}, bf16[128,416]{1,0:T(8,128)(2,1)S(1)}, u32[]{:S(2)}, u32[]{:S(2)}) collective-permute-start(bf16[128,416]{1,0:T(8,128)(2,1)S(1)} %shard_map.114.refs_0_), channel_id=1, source_target_pairs={{0,8},{1,9},{2,10},{3,11},{4,12},{5,13},{6,14},{7,15},{8,0},{9,1},... | collective-permute-start | bytes 319496 | tf_op jit(solution)/shard_map/ppermute | solution.py:599
  14.6 6.4 %collective-permute-start.9 = (bf16[256,416]{1,0:T(8,128)(2,1)S(1)}, bf16[256,416]{1,0:T(8,128)(2,1)S(1)}, u32[]{:S(2)}, u32[]{:S(2)}) collective-permute-start(bf16[256,416]{1,0:T(8,128)(2,1)S(1)} %shard_map.115.refs_0_), channel_id=1, source_target_pairs={{0,1},{1,0},{2,3},{3,2},{4,5},{5,4},{6,7},{7,6},{8,9},{9,8},{10,11... | collective-permute-start | bytes 638984 | tf_op jit(solution)/shard_map/ppermute | solution.py:599
  16.2 6.4 %collective-permute-start = (f32[22,8,128]{2,1,0:T(8,128)S(1)}, f32[22,8,128]{2,1,0:T(8,128)S(1)}, u32[]{:S(2)}, u32[]{:S(2)}) collective-permute-start(f32[22,8,128]{2,1,0:T(8,128)S(1)} %get-tuple-element.21.my_up), channel_id=1, source_target_pairs={{0,4},{4,8},{8,12},{12,16},{16,20},{20,24},{24,28},{28,0},{1,5},{5... | collective-permute-start | bytes 270344 | tf_op jit(solution)/shard_map/ppermute | solution.py:608
  16.3 6.4 %collective-permute-start.1 = (f32[22,8,128]{2,1,0:T(8,128)S(1)}, f32[22,8,128]{2,1,0:T(8,128)S(1)}, u32[]{:S(2)}, u32[]{:S(2)}) collective-permute-start(f32[22,8,128]{2,1,0:T(8,128)S(1)} %get-tuple-element.22.my_down), channel_id=1, source_target_pairs={{4,0},{8,4},{12,8},{16,12},{20,16},{24,20},{28,24},{0,28},{5,1},{9... | collective-permute-start | bytes 270344 | tf_op jit(solution)/shard_map/ppermute | solution.py:609
  21.0 33.3 %collective-permute-start.10 = (bf16[512,512]{1,0:T(8,128)(2,1)S(1)}, bf16[512,512]{1,0:T(8,128)(2,1)S(1)}, u32[]{:S(2)}, u32[]{:S(2)}) collective-permute-start(bf16[512,512]{1,0:T(8,128)(2,1)S(1)} %shard_map.116.a), channel_id=1, source_target_pairs={{0,4},{1,5},{2,6},{3,7},{4,0},{5,1},{6,2},{7,3},{8,12},{9,13},{10,... | collective-permute-start | bytes 1572872 | tf_op jit(solution)/shard_map/ppermute | solution.py:599
  22.8 6.4 %collective-permute-start.2 = (f32[72,128]{1,0:T(8,128)S(1)}, f32[72,128]{1,0:T(8,128)S(1)}, u32[]{:S(2)}, u32[]{:S(2)}) collective-permute-start(f32[72,128]{1,0:T(8,128)S(1)} %get-tuple-element.27.my_east), channel_id=1, source_target_pairs={{0,1},{1,2},{2,3},{3,0},{4,5},{5,6},{6,7},{7,4},{8,9},{9,10},{10,1... | collective-permute-start | bytes 110600 | tf_op jit(solution)/shard_map/ppermute | solution.py:612
  23.8 13.5 %copy-start.7 = (s32[32,128]{1,0:T(8,128)S(1)}, s32[32,128]{1,0:T(8,128)}, u32[]{:S(2)}) copy-start(s32[32,128]{1,0:T(8,128)} %rl.1) | copy-start | bytes 49156
  23.8 13.5 %copy-start.8 = (f32[32,128]{1,0:T(8,128)S(1)}, f32[32,128]{1,0:T(8,128)}, u32[]{:S(2)}) copy-start(f32[32,128]{1,0:T(8,128)} %w_ref.1) | copy-start | bytes 49156
  23.8 13.5 %copy-start.9 = (s32[32]{0:T(128)S(1)}, s32[32]{0:T(128)}, u32[]{:S(2)}) copy-start(s32[32]{0:T(128)} %param.14) | copy-start | bytes 388
  23.8 5.4 %collective-permute-start.3 = (f32[72,128]{1,0:T(8,128)S(1)}, f32[72,128]{1,0:T(8,128)S(1)}, u32[]{:S(2)}, u32[]{:S(2)}) collective-permute-start(f32[72,128]{1,0:T(8,128)S(1)} %get-tuple-element.28.my_west), channel_id=1, source_target_pairs={{1,0},{2,1},{3,2},{0,3},{5,4},{6,5},{7,6},{4,7},{9,8},{10,9},{11,1... | collective-permute-start | bytes 110600 | tf_op jit(solution)/shard_map/ppermute | solution.py:613
  32.0 1.0 %copy-start.3 = (f32[64,32,128]{2,1,0:T(8,128)}, f32[64,32,128]{2,1,0:T(8,128)S(1)}, u32[]{:S(2)}) copy-start(f32[64,32,128]{2,1,0:T(8,128)S(1)} %get-tuple-element.29.l_ref) | copy-start | bytes 3145732
  32.9 13.7 %copy-start.2 = (bf16[64,2048]{1,0:T(8,128)(2,1)S(1)}, bf16[64,2048]{1,0:T(8,128)(2,1)}, u32[]{:S(2)}) copy-start(bf16[64,2048]{1,0:T(8,128)(2,1)} %cov_ref.5) | copy-start | bytes 786436
  32.9 6.7 %collective-permute-start.4 = (f32[32,128]{1,0:T(8,128)S(1)}, f32[32,128]{1,0:T(8,128)S(1)}, u32[]{:S(2)}, u32[]{:S(2)}) collective-permute-start(f32[32,128]{1,0:T(8,128)S(1)} %get-tuple-element.30.refs_0_), channel_id=1, source_target_pairs={{0,1},{1,0},{2,3},{3,2},{4,5},{5,4},{6,7},{7,6},{8,9},{9,8},{10,11... | collective-permute-start | bytes 49160 | tf_op jit(solution)/shard_map/ppermute | solution.py:622
  34.2 5.4 %collective-permute-start.5 = (f32[32,128]{1,0:T(8,128)S(1)}, f32[32,128]{1,0:T(8,128)S(1)}, u32[]{:S(2)}, u32[]{:S(2)}) collective-permute-start(f32[32,128]{1,0:T(8,128)S(1)} %get-tuple-element.30.refs_0_), channel_id=1, source_target_pairs={{0,2},{1,3},{2,0},{3,1},{4,6},{5,7},{6,4},{7,5},{8,10},{9,11},{10,... | collective-permute-start | bytes 49160 | tf_op jit(solution)/shard_map/ppermute | solution.py:622
  37.2 5.5 %collective-permute-start.6 = (f32[32,128]{1,0:T(8,128)S(1)}, f32[32,128]{1,0:T(8,128)S(1)}, u32[]{:S(2)}, u32[]{:S(2)}) collective-permute-start(f32[32,128]{1,0:T(8,128)S(1)} %get-tuple-element.30.refs_0_), channel_id=1, source_target_pairs={{0,3},{1,2},{2,1},{3,0},{4,7},{5,6},{6,5},{7,4},{8,11},{9,10},{10,... | collective-permute-start | bytes 49160 | tf_op jit(solution)/shard_map/ppermute | solution.py:622
  38.7 17.5 %copy-start.6 = (s32[32,256]{1,0:T(8,128)S(1)}, s32[32,256]{1,0:T(8,128)}, u32[]{:S(2)}) copy-start(s32[32,256]{1,0:T(8,128)} %tr.1) | copy-start | bytes 98308
  43.7 16.4 %all-to-all-start = ((f32[32,16,128]{2,1,0:T(8,128)}), f32[32,16,128]{2,1,0:T(8,128)S(1)}, u32[]{:S(2)}, u32[]{:S(2)}) async-start(f32[32,16,128]{2,1,0:T(8,128)} %get-tuple-element.37), calls=%async_computation | async-start | bytes 524288 | tf_op jit(solution)/shard_map/all_to_all | solution.py:629
  46.6 12.1 %copy-start.4 = (f32[64,32,128]{2,1,0:T(8,128)S(1)}, f32[64,32,128]{2,1,0:T(8,128)}, u32[]{:S(2)}) copy-start(f32[64,32,128]{2,1,0:T(8,128)} %copy-done.3) | copy-start | bytes 3145732
  46.7 7.7 %collective-permute-start.11 = (bf16[64,1024]{1,0:T(8,128)(2,1)S(1)}, bf16[64,1024]{1,0:T(8,128)(2,1)S(1)}, u32[]{:S(2)}, u32[]{:S(2)}) collective-permute-start(bf16[64,1024]{1,0:T(8,128)(2,1)S(1)} %shard_map.117), channel_id=1, source_target_pairs={{0,16},{1,17},{2,18},{3,19},{4,20},{5,21},{6,22},{7,23},{8,24},{9,... | collective-permute-start | bytes 393224 | tf_op jit(solution)/shard_map/ppermute | solution.py:632
  54.8 5.4 %collective-permute-start.12 = (f32[64,416]{1,0:T(8,128)S(1)}, f32[64,416]{1,0:T(8,128)S(1)}, u32[]{:S(2)}, u32[]{:S(2)}) collective-permute-start(f32[64,416]{1,0:T(8,128)S(1)} %get-tuple-element.39), channel_id=1, source_target_pairs={{0,16},{1,17},{2,18},{3,19},{4,20},{5,21},{6,22},{7,23},{8,24},{9,... | collective-permute-start | bytes 319496 | tf_op jit(solution)/shard_map/ppermute | solution.py:634
